TPU v7x, 256 devices: a whole 4x4x8 slice. The times are simulated.
256 devices in a mesh: pb: 16 (over x, y_hi, core), ka: 8 (over z), ga: 2 (over y_lo).
Axes of the slice: x: 4, y: 4 (y_hi: 2, y_lo: 2; y = y_hi * 2 + y_lo), z: 8, core: 2. Of those that a mesh axis runs over, the one named last changes fastest.
Arguments:
- queries: bfloat16 [16, 2048, 768], P(None, 'pb', 'ga'), may hold values from -6 to 6
- comp_keys: bfloat16 [8192, 768], P(('ka', 'pb'), 'ga'), may hold values from -6 to 6
- comp_values: bfloat16 [8192, 512], P(('ka', 'pb'), 'ga'), may hold values from -6 to 6
- outputs: bfloat16 [16, 2048, 512], P(None, 'pb', 'ga'), may hold values from -1.1953125 to 1.1953125
- grad_out: bfloat16 [16, 2048, 512], P(None, 'pb', 'ga'), may hold values from -300 to 300
- log_sums: float32 [4, 16, 2048], P('ga', None, 'pb'), may hold values from 7 to 10
- visible: int32 [32, 8192], P('pb', 'ka'), may hold values from 0 to 1, as said below
Outputs:
- grad_queries: float32 [16, 2048, 768], P('ka', 'pb', 'ga')
- grad_keys: float32 [8192, 768], P(('ka', 'pb'), 'ga')
- grad_values: float32 [8192, 512], P(('ka', 'pb'), 'ga')
Inputs may be any that keep to these rules, and one draw needn't show every extreme that they name: The queries are the last 2048 positions of a sequence of 131072 positions, and compressed key j covers positions 16 * j to 16 * j + 31. visible[b, j] is 1 exactly when key j ends before the first position of query block b and starts no earlier than the start of the document that holds that position; the sequence is packed from a few documents.
All inputs are finite; a program needn't handle non-finite values.
Results may differ from a plain program's by a relative error of at most 0.0029.
Values may be sent and summed in bfloat16 or wider, within the bound.
No kernel may reach another device: no remote copies, remote signals or barrier semaphores. Data moves between devices by JAX's collectives and lax.ppermute only.
A program may use at most 64 MiB of HBM per device.

v0:
```python
import jax
import jax.numpy as jnp
from jax import lax
from jax.sharding import PartitionSpec as P

DK = 192
DV = 128
QBLK = 64


def from_everyone(array, axis):
    copies = jnp.broadcast_to(array, (lax.axis_size(axis), *array.shape))
    return lax.all_to_all(copies, axis, split_axis=0, concat_axis=0, tiled=True)


def in_order(pieces, dim):
    pieces = jnp.moveaxis(pieces, 0, dim)
    shape = pieces.shape
    return pieces.reshape(*shape[:dim], shape[dim] * shape[dim + 1], *shape[dim + 2 :])


def collect(array, axis, dim):
    pieces = from_everyone(array, axis)
    return in_order(pieces, dim)


def in_one_piece(arrays, axis, dim, along):
    widths = [a.shape[along] for a in arrays]
    both = jnp.concatenate(arrays, axis=along)
    result = collect(both, axis, dim)
    return tuple(jnp.split(result, [sum(widths[:k]) for k in range(1, len(widths))], axis=along))


def in_blocks(array, dim, count):
    shape = array.shape
    pieces = array.reshape(*shape[:dim], count, shape[dim] // count, *shape[dim + 1 :])
    return jnp.moveaxis(pieces, dim, 0)


def summed_on_arrival(array, axis, dim):
    pieces = in_blocks(array, dim, lax.axis_size(axis))
    arrived = lax.all_to_all(pieces, axis, split_axis=0, concat_axis=0, tiled=True)
    return arrived.sum(axis=0)


def side_by_side(arrays, axis, dim, along):
    both = jnp.concatenate(arrays, axis=along)
    result, at, finished = (lax.psum_scatter(both, axis, scatter_dimension=dim, tiled=True), 0, [])
    for a in arrays:
        finished.append(lax.slice_in_dim(result, at, at + a.shape[along], axis=along))
        at += a.shape[along]
    return tuple(finished)


def group_grads(query_group, grad_group, row_delta, row_lse, key_group, value_group, mask_part):
    head_count, query_count, _ = query_group.shape
    length = key_group.shape[0]
    softmax_scale = DK ** (-0.5)
    scores = (
        jnp.einsum("hqd,kd->hqk", query_group, key_group, preferred_element_type=jnp.float32)
        * softmax_scale
    )
    weights = mask_part.astype(jnp.float32)[None, :, None, :]
    probs_full = (
        jnp.exp(scores - row_lse[:, :, None]).reshape(head_count, query_count // QBLK, QBLK, length)
        * weights
    )
    probs_full = probs_full.reshape(head_count, query_count, length)
    probs_low = probs_full.astype(jnp.bfloat16)
    grad_probs = jnp.einsum(
        "hqd,kd->hqk", grad_group, value_group, preferred_element_type=jnp.float32
    )
    grad_scores = (probs_full * (grad_probs - row_delta[:, :, None])).astype(jnp.bfloat16)
    value_grad = jnp.einsum(
        "hqk,hqd->kd", probs_low, grad_group, preferred_element_type=jnp.float32
    )
    key_grad = (
        jnp.einsum("hqk,hqd->kd", grad_scores, query_group, preferred_element_type=jnp.float32)
        * softmax_scale
    )
    query_grad = (
        jnp.einsum("hqk,kd->hqd", grad_scores, key_group, preferred_element_type=jnp.float32)
        * softmax_scale
    )
    return (query_grad, key_grad, value_grad)


def piece_grads(arrays, key_part, value_part, mask_part):
    queries, grad_out, deltas, log_sums = arrays
    groups = key_part.shape[1] // DK
    results = []
    for group_index in range(groups):
        results.append(
            group_grads(
                queries[:, :, group_index * DK : (group_index + 1) * DK],
                grad_out[:, :, group_index * DV : (group_index + 1) * DV],
                deltas[group_index],
                log_sums[group_index],
                key_part[:, group_index * DK : (group_index + 1) * DK],
                value_part[:, group_index * DV : (group_index + 1) * DV],
                mask_part,
            )
        )
    return (
        jnp.concatenate([entry[0] for entry in results], axis=2),
        jnp.concatenate([entry[1] for entry in results], axis=1),
        jnp.concatenate([entry[2] for entry in results], axis=1),
    )


def guarded(arrays, key_part, value_part, mask_part):

    def compute(operands):
        return piece_grads(arrays, operands[0], operands[1], operands[2])

    def nothing(operands):
        head_count, query_count = (arrays[0].shape[0], arrays[0].shape[1])
        length = operands[0].shape[0]
        return (
            jnp.zeros((head_count, query_count, operands[0].shape[1]), jnp.float32),
            jnp.zeros((length, operands[0].shape[1]), jnp.float32),
            jnp.zeros((length, operands[1].shape[1]), jnp.float32),
        )

    return lax.cond(jnp.any(mask_part > 0), compute, nothing, (key_part, value_part, mask_part))


def key_blocks(arrays, key_part, value_part, mask_part):
    length = key_part.shape[0]
    block_rows = 512
    number = length // block_rows
    key_stack = key_part.reshape(number, block_rows, key_part.shape[1])
    value_stack = value_part.reshape(number, block_rows, value_part.shape[1])
    mask_stack = mask_part.reshape(mask_part.shape[0], number, block_rows).transpose(1, 0, 2)

    def advance(running, inputs):
        query_grad, key_grad, value_grad = guarded(arrays, inputs[0], inputs[1], inputs[2])
        return (running + query_grad, (key_grad, value_grad))

    initial = jnp.zeros((arrays[0].shape[0], arrays[0].shape[1], key_part.shape[1]), jnp.float32)
    summed, (key_grads, value_grads) = lax.scan(
        advance, initial, (key_stack, value_stack, mask_stack)
    )
    return (
        summed,
        key_grads.reshape(length, key_part.shape[1]),
        value_grads.reshape(length, value_part.shape[1]),
    )


def per_device(queries, comp_keys, comp_values, outputs, grad_out, log_sums, visible):
    groups = comp_keys.shape[1] // DK
    deltas = jnp.stack(
        [
            jnp.einsum(
                "hqd,hqd->hq",
                grad_out[:, :, group_index * DV : (group_index + 1) * DV],
                outputs[:, :, group_index * DV : (group_index + 1) * DV],
                preferred_element_type=jnp.float32,
            )
            for group_index in range(groups)
        ]
    )
    arrays = (queries, grad_out, deltas, log_sums)
    head_count, query_count = (queries.shape[0], queries.shape[1])
    gathered_rows = lax.axis_size("pb") * comp_keys.shape[0]
    initial = (
        jnp.zeros((head_count, query_count, groups * DK), jnp.float32),
        jnp.zeros((gathered_rows, groups * DK), jnp.float32),
        jnp.zeros((gathered_rows, groups * DV), jnp.float32),
    )
    offset = jnp.int32(0)
    key_part, value_part = in_one_piece((comp_keys, comp_values), "pb", 0, 1)
    query_grad, key_grad, value_grad = key_blocks(arrays, key_part, value_part, visible)
    key_term_all = lax.dynamic_update_slice_in_dim(initial[1], key_grad, offset, 0)
    value_term = lax.dynamic_update_slice_in_dim(initial[2], value_grad, offset, 0)
    query_out = summed_on_arrival(query_grad, "ka", 0)
    key_out, value_out = side_by_side((key_term_all, value_term), "pb", 0, 1)
    return (query_out, key_out, value_out)


def solution(mesh):
    return jax.shard_map(
        per_device,
        mesh=mesh,
        in_specs=(
            P(None, "pb", "ga"),
            P(("ka", "pb"), "ga"),
            P(("ka", "pb"), "ga"),
            P(None, "pb", "ga"),
            P(None, "pb", "ga"),
            P("ga", None, "pb"),
            P("pb", "ka"),
        ),
        out_specs=(P("ka", "pb", "ga"), P(("ka", "pb"), "ga"), P(("ka", "pb"), "ga")),
        check_vma=False,
    )
```

profile of v0, /device:TPU:1, one launch (start us, length us, event | category | flops | bytes accessed | tf_op | source)
XLA Modules:
  0.0 198.0 jit_solution(13948015352608374985)
XLA Ops:
  7.2 0.9 pad_maximum_fusion.2
  8.1 1.3 broadcast_in_dim.33
  9.4 8.4 %all-to-all-start = ((bf16[16,64,640]{2,1,0:T(8,128)(2,1)}), bf16[16,64,640]{2,1,0:T(8,128)(2,1)S(1)}, u32[]{:S(2)}, u32[]{:S(2)}) async-start(bf16[16,64,640]{2,1,0:T(8,128)(2,1)} %broadcast_in_dim.33), calls=%async_computation | async-start | bytes 2621440 | tf_op jit(solution)/shard_map/all_to_all | solution.py:13
  17.9 1.7 copy.45
  19.5 2.2 %fusion.28 = (f32[16,128]{1,0:T(8,128)S(1)}, f32[16,128]{1,0:T(8,128)S(1)}) fusion(bf16[16,128,256]{2,1,0:T(8,128)(2,1)} %param.14, bf16[16,128,256]{2,1,0:T(8,128)(2,1)} %param.15), kind=kLoop, calls=%fused_computation.48 | loop fusion | flops 2093056 | bytes 2113536 | tf_op jit(solution)/shard_map/hqd,hqd->hq/dot_general | solution.py:155
  21.7 16.0 %all-to-all-done = bf16[16,64,640]{2,1,0:T(8,128)(2,1)S(1)} async-done(((bf16[16,64,640]{2,1,0:T(8,128)(2,1)}), bf16[16,64,640]{2,1,0:T(8,128)(2,1)S(1)}, u32[]{:S(2)}, u32[]{:S(2)}) %all-to-all-start) | async-done | bytes 1310752 | tf_op jit(solution)/shard_map/all_to_all | solution.py:13
  37.7 0.9 split.9
  38.7 1.2 copy.44
  39.9 22.6 %while.15 = (s32[]{:T(128)}, f32[16,128,384]{1,2,0:T(8,128)}, f32[2,512,384]{2,1,0:T(8,128)}, f32[2,512,256]{2,1,0:T(8,128)}, s32[2,2,512]{2,1,0:T(2,128)S(1)}, ...) while((s32[]{:T(128)}, f32[16,128,384]{1,2,0:T(8,128)}, ...), condition=%wide.region_4.5_spmd.clone, body=%wide.region_0.4_spmd.clone.sunk | while | flops 3514305536 | bytes 94212960 | solution.py:141
  39.9 0.6 compare_reduce_fusion.2
  41.2 2.2 %conditional.3 = (f32[16,128,384]{1,2,0:T(8,128)S(1)}, f32[1,512,384]{1,2,0:T(8,128)}, f32[1,512,256]{1,2,0:T(8,128)}) conditional(s32[]{:T(128)} %convert_element_type.41, () %tuple.55, (bf16[2,512,384]{1,2,0:T(8,128)(2,1)}, s32[]{:T(128)}, bf16[16,128,384]{1,2,0:T(8,128)(2,1)}, f32[2,16,128]{2,1,0:T(8,128)S(1)}, s32[2,512]{1,0:T(2,128)S(1)}, ...), branch_computations={%region_2.2_spmd, %region_3.3_spmd} | conditional | flops 3512730624 | bytes 66940988 | solution.py:125
  41.2 0.8 broadcast_in_dim.25
  42.0 1.1 broadcast_in_dim.24
  43.4 2.0 select_add_fusion.2
  45.4 1.4 copy.75
  46.7 0.8 constant_dynamic-update-slice_fusion.5
  47.6 1.4 copy.74
  49.0 1.2 copy-done.3
  51.5 2.2 %conditional.3 = (f32[16,128,384]{1,2,0:T(8,128)S(1)}, f32[1,512,384]{1,2,0:T(8,128)}, f32[1,512,256]{1,2,0:T(8,128)}) conditional(s32[]{:T(128)} %convert_element_type.41, () %tuple.55, (bf16[2,512,384]{1,2,0:T(8,128)(2,1)}, s32[]{:T(128)}, bf16[16,128,384]{1,2,0:T(8,128)(2,1)}, f32[2,16,128]{2,1,0:T(8,128)S(1)}, s32[2,512]{1,0:T(2,128)S(1)}, ...), branch_computations={%region_2.2_spmd, %region_3.3_spmd} | conditional | flops 3512730624 | bytes 66940988 | solution.py:125
  51.5 0.8 broadcast_in_dim.25
  52.4 1.1 broadcast_in_dim.24
  53.8 3.9 %select_add_fusion.2 = f32[16,128,384]{1,2,0:T(8,128)} fusion(f32[16,128,384]{1,2,0:T(8,128)S(1)} %get-tuple-element.340, f32[16,128,384]{1,2,0:T(8,128)} %get-tuple-element.364, pred[]{:T(512)S(6)} %compare.3), kind=kLoop, calls=%fused_computation.41.clone.1 | loop fusion | flops 1572864 | bytes 9437185 | tf_op jit(solution)/shard_map/while/body/eval_jaxpr/add | solution.py:138
  57.6 1.4 copy.75
  59.0 0.8 constant_dynamic-update-slice_fusion.5
  59.8 1.4 copy.74
  61.3 1.2 copy-done.3
  62.5 41.5 %all-to-all-start.1 = ((f32[8,2,128,384]{2,3,1,0:T(8,128)}), f32[8,2,128,384]{2,3,1,0:T(8,128)S(1)}, u32[]{:S(2)}, u32[]{:S(2)}) async-start(f32[8,2,128,384]{2,3,1,0:T(8,128)} %bitcast.81), calls=%async_computation.1 | async-start | bytes 6291456 | tf_op jit(solution)/shard_map/all_to_all | solution.py:42
  104.0 3.4 %pad_maximum_fusion.1 = f32[1024,640]{1,0:T(8,128)} fusion(f32[1024,256]{1,0:T(8,128)} %bitcast.88, f32[1024,384]{1,0:T(8,128)} %bitcast.87), kind=kLoop, calls=%fused_computation.46 | loop fusion | flops 655360 | bytes 5242880 | tf_op jit(solution)/shard_map/concatenate | solution.py:47
  107.4 79.6 %reduce-scatter.2.cloned.1.call-done = f32[64,640]{1,0:T(8,128)} async-done(((f32[1024,640]{1,0:T(8,128)}), f32[64,640]{1,0:T(8,128)}) %reduce-scatter.2.cloned.1.call-update) | async-done | bytes 163856 | tf_op jit(solution)/shard_map/reduce_scatter | solution.py:48
  187.0 1.5 slice.79
  188.5 1.5 slice.78
  190.2 0.9 copy.48
  (25 shorter events, 1.7 us)
Async XLA Ops:
  7.2 10.7 %copy-start.1 = (bf16[16,128,384]{2,1,0:T(8,128)(2,1)S(1)}, bf16[16,128,384]{2,1,0:T(8,128)(2,1)}, u32[]{:S(2)}) copy-start(bf16[16,128,384]{2,1,0:T(8,128)(2,1)} %param.11) | copy-start | bytes 4718596
  9.4 28.3 %all-to-all-start = ((bf16[16,64,640]{2,1,0:T(8,128)(2,1)}), bf16[16,64,640]{2,1,0:T(8,128)(2,1)S(1)}, u32[]{:S(2)}, u32[]{:S(2)}) async-start(bf16[16,64,640]{2,1,0:T(8,128)(2,1)} %broadcast_in_dim.33), calls=%async_computation | async-start | bytes 2621440 | tf_op jit(solution)/shard_map/all_to_all | solution.py:13
  19.5 20.3 %copy-start.4 = (f32[2,16,128]{2,1,0:T(8,128)S(1)}, f32[2,16,128]{2,1,0:T(8,128)}, u32[]{:S(2)}) copy-start(f32[2,16,128]{2,1,0:T(8,128)} %param.16) | copy-start | bytes 49156
  19.5 20.3 %copy-start.5 = (s32[2,1024]{1,0:T(2,128)S(1)}, s32[2,1024]{1,0:T(2,128)}, u32[]{:S(2)}) copy-start(s32[2,1024]{1,0:T(2,128)} %param.17) | copy-start | bytes 24580
  45.4 3.6 %copy-start.2 = (f32[2,512,384]{2,1,0:T(8,128)S(1)}, f32[2,512,384]{2,1,0:T(8,128)}, u32[]{:S(2)}) copy-start(f32[2,512,384]{2,1,0:T(8,128)} %get-tuple-element.365) | copy-start | bytes 4718596 | tf_op jit(solution)/shard_map/while
  49.0 1.2 copy-start.3
  57.6 3.6 %copy-start.2 = (f32[2,512,384]{2,1,0:T(8,128)S(1)}, f32[2,512,384]{2,1,0:T(8,128)}, u32[]{:S(2)}) copy-start(f32[2,512,384]{2,1,0:T(8,128)} %get-tuple-element.365) | copy-start | bytes 4718596 | tf_op jit(solution)/shard_map/while
  61.3 1.2 copy-start.3
  62.5 127.5 %all-to-all-start.1 = ((f32[8,2,128,384]{2,3,1,0:T(8,128)}), f32[8,2,128,384]{2,3,1,0:T(8,128)S(1)}, u32[]{:S(2)}, u32[]{:S(2)}) async-start(f32[8,2,128,384]{2,3,1,0:T(8,128)} %bitcast.81), calls=%async_computation.1 | async-start | bytes 6291456 | tf_op jit(solution)/shard_map/all_to_all | solution.py:42
  104.0 83.0 %reduce-scatter.2.cloned.1.call-start = ((), (), s32[]{:S(2)}) async-start(), calls=%async_computation.3 | async-start | bytes 2785280 | tf_op jit(solution)/shard_map/reduce_scatter | solution.py:48
Sparse Core Ops, SparseCore 0:
  109.0 77.9 reduce-scatter.1
where the time goes:
time: 200 us; the launch traced here: 198 us
  waiting for transfers between devices  95.6 us (48%)
  starting transfers between devices  50 us (25%)
  local copies, waits for them, and re-layouts  23.1 us (12%)
  between operations  14.1 us (7%)
  other arithmetic  13.8 us (7%)
    reduce_scatter x1, waiting for transfers between devices, side_by_side(): lax.psum_scatter(both, axis, scatter_dimension=dim, tiled=True)  79.6 us
    all_to_all x1, starting transfers between devices, summed_on_arrival(): lax.all_to_all(pieces, axis, split_axis=0, concat_axis=0, tiled=True)  41.5 us
    all_to_all x1, waiting for transfers between devices, from_everyone(): return lax.all_to_all(copies, axis, split_axis=0, concat_axis=0, tiled=True)  16 us
    all_to_all x1, starting transfers between devices, from_everyone(): return lax.all_to_all(copies, axis, split_axis=0, concat_axis=0, tiled=True)  8.44 us
    dynamic_update_slice x8, local copies, waits for them, and re-layouts, key_blocks(): lax.scan(advance, initial, (key_stack, value_stack, mask_stack))  7.27 us
    add x2, other arithmetic, advance(): return (running + query_grad, (key_grad, value_grad))  5.84 us
  transfers between devices with their start and end apart: 3, of which 2 were waited for; matrix products, arithmetic and copies ran while one was open for 5% of the time, Pallas kernels for 0%

commit v1 on v0

v1 whole, which is shorter than its diff:
```python
import math

import jax
import jax.numpy as jnp
from jax import lax
from jax.experimental import pallas as pl
from jax.experimental.pallas import tpu as pltpu
from jax.sharding import PartitionSpec as P

DK = 192
DV = 128
QBLK = 64
LANES = 128
WIN = 256
SCALE = 1.0 / math.sqrt(DK)
LOG2E = math.log2(math.e)
KEY_TILE = 256
HEADS = 4


def grad_kernel(group, q_ref, do_ref, own_ref, par_ref, lse_ref, delta_ref, mask_ref,
                dqt_ref, own_out, par_out, kz, kt, acc_k, acc_v):
    heads = q_ref.shape[0]
    half = own_ref.shape[0]
    lo = group * LANES
    vlo = 3 * LANES + group * LANES
    lane = lax.broadcasted_iota(jnp.int32, (KEY_TILE, WIN), 1)
    keep = (lane < DK) if group == 0 else (lane >= WIN - DK)
    tiles = []
    for side, ref in enumerate((own_ref, par_ref)):
        for t in range(half // KEY_TILE):
            tiles.append((ref, t * KEY_TILE, side * half + t * KEY_TILE))
    for ref, at, row in tiles:
        k = jnp.where(keep, ref[at:at + KEY_TILE, lo:lo + WIN], jnp.zeros((), jnp.bfloat16))
        kz[row:row + KEY_TILE, :] = k
        kt[:, row:row + KEY_TILE] = k.T
    acc_k[...] = jnp.zeros_like(acc_k)
    acc_v[...] = jnp.zeros_like(acc_v)
    first = 0 if group == 0 else WIN - DK
    rows = HEADS * q_ref.shape[1]
    nt = (((1,), (1,)), ((), ()))
    nn = (((1,), (0,)), ((), ()))
    f32 = jnp.float32

    def dot(a, b, dims):
        return lax.dot_general(a, b, dims, preferred_element_type=f32)

    def chunk(i, carry):
        h = i * HEADS
        q = q_ref[pl.ds(h, HEADS), :, lo:lo + WIN].reshape(rows, WIN)
        do = do_ref[pl.ds(h, HEADS), :, lo:lo + DV].reshape(rows, DV)
        lse = jnp.concatenate([lse_ref[pl.ds(h + j, 1), :] for j in range(HEADS)], axis=1) * LOG2E
        delta = jnp.concatenate([delta_ref[pl.ds(h + j, 1), :] for j in range(HEADS)], axis=1)
        dqt = jnp.zeros((DK, rows), f32)
        for ref, at, row in tiles:
            s = dot(kz[row:row + KEY_TILE, :], q, nt)
            dp = dot(ref[at:at + KEY_TILE, vlo:vlo + DV], do, nt)
            m = mask_ref[row:row + KEY_TILE, :]
            m = jnp.concatenate([m] * HEADS, axis=1)
            p = jnp.exp2(s * (SCALE * LOG2E) - lse) * m
            ds = (p * (dp - delta)).astype(jnp.bfloat16)
            p = p.astype(jnp.bfloat16)
            acc_v[row:row + KEY_TILE, :] += dot(p, do, nn)
            acc_k[row:row + KEY_TILE, :] += dot(ds, q, nn)
            dqt = dqt + dot(kt[first:first + DK, row:row + KEY_TILE], ds, nn)
        dqt = (dqt * SCALE).astype(jnp.bfloat16)
        for j in range(HEADS):
            dqt_ref[h + j, :, :] = dqt[:, j * LANES:(j + 1) * LANES]
        return carry

    lax.fori_loop(0, heads // HEADS, chunk, 0)
    own_out[:, :WIN] = acc_k[:half, :] * SCALE
    own_out[:, WIN:] = acc_v[:half, :]
    par_out[:, :WIN] = (acc_k[half:, :] * SCALE).astype(jnp.bfloat16)
    par_out[:, WIN:] = acc_v[half:, :].astype(jnp.bfloat16)


def group_grads(group, q, do, own, par, lse, delta, mask):
    heads, count, _ = q.shape
    half = own.shape[0]
    keys = 2 * half
    vmem = pl.BlockSpec(memory_space=pltpu.VMEM)
    flops = 2 * heads * count * keys * (3 * DK + 2 * DV)
    return pl.pallas_call(
        lambda *refs: grad_kernel(group, *refs),
        out_shape=(
            jax.ShapeDtypeStruct((heads, DK, count), jnp.bfloat16),
            jax.ShapeDtypeStruct((half, WIN + DV), jnp.float32),
            jax.ShapeDtypeStruct((half, WIN + DV), jnp.bfloat16),
        ),
        in_specs=[vmem] * 7,
        out_specs=(vmem, vmem, vmem),
        scratch_shapes=[
            pltpu.VMEM((keys, WIN), jnp.bfloat16),
            pltpu.VMEM((WIN, keys), jnp.bfloat16),
            pltpu.VMEM((keys, WIN), jnp.float32),
            pltpu.VMEM((keys, DV), jnp.float32),
        ],
        cost_estimate=pl.CostEstimate(flops=flops, bytes_accessed=8_000_000, transcendentals=heads * count * keys),
        compiler_params=pltpu.CompilerParams(vmem_limit_bytes=40 * 1024 * 1024),
        name=f"grads_{group}",
    )(q, do, own, par, lse, delta, mask)


def per_device(queries, comp_keys, comp_values, outputs, grad_out, log_sums, visible):
    pb = lax.axis_size("pb")
    ka = lax.axis_size("ka")
    chips = pb // 2
    core = lax.rem(lax.axis_index("pb"), 2)
    same_core = [[2 * i + c for i in range(chips)] for c in range(2)]
    other_core = [(i, i ^ 1) for i in range(pb)]
    rows = comp_keys.shape[0]
    groups = comp_keys.shape[1] // DK

    both = jnp.concatenate([comp_keys, comp_values], axis=1)
    own = lax.all_to_all(
        jnp.broadcast_to(both, (chips, *both.shape)), "pb", 0, 0, axis_index_groups=same_core, tiled=True
    ).reshape(chips * rows, both.shape[1])
    par = lax.ppermute(own, "pb", other_core)

    delta = [
        jnp.sum(
            grad_out[:, :, g * DV:(g + 1) * DV].astype(jnp.float32)
            * outputs[:, :, g * DV:(g + 1) * DV].astype(jnp.float32),
            axis=2,
        )
        for g in range(groups)
    ]
    seen = visible.reshape(visible.shape[0], chips, 2, rows)
    seen = jnp.where(core == 0, seen, seen[:, :, ::-1])
    seen = seen.transpose(2, 1, 3, 0).reshape(2 * chips * rows, visible.shape[0])
    mask = jnp.repeat(seen.astype(jnp.float32), QBLK, axis=1)

    heads, count, _ = queries.shape
    summed_q, summed_kv = [], []
    for g in range(groups):
        dqt, own_g, par_g = group_grads(g, queries, grad_out, own, par, log_sums[g], delta[g], mask)
        arrived = lax.all_to_all(dqt.reshape(ka, heads // ka, DK, count), "ka", 0, 0, tiled=True)
        summed_q.append(arrived)
        from_other = lax.ppermute(par_g, "pb", other_core)
        chip_sum = (own_g + from_other.astype(jnp.float32)).astype(jnp.bfloat16)
        pieces = lax.all_to_all(
            chip_sum.reshape(chips, rows, WIN + DV), "pb", 0, 0, axis_index_groups=same_core, tiled=True
        )
        summed_kv.append(pieces)
    dq = jnp.concatenate([a.astype(jnp.float32).sum(axis=0) for a in summed_q], axis=1).transpose(0, 2, 1)
    kv = [a.astype(jnp.float32).sum(axis=0) for a in summed_kv]
    dk = jnp.concatenate([kv[0][:, :DK], kv[1][:, WIN - DK:WIN]], axis=1)
    dv = jnp.concatenate([kv[0][:, WIN:], kv[1][:, WIN:]], axis=1)
    return (dq, dk, dv)


def solution(mesh):
    return jax.shard_map(
        per_device,
        mesh=mesh,
        in_specs=(
            P(None, "pb", "ga"),
            P(("ka", "pb"), "ga"),
            P(("ka", "pb"), "ga"),
            P(None, "pb", "ga"),
            P(None, "pb", "ga"),
            P("ga", None, "pb"),
            P("pb", "ka"),
        ),
        out_specs=(P("ka", "pb", "ga"), P(("ka", "pb"), "ga"), P(("ka", "pb"), "ga")),
        check_vma=False,
    )
```

time: 200 us -> 123 us (0.61)
  waiting for transfers between devices: 95.6 us -> 27.7 us
  blocking collectives: 0 us -> 58.8 us
  starting transfers between devices: 50 us -> 9.8 us
  local copies, waits for them, and re-layouts: 23.1 us -> 4.46 us
  Pallas kernels: 0 us -> 14.2 us
  between operations: 14.1 us -> 0.87 us
  other arithmetic: 13.8 us -> 5.5 us
    reduce_scatter x1 -> x0, waiting for transfers between devices: 79.6 us -> none  [side_by_side(): lax.psum_scatter(both, axis, scatter_dimension=dim, tiled=True)]
    all_to_all x0 -> x3, blocking collectives: none -> 58.8 us  [the longest x1 28.2 us: per_device(): lax.all_to_all(dqt.reshape(ka, heads // ka, DK, count), 'ka', 0, 0, tiled...]
    all_to_all x2, starting transfers between devices: 49.9 us -> 7 us  [the longest x1 3.55 us: per_device(): lax.all_to_all(dqt.reshape(ka, heads // ka, DK, count), 'ka', 0, 0, tiled...]
    pallas_call x0 -> x2, Pallas kernels: none -> 14.2 us  [group_grads(): pl.pallas_call(lambda *refs: grad_kernel(group, *refs), out_shape=(jax.Sh...]
    all_to_all x2, waiting for transfers between devices: 16 us -> 27.7 us  [the longest x1 18.4 us: per_device(): lax.all_to_all(dqt.reshape(ka, heads // ka, DK, count), 'ka', 0, 0, tiled...]
    dynamic_update_slice x8 -> x0, local copies, waits for them, and re-layouts: 7.27 us -> none  [key_blocks(): lax.scan(advance, initial, (key_stack, value_stack, mask_stack))]
    add x2 -> x0, other arithmetic: 5.84 us -> none  [advance(): return (running + query_grad, (key_grad, value_grad))]
    broadcast_in_dim x5 -> x2, local copies, waits for them, and re-layouts: 5.1 us -> 0.1 us  [the longest x1 0.05 us: per_device(): jnp.broadcast_to(both, (chips, *both.shape))]
  transfers between devices with their start and end apart: 3 -> 5, of which waited for: 2 -> 2; matrix products, arithmetic and copies ran while one was open for 5% -> 4% of each run, Pallas kernels for 0% -> 6%
where the time goes in v1:
time: 123 us; the launch traced here: 121 us
  blocking collectives  58.8 us (48%)
  waiting for transfers between devices  27.7 us (23%)
  Pallas kernels  14.2 us (12%)
  starting transfers between devices  9.8 us (8%)
  other arithmetic  5.5 us (4%)
  local copies, waits for them, and re-layouts  4.46 us (4%)
    all_to_all x1, blocking collectives, per_device(): lax.all_to_all(dqt.reshape(ka, heads // ka, DK, count), 'ka', 0, 0, tiled...  28.2 us
    all_to_all x1, blocking collectives, per_device(): lax.all_to_all(jnp.broadcast_to(both, (chips, *both.shape)), 'pb', 0, 0,...  19 us
    all_to_all x1, waiting for transfers between devices, per_device(): lax.all_to_all(dqt.reshape(ka, heads // ka, DK, count), 'ka', 0, 0, tiled...  18.4 us
    pallas_call x2, Pallas kernels, group_grads(): pl.pallas_call(lambda *refs: grad_kernel(group, *refs), out_shape=(jax.Sh...  14.2 us
    all_to_all x1, blocking collectives, per_device(): lax.all_to_all(chip_sum.reshape(chips, rows, WIN + DV), 'pb', 0, 0, axis_...  11.7 us
    all_to_all x1, waiting for transfers between devices, per_device(): lax.all_to_all(chip_sum.reshape(chips, rows, WIN + DV), 'pb', 0, 0, axis_...  9.24 us
    unnamed x21, local copies, waits for them, and re-layouts  3.9 us
    all_to_all x1, starting transfers between devices, per_device(): lax.all_to_all(dqt.reshape(ka, heads // ka, DK, count), 'ka', 0, 0, tiled...  3.55 us
  transfers between devices with their start and end apart: 5, of which 2 were waited for; matrix products, arithmetic and copies ran while one was open for 4% of the time, Pallas kernels for 6%

profile of v1, /device:TPU:1, one launch (start us, length us, event | category | flops | bytes accessed | tf_op | source)
XLA Modules:
  0.0 121.3 jit_solution(6274881146195508879)
XLA Ops:
  0.6 0.8 pad_maximum_fusion.1
  1.5 0.1 broadcast_in_dim.6
  1.6 19.0 %all_to_all.25 = bf16[8,64,640]{2,1,0:T(8,128)(2,1)S(1)} all-to-all(bf16[8,64,640]{2,1,0:T(8,128)(2,1)S(1)} %broadcast_in_dim.6), channel_id=1, replica_groups={{0,32,64,96,128,160,192,224},{16,48,80,112,144,176,208,240},{1,33,65,97..., dimensions={0} | all-to-all | bytes 1310720 | tf_op jit(solution)/shard_map/all_to_all | solution.py:116
  20.5 2.2 %collective-permute-start = (bf16[512,640]{1,0:T(8,128)(2,1)S(1)}, bf16[512,640]{1,0:T(8,128)(2,1)S(1)}, u32[]{:S(2)}, u32[]{:S(2)}) collective-permute-start(bf16[512,640]{1,0:T(8,128)(2,1)S(1)} %bitcast.19), channel_id=1, source_target_pairs={{0,16},{16,0},{32,48},{48,32},{64,80},{80,64},{96,112},{112,96},{1... | collective-permute-start | bytes 1966088 | tf_op jit(solution)/shard_map/ppermute | solution.py:119
  22.7 0.1 reshape.30
  22.8 0.1 convert_element_type.49
  23.0 0.0 copy-start.8
  23.0 0.2 copy.16.refs_6_
  23.2 2.0 %multiply_reduce_fusion.1 = (f32[16,128]{1,0:T(8,128)S(1)}, f32[16,128]{1,0:T(8,128)S(1)}) fusion(bf16[16,128,256]{2,1,0:T(8,128)(2,1)} %param.10, bf16[16,128,256]{2,1,0:T(8,128)(2,1)S(1)} %copy-done), kind=kLoop, calls=%fused_computation.3 | loop fusion | flops 2093056 | bytes 2113536 | tf_op jit(solution)/shard_map/reduce_sum | solution.py:122
  25.3 0.8 copy-done.4
  26.1 1.1 copy-done.5
  27.2 6.6 %grads_0.1 = (bf16[16,192,128]{2,1,0:T(8,128)(2,1)S(1)}, f32[512,384]{1,0:T(8,128)S(1)}, bf16[512,384]{1,0:T(8,128)(2,1)S(1)}) custom-call(bf16[16,128,384]{2,1,0:T(8,128)(2,1)S(1)} %copy-done.3, bf16[16,128,256]{2,1,0:T(8,128)(2,1)S(1)} %copy-done, bf16[512,640]{1,0:T(8,128)(2,1)S(1)} %bitcast.20, bf16[512,640]{1,0:T(8,128)(2,1)S(1)} %copy-done.5, ...), custom_call_target="tpu_custom_call" | custom-call | flops 3489660928 | bytes 8000000 | tf_op jit(solution)/shard_map/grads_0/pallas_call | solution.py:84
  33.8 0.1 collective-permute-start.1
  33.9 1.0 copy-done.2
  35.0 7.6 %grads_1.1 = (bf16[16,192,128]{2,1,0:T(8,128)(2,1)}, f32[512,384]{1,0:T(8,128)S(1)}, bf16[512,384]{1,0:T(8,128)(2,1)}) custom-call(bf16[16,128,384]{2,1,0:T(8,128)(2,1)S(1)} %copy-done.3, bf16[16,128,256]{2,1,0:T(8,128)(2,1)S(1)} %copy-done, bf16[512,640]{1,0:T(8,128)(2,1)S(1)} %bitcast.21, bf16[512,640]{1,0:T(8,128)(2,1)S(1)} %copy-done.5, ...), custom_call_target="tpu_custom_call" | custom-call | flops 3489660928 | bytes 8000000 | tf_op jit(solution)/shard_map/grads_1/pallas_call | solution.py:84
  42.5 0.5 collective-permute-start.2
  43.0 0.8 add_convert_fusion.1
  43.9 3.5 %all-to-all-start.3 = ((bf16[8,64,384]{2,1,0:T(8,128)(2,1)}), bf16[8,64,384]{2,1,0:T(8,128)(2,1)S(1)}, u32[]{:S(2)}, u32[]{:S(2)}) async-start(bf16[8,64,384]{2,1,0:T(8,128)(2,1)} %bitcast.8), calls=%async_computation.3 | async-start | bytes 786432 | tf_op jit(solution)/shard_map/all_to_all | solution.py:142
  47.3 0.1 add_convert_fusion
  47.4 9.2 %all-to-all-done.3 = bf16[8,64,384]{2,1,0:T(8,128)(2,1)S(1)} async-done(((bf16[8,64,384]{2,1,0:T(8,128)(2,1)}), bf16[8,64,384]{2,1,0:T(8,128)(2,1)S(1)}, u32[]{:S(2)}, u32[]{:S(2)}) %all-to-all-start.3) | async-done | bytes 393248 | tf_op jit(solution)/shard_map/all_to_all | solution.py:142
  56.6 11.7 %all_to_all.26 = bf16[8,64,384]{2,1,0:T(8,128)(2,1)S(1)} all-to-all(bf16[8,64,384]{2,1,0:T(8,128)(2,1)S(1)} %bitcast.23), channel_id=1, replica_groups={{0,32,64,96,128,160,192,224},{16,48,80,112,144,176,208,240},{1,33,65,97..., dimensions={0} | all-to-all | bytes 786432 | tf_op jit(solution)/shard_map/all_to_all | solution.py:142
  68.3 28.2 %all_to_all.27 = bf16[8,2,192,128]{3,2,1,0:T(8,128)(2,1)S(1)} all-to-all(bf16[8,2,192,128]{3,2,1,0:T(8,128)(2,1)S(1)} %bitcast.18), channel_id=1, replica_groups=mesh['pb'=16,'ka'=8,'ga'=2] {'ka'}, dimensions={0} | all-to-all | bytes 1572864 | tf_op jit(solution)/shard_map/all_to_all | solution.py:138
  96.5 3.5 %all-to-all-start.2 = ((bf16[8,2,192,128]{3,2,1,0:T(8,128)(2,1)}), bf16[8,2,192,128]{3,2,1,0:T(8,128)(2,1)S(1)}, u32[]{:S(2)}, u32[]{:S(2)}) async-start(bf16[8,2,192,128]{3,2,1,0:T(8,128)(2,1)} %bitcast.6), calls=%async_computation.2 | async-start | bytes 1572864 | tf_op jit(solution)/shard_map/all_to_all | solution.py:138
  100.1 0.1 convert_reduce_fusion.3
  100.2 0.1 convert_reduce_fusion.2
  100.2 0.1 slice.41
  100.3 0.6 pad_maximum_fusion.2
  101.0 0.7 pad_maximum_fusion
  101.7 0.1 convert_reduce_fusion.1
  101.8 18.4 %all-to-all-done.2 = bf16[8,2,192,128]{3,2,1,0:T(8,128)(2,1)S(1)} async-done(((bf16[8,2,192,128]{3,2,1,0:T(8,128)(2,1)}), bf16[8,2,192,128]{3,2,1,0:T(8,128)(2,1)S(1)}, u32[]{:S(2)}, u32[]{:S(2)}) %all-to-all-start.2) | async-done | bytes 786464 | tf_op jit(solution)/shard_map/all_to_all | solution.py:138
  120.3 0.1 convert_reduce_fusion
  120.4 0.9 copy.18
  (27 shorter events, 0.1 us)
Async XLA Ops:
  0.6 22.1 %copy-start.9 = (s32[2,1024]{1,0:T(2,128)S(1)}, s32[2,1024]{1,0:T(2,128)}, u32[]{:S(2)}) copy-start(s32[2,1024]{1,0:T(2,128)} %param.13) | copy-start | bytes 24580
  1.5 21.6 %copy-start = (bf16[16,128,256]{2,1,0:T(8,128)(2,1)S(1)}, bf16[16,128,256]{2,1,0:T(8,128)(2,1)}, u32[]{:S(2)}) copy-start(bf16[16,128,256]{2,1,0:T(8,128)(2,1)} %refs_1_.3) | copy-start | bytes 3145732
  20.5 4.8 %collective-permute-start = (bf16[512,640]{1,0:T(8,128)(2,1)S(1)}, bf16[512,640]{1,0:T(8,128)(2,1)S(1)}, u32[]{:S(2)}, u32[]{:S(2)}) collective-permute-start(bf16[512,640]{1,0:T(8,128)(2,1)S(1)} %bitcast.19), channel_id=1, source_target_pairs={{0,16},{16,0},{32,48},{48,32},{64,80},{80,64},{96,112},{112,96},{1... | collective-permute-start | bytes 1966088 | tf_op jit(solution)/shard_map/ppermute | solution.py:119
  23.0 2.3 %copy-start.8 = (f32[2,16,128]{2,1,0:T(8,128)S(1)}, f32[2,16,128]{2,1,0:T(8,128)}, u32[]{:S(2)}) copy-start(f32[2,16,128]{2,1,0:T(8,128)} %param.12) | copy-start | bytes 49156
  23.2 10.6 %copy-start.1 = (f32[1024,128]{1,0:T(8,128)}, f32[1024,128]{1,0:T(8,128)S(1)}, u32[]{:S(2)}) copy-start(f32[1024,128]{1,0:T(8,128)S(1)} %copy.16.refs_6_) | copy-start | bytes 1572868
  23.2 2.9 %copy-start.3 = (bf16[16,128,384]{2,1,0:T(8,128)(2,1)S(1)}, bf16[16,128,384]{2,1,0:T(8,128)(2,1)}, u32[]{:S(2)}) copy-start(bf16[16,128,384]{2,1,0:T(8,128)(2,1)} %refs_0_.3) | copy-start | bytes 4718596
  25.3 0.8 copy-start.4
  26.1 1.1 copy-start.5
  33.8 9.2 %collective-permute-start.1 = (bf16[512,384]{1,0:T(8,128)(2,1)S(1)}, bf16[512,384]{1,0:T(8,128)(2,1)S(1)}, u32[]{:S(2)}, u32[]{:S(2)}) collective-permute-start(bf16[512,384]{1,0:T(8,128)(2,1)S(1)} %get-tuple-element.12), channel_id=1, source_target_pairs={{0,16},{16,0},{32,48},{48,32},{64,80},{80,64},{96,112},{112,96},{1... | collective-permute-start | bytes 1179656 | tf_op jit(solution)/shard_map/ppermute | solution.py:140
  33.9 1.0 copy-start.2
  42.5 4.8 %collective-permute-start.2 = (bf16[512,384]{1,0:T(8,128)(2,1)}, bf16[512,384]{1,0:T(8,128)(2,1)S(1)}, u32[]{:S(2)}, u32[]{:S(2)}) collective-permute-start(bf16[512,384]{1,0:T(8,128)(2,1)} %get-tuple-element.14), channel_id=1, source_target_pairs={{0,16},{16,0},{32,48},{48,32},{64,80},{80,64},{96,112},{112,96},{1... | collective-permute-start | bytes 1179656 | tf_op jit(solution)/shard_map/ppermute | solution.py:140
  43.9 12.8 %all-to-all-start.3 = ((bf16[8,64,384]{2,1,0:T(8,128)(2,1)}), bf16[8,64,384]{2,1,0:T(8,128)(2,1)S(1)}, u32[]{:S(2)}, u32[]{:S(2)}) async-start(bf16[8,64,384]{2,1,0:T(8,128)(2,1)} %bitcast.8), calls=%async_computation.3 | async-start | bytes 786432 | tf_op jit(solution)/shard_map/all_to_all | solution.py:142
  56.6 11.7 %copy-start.6 = (bf16[8,64,384]{2,1,0:T(8,128)(2,1)}, bf16[8,64,384]{2,1,0:T(8,128)(2,1)S(1)}, u32[]{:S(2)}) copy-start(bf16[8,64,384]{2,1,0:T(8,128)(2,1)S(1)} %all-to-all-done.3) | copy-start | bytes 1179652
  68.3 31.7 %copy-start.7 = (bf16[8,64,384]{2,1,0:T(8,128)(2,1)S(1)}, bf16[8,64,384]{2,1,0:T(8,128)(2,1)}, u32[]{:S(2)}) copy-start(bf16[8,64,384]{2,1,0:T(8,128)(2,1)} %copy-done.6) | copy-start | bytes 1179652
  96.5 23.7 %all-to-all-start.2 = ((bf16[8,2,192,128]{3,2,1,0:T(8,128)(2,1)}), bf16[8,2,192,128]{3,2,1,0:T(8,128)(2,1)S(1)}, u32[]{:S(2)}, u32[]{:S(2)}) async-start(bf16[8,2,192,128]{3,2,1,0:T(8,128)(2,1)} %bitcast.6), calls=%async_computation.2 | async-start | bytes 1572864 | tf_op jit(solution)/shard_map/all_to_all | solution.py:138

commit v2 on v1

v2 whole, which is shorter than its diff:
```python
import math

import jax
import jax.numpy as jnp
from jax import lax
from jax.experimental import pallas as pl
from jax.experimental.pallas import tpu as pltpu
from jax.sharding import PartitionSpec as P

DK = 192
DV = 128
QBLK = 64
LANES = 128
GROUPS = 2
WIN = 256
SCALE = 1.0 / math.sqrt(DK)
LOG2E = math.log2(math.e)
KEY_TILE = 256
HEADS = 4
NT = (((1,), (1,)), ((), ()))
NN = (((1,), (0,)), ((), ()))


def dot(a, b, dims):
    return lax.dot_general(a, b, dims, preferred_element_type=jnp.float32)


def key_tiles(own_ref, par_ref):
    half = own_ref.shape[0]
    return [
        (ref, t * KEY_TILE, side * half + t * KEY_TILE)
        for side, ref in enumerate((own_ref, par_ref))
        for t in range(half // KEY_TILE)
    ]


def key_window(group, ref, at):
    lane = lax.broadcasted_iota(jnp.int32, (KEY_TILE, WIN), 1)
    keep = (lane < DK) if group == 0 else (lane >= WIN - DK)
    lo = group * LANES
    return jnp.where(keep, ref[at:at + KEY_TILE, lo:lo + WIN], jnp.zeros((), jnp.bfloat16))


def chunk_rows(group, h, q_ref, do_ref, lse_ref, delta_ref):
    rows = HEADS * q_ref.shape[1]
    lo = group * LANES
    q = q_ref[pl.ds(h, HEADS), :, lo:lo + WIN].reshape(rows, WIN)
    do = do_ref[pl.ds(h, HEADS), :, lo:lo + DV].reshape(rows, DV)
    lse = jnp.concatenate([lse_ref[group, pl.ds(h + j, 1), :] for j in range(HEADS)], axis=1) * LOG2E
    delta = jnp.concatenate([delta_ref[group, pl.ds(h + j, 1), :] for j in range(HEADS)], axis=1)
    return q, do, lse, delta


def tile_terms(key, value, mask, q, do, lse, delta):
    s = dot(key, q, NT)
    dp = dot(value, do, NT)
    p = jnp.exp2(s * (SCALE * LOG2E) - lse) * jnp.concatenate([mask] * HEADS, axis=1)
    ds = (p * (dp - delta)).astype(jnp.bfloat16)
    return p.astype(jnp.bfloat16), ds


def query_kernel(q_ref, do_ref, own_ref, par_ref, lse_ref, delta_ref, mask_ref, dqt_ref, kz, kt):
    tiles = key_tiles(own_ref, par_ref)
    for group in range(GROUPS):
        vlo = 3 * LANES + group * LANES
        first = 0 if group == 0 else WIN - DK
        for ref, at, row in tiles:
            k = key_window(group, ref, at)
            kz[row:row + KEY_TILE, :] = k
            kt[:, row:row + KEY_TILE] = k.T

        def chunk(i, carry):
            h = i * HEADS
            q, do, lse, delta = chunk_rows(group, h, q_ref, do_ref, lse_ref, delta_ref)
            dqt = jnp.zeros((DK, q.shape[0]), jnp.float32)
            for ref, at, row in tiles:
                _, ds = tile_terms(
                    kz[row:row + KEY_TILE, :], ref[at:at + KEY_TILE, vlo:vlo + DV],
                    mask_ref[row:row + KEY_TILE, :], q, do, lse, delta,
                )
                dqt = dqt + dot(kt[first:first + DK, row:row + KEY_TILE], ds, NN)
            dqt = (dqt * SCALE).astype(jnp.bfloat16)
            for j in range(HEADS):
                dqt_ref[h + j, group * DK:(group + 1) * DK, :] = dqt[:, j * LANES:(j + 1) * LANES]
            return carry

        lax.fori_loop(0, q_ref.shape[0] // HEADS, chunk, 0)


def key_kernel(q_ref, do_ref, own_ref, par_ref, lse_ref, delta_ref, mask_ref, own_out, par_out, kz, acc_k, acc_v):
    half = own_ref.shape[0]
    tiles = key_tiles(own_ref, par_ref)
    for group in range(GROUPS):
        vlo = 3 * LANES + group * LANES
        for ref, at, row in tiles:
            kz[row:row + KEY_TILE, :] = key_window(group, ref, at)
        acc_k[group, :, :] = jnp.zeros(acc_k.shape[1:], jnp.float32)
        acc_v[...] = jnp.zeros_like(acc_v)

        def chunk(i, carry):
            q, do, lse, delta = chunk_rows(group, i * HEADS, q_ref, do_ref, lse_ref, delta_ref)
            for ref, at, row in tiles:
                p, ds = tile_terms(
                    kz[row:row + KEY_TILE, :], ref[at:at + KEY_TILE, vlo:vlo + DV],
                    mask_ref[row:row + KEY_TILE, :], q, do, lse, delta,
                )
                acc_v[row:row + KEY_TILE, :] += dot(p, do, NN)
                acc_k[group, row:row + KEY_TILE, :] += dot(ds, q, NN)
            return carry

        lax.fori_loop(0, q_ref.shape[0] // HEADS, chunk, 0)
        own_out[:, vlo:vlo + DV] = acc_v[:half, :]
        par_out[:, vlo:vlo + DV] = acc_v[half:, :].astype(par_out.dtype)
    low = lax.broadcasted_iota(jnp.int32, (half, LANES), 1) < DK - LANES
    for side, out in enumerate((own_out, par_out)):
        at = side * half
        a = acc_k[0, at:at + half, :] * SCALE
        b = acc_k[1, at:at + half, :] * SCALE
        out[:, :LANES] = a[:, :LANES].astype(out.dtype)
        out[:, LANES:2 * LANES] = jnp.where(low, a[:, LANES:], b[:, :LANES]).astype(out.dtype)
        out[:, 2 * LANES:3 * LANES] = b[:, LANES:].astype(out.dtype)


def grads(q, do, own, par, lse, delta, mask, which):
    heads, count, width = q.shape
    half, both = own.shape
    keys = 2 * half
    vmem = pl.BlockSpec(memory_space=pltpu.VMEM)
    work = 2 * GROUPS * heads * count * keys
    if which == "query":
        return pl.pallas_call(
            query_kernel,
            out_shape=jax.ShapeDtypeStruct((heads, width, count), jnp.bfloat16),
            in_specs=[vmem] * 7,
            out_specs=vmem,
            scratch_shapes=[pltpu.VMEM((keys, WIN), jnp.bfloat16), pltpu.VMEM((WIN, keys), jnp.bfloat16)],
            cost_estimate=pl.CostEstimate(
                flops=work * (2 * DK + DV), bytes_accessed=7_000_000, transcendentals=work // 2),
            compiler_params=pltpu.CompilerParams(vmem_limit_bytes=24 * 1024 * 1024),
            name="query_grads",
        )(q, do, own, par, lse, delta, mask)
    return pl.pallas_call(
        key_kernel,
        out_shape=(
            jax.ShapeDtypeStruct((half, both), jnp.float32),
            jax.ShapeDtypeStruct((half, both), jnp.bfloat16),
        ),
        in_specs=[vmem] * 7,
        out_specs=(vmem, vmem),
        scratch_shapes=[
            pltpu.VMEM((keys, WIN), jnp.bfloat16),
            pltpu.VMEM((GROUPS, keys, WIN), jnp.float32),
            pltpu.VMEM((keys, DV), jnp.float32),
        ],
        cost_estimate=pl.CostEstimate(
            flops=work * 2 * (DK + DV), bytes_accessed=8_000_000, transcendentals=work // 2),
        compiler_params=pltpu.CompilerParams(vmem_limit_bytes=24 * 1024 * 1024),
        name="key_grads",
    )(q, do, own, par, lse, delta, mask)


def per_device(queries, comp_keys, comp_values, outputs, grad_out, log_sums, visible):
    pb = lax.axis_size("pb")
    ka = lax.axis_size("ka")
    chips = pb // 2
    core = lax.rem(lax.axis_index("pb"), 2)
    same_core = [[2 * i + c for i in range(chips)] for c in range(2)]
    other_core = [(i, i ^ 1) for i in range(pb)]
    rows = comp_keys.shape[0]
    heads, count, width = queries.shape

    both = jnp.concatenate([comp_keys, comp_values], axis=1)
    own = lax.all_to_all(
        jnp.broadcast_to(both, (chips, *both.shape)), "pb", 0, 0, axis_index_groups=same_core, tiled=True
    ).reshape(chips * rows, both.shape[1])
    delta = jnp.stack([
        jnp.sum(
            grad_out[:, :, g * DV:(g + 1) * DV].astype(jnp.float32)
            * outputs[:, :, g * DV:(g + 1) * DV].astype(jnp.float32),
            axis=2,
        )
        for g in range(GROUPS)
    ])
    seen = visible.reshape(visible.shape[0], chips, 2, rows)
    seen = jnp.where(core == 0, seen, seen[:, :, ::-1])
    seen = seen.transpose(2, 1, 3, 0).reshape(2 * chips * rows, visible.shape[0])
    mask = jnp.repeat(seen.astype(jnp.float32), QBLK, axis=1)
    own, delta, mask = lax.optimization_barrier((own, delta, mask))
    par = lax.ppermute(own, "pb", other_core)

    args = (queries, grad_out, own, par, log_sums, delta, mask)
    dqt = grads(*args, "query")
    arrived_q = lax.all_to_all(dqt.reshape(ka, heads // ka, width, count), "ka", 0, 0, tiled=True)

    own_kv, par_kv = grads(*args, "key")
    from_other = lax.ppermute(par_kv, "pb", other_core)
    chip_sum = (own_kv + from_other.astype(jnp.float32)).astype(jnp.bfloat16)
    arrived_kv = lax.all_to_all(
        chip_sum.reshape(chips, rows, both.shape[1]), "pb", 0, 0, axis_index_groups=same_core, tiled=True
    )
    kv = arrived_kv.astype(jnp.float32).sum(axis=0)
    dq = arrived_q.astype(jnp.float32).sum(axis=0).transpose(0, 2, 1)
    return (dq, kv[:, :width], kv[:, width:])


def solution(mesh):
    return jax.shard_map(
        per_device,
        mesh=mesh,
        in_specs=(
            P(None, "pb", "ga"),
            P(("ka", "pb"), "ga"),
            P(("ka", "pb"), "ga"),
            P(None, "pb", "ga"),
            P(None, "pb", "ga"),
            P("ga", None, "pb"),
            P("pb", "ka"),
        ),
        out_specs=(P("ka", "pb", "ga"), P(("ka", "pb"), "ga"), P(("ka", "pb"), "ga")),
        check_vma=False,
    )
```

time: 123 us -> 109 us (0.89); the launches traced: 121 us -> 109 us
  blocking collectives: 58.8 us -> 0 us
  waiting for transfers between devices: 27.7 us -> 52.2 us
  starting transfers between devices: 9.8 us -> 21.6 us
  Pallas kernels: 14.2 us -> 24.1 us
  local copies, waits for them, and re-layouts: 4.46 us -> 6.33 us
  other arithmetic: 5.5 us -> 4.01 us
    all_to_all x3 -> x0, blocking collectives: 58.8 us -> none  [the longest x1 28.2 us: per_device(): lax.all_to_all(dqt.reshape(ka, heads // ka, DK, count), 'ka', 0, 0, tiled...]
    all_to_all x2 -> x3, waiting for transfers between devices: 27.7 us -> 48.9 us  [the longest x1 38 us: per_device(): lax.all_to_all(dqt.reshape(ka, heads // ka, width, count), 'ka', 0, 0, ti...]
    all_to_all x2 -> x3, starting transfers between devices: 7 us -> 19.9 us  [the longest x1 8.18 us: per_device(): lax.all_to_all(dqt.reshape(ka, heads // ka, width, count), 'ka', 0, 0, ti...]
    pallas_call x2, Pallas kernels: 14.2 us -> 24.1 us  [the longest x1 12.9 us: grads(): pl.pallas_call(query_kernel, out_shape=jax.ShapeDtypeStruct((heads, width...]
    ppermute x2 -> x1, waiting for transfers between devices: 0.01 us -> 1.73 us  [per_device(): from_other = lax.ppermute(par_kv, 'pb', other_core)]
    ppermute x1, waiting for transfers between devices: 0.01 us -> 1.53 us  [per_device(): par = lax.ppermute(own, 'pb', other_core)]
    reduce_sum x1, other arithmetic: 2.03 us -> 0.61 us  [per_device(): jnp.sum(grad_out[:, :, g * DV:(g + 1) * DV].astype(jnp.float32) * outputs...]
    concatenate x2 -> x0, other arithmetic: 1.37 us -> none  [the longest x1 0.73 us: per_device(): dk = jnp.concatenate([kv[0][:, :DK], kv[1][:, WIN - DK:WIN]], axis=1)]
  transfers between devices with their start and end apart: 5 -> 5, of which waited for: 2 -> 4; matrix products, arithmetic and copies ran while one was open for 4% -> 3% of each run, Pallas kernels for 6% -> 12%
where the time goes in v2:
time: 109 us
  waiting for transfers between devices  52.2 us (48%)
  Pallas kernels  24.1 us (22%)
  starting transfers between devices  21.6 us (20%)
  local copies, waits for them, and re-layouts  6.33 us (6%)
  other arithmetic  4.01 us (4%)
    all_to_all x1, waiting for transfers between devices, per_device(): lax.all_to_all(dqt.reshape(ka, heads // ka, width, count), 'ka', 0, 0, ti...  38 us
    pallas_call x1, Pallas kernels, grads(): pl.pallas_call(query_kernel, out_shape=jax.ShapeDtypeStruct((heads, width...  12.9 us
    pallas_call x1, Pallas kernels, grads(): pl.pallas_call(key_kernel, out_shape=(jax.ShapeDtypeStruct((half, both),...  11.2 us
    all_to_all x1, waiting for transfers between devices, per_device(): lax.all_to_all(jnp.broadcast_to(both, (chips, *both.shape)), 'pb', 0, 0,...  11 us
    all_to_all x1, starting transfers between devices, per_device(): lax.all_to_all(dqt.reshape(ka, heads // ka, width, count), 'ka', 0, 0, ti...  8.18 us
    all_to_all x1, starting transfers between devices, per_device(): lax.all_to_all(jnp.broadcast_to(both, (chips, *both.shape)), 'pb', 0, 0,...  7.47 us
    all_to_all x1, starting transfers between devices, per_device(): lax.all_to_all(chip_sum.reshape(chips, rows, both.shape[1]), 'pb', 0, 0,...  4.2 us
    unnamed x13, local copies, waits for them, and re-layouts  3.74 us
  transfers between devices with their start and end apart: 5, of which 4 were waited for; matrix products, arithmetic and copies ran while one was open for 3% of the time, Pallas kernels for 12%

profile of v2, /device:TPU:1, one launch (start us, length us, event | category | flops | bytes accessed | tf_op | source)
XLA Modules:
  0.0 109.0 jit_solution(3387185681626018230)
XLA Ops:
  0.6 0.0 copy-start.5
  0.6 0.0 copy-start.4
  0.7 0.0 copy-start
  0.7 1.0 pad_maximum_fusion
  1.6 0.9 broadcast_in_dim.6
  2.5 7.5 %all-to-all-start = ((bf16[8,64,640]{2,1,0:T(8,128)(2,1)}), bf16[8,64,640]{2,1,0:T(8,128)(2,1)S(1)}, u32[]{:S(2)}, u32[]{:S(2)}) async-start(bf16[8,64,640]{2,1,0:T(8,128)(2,1)} %broadcast_in_dim.6), calls=%async_computation | async-start | bytes 1310720 | tf_op jit(solution)/shard_map/all_to_all | solution.py:173
  10.0 0.1 reshape.24
  10.1 0.1 convert_element_type.39
  10.2 0.0 copy-done.4
  10.2 0.0 copy-start.3
  10.2 0.6 multiply_reduce_fusion.1
  10.9 11.0 %all-to-all-done = bf16[8,64,640]{2,1,0:T(8,128)(2,1)S(1)} async-done(((bf16[8,64,640]{2,1,0:T(8,128)(2,1)}), bf16[8,64,640]{2,1,0:T(8,128)(2,1)S(1)}, u32[]{:S(2)}, u32[]{:S(2)}) %all-to-all-start) | async-done | bytes 655392 | tf_op jit(solution)/shard_map/all_to_all | solution.py:173
  21.9 1.3 %collective-permute-start = (bf16[512,640]{1,0:T(8,128)(2,1)S(1)}, bf16[512,640]{1,0:T(8,128)(2,1)S(1)}, u32[]{:S(2)}, u32[]{:S(2)}) collective-permute-start(bf16[512,640]{1,0:T(8,128)(2,1)S(1)} %bitcast.13), channel_id=1, source_target_pairs={{0,16},{16,0},{32,48},{48,32},{64,80},{80,64},{96,112},{112,96},{1... | collective-permute-start | bytes 1966088 | tf_op jit(solution)/shard_map/ppermute | solution.py:189
  23.2 0.2 copy.16.mask_ref
  23.4 1.5 %collective-permute-done.par_ref = bf16[512,640]{1,0:T(8,128)(2,1)S(1)} collective-permute-done((bf16[512,640]{1,0:T(8,128)(2,1)S(1)}, bf16[512,640]{1,0:T(8,128)(2,1)S(1)}, u32[]{:S(2)}, u32[]{:S(2)}) %collective-permute-start) | collective-permute-done | bytes 655392 | tf_op jit(solution)/shard_map/ppermute | solution.py:189
  24.9 1.4 %copy-done.1 = bf16[16,128,384]{2,1,0:T(8,128)(2,1)S(1)} copy-done((bf16[16,128,384]{2,1,0:T(8,128)(2,1)S(1)}, bf16[16,128,384]{2,1,0:T(8,128)(2,1)}, u32[]{:S(2)}) %copy-start.1) | copy-done | bytes 1572888
  26.4 11.2 %key_grads.1 = (f32[512,640]{1,0:T(8,128)S(1)}, bf16[512,640]{1,0:T(8,128)(2,1)S(1)}) custom-call(bf16[16,128,384]{2,1,0:T(8,128)(2,1)S(1)} %copy-done.1, bf16[16,128,256]{2,1,0:T(8,128)(2,1)S(1)} %copy-done, bf16[512,640]{1,0:T(8,128)(2,1)S(1)} %bitcast.14, bf16[512,640]{1,0:T(8,128)(2,1)S(1)} %collective-permute-done.par_ref, f32[2,16,128]{2,1,0:T(8,128)S(1)} %copy-done.3, ...), custom_call_target="tpu_custom_call" | custom-call | flops 5368709120 | bytes 8000000 | tf_op jit(solution)/shard_map/key_grads/pallas_call | solution.py:142
  37.6 0.5 collective-permute-start.1
  38.0 1.7 %collective-permute-done.1 = bf16[512,640]{1,0:T(8,128)(2,1)S(1)} collective-permute-done((bf16[512,640]{1,0:T(8,128)(2,1)S(1)}, bf16[512,640]{1,0:T(8,128)(2,1)S(1)}, u32[]{:S(2)}, u32[]{:S(2)}) %collective-permute-start.1) | collective-permute-done | bytes 655392 | tf_op jit(solution)/shard_map/ppermute | solution.py:196
  39.8 1.0 add_convert_fusion
  40.8 4.2 %all-to-all-start.2 = ((bf16[8,64,640]{2,1,0:T(8,128)(2,1)}), bf16[8,64,640]{2,1,0:T(8,128)(2,1)}, u32[]{:S(2)}, u32[]{:S(2)}) async-start(bf16[8,64,640]{2,1,0:T(8,128)(2,1)} %bitcast.16), calls=%async_computation.2 | async-start | bytes 1310720 | tf_op jit(solution)/shard_map/all_to_all | solution.py:198
  45.0 0.0 copy-start.2
  45.0 1.4 %copy-done.2 = bf16[16,128,384]{2,1,0:T(8,128)(2,1)S(1)} copy-done((bf16[16,128,384]{2,1,0:T(8,128)(2,1)S(1)}, bf16[16,128,384]{2,1,0:T(8,128)(2,1)}, u32[]{:S(2)}) %copy-start.2) | copy-done | bytes 1572888
  46.4 12.9 %query_grads.1 = bf16[16,384,128]{2,1,0:T(8,128)(2,1)} custom-call(bf16[16,128,384]{2,1,0:T(8,128)(2,1)S(1)} %copy-done.2, bf16[16,128,256]{2,1,0:T(8,128)(2,1)S(1)} %copy-done, bf16[512,640]{1,0:T(8,128)(2,1)S(1)} %bitcast.15, bf16[512,640]{1,0:T(8,128)(2,1)S(1)} %collective-permute-done.par_ref, f32[2,16,128]{2,1,0:T(8,128)S(1)} %copy-done.3, ...), custom_call_target="tpu_custom_call" | custom-call | flops 4294967296 | bytes 7000000 | tf_op jit(solution)/shard_map/query_grads/pallas_call | solution.py:131
  59.3 0.0 all-to-all-done.2
  59.3 8.2 %all-to-all-start.1 = ((bf16[8,2,384,128]{3,2,1,0:T(8,128)(2,1)}), bf16[8,2,384,128]{3,2,1,0:T(8,128)(2,1)S(1)}, u32[]{:S(2)}, u32[]{:S(2)}) async-start(bf16[8,2,384,128]{3,2,1,0:T(8,128)(2,1)} %bitcast.5), calls=%async_computation.1 | async-start | bytes 3145728 | tf_op jit(solution)/shard_map/all_to_all | solution.py:193
  67.5 1.2 %convert_reduce_fusion.1 = f32[64,640]{1,0:T(8,128)S(1)} fusion(bf16[8,64,640]{2,1,0:T(8,128)(2,1)} %all-to-all-done.2), kind=kLoop, calls=%fused_computation.1 | loop fusion | flops 614400 | bytes 819200 | tf_op jit(solution)/shard_map/reduce_sum | solution.py:201
  68.7 0.6 slice.24
  69.3 0.6 slice.25
  69.9 38.0 %all-to-all-done.1 = bf16[8,2,384,128]{3,2,1,0:T(8,128)(2,1)S(1)} async-done(((bf16[8,2,384,128]{3,2,1,0:T(8,128)(2,1)}), bf16[8,2,384,128]{3,2,1,0:T(8,128)(2,1)S(1)}, u32[]{:S(2)}, u32[]{:S(2)}) %all-to-all-start.1) | async-done | bytes 1572896 | tf_op jit(solution)/shard_map/all_to_all | solution.py:193
  107.9 0.2 convert_reduce_fusion
  108.1 0.9 copy.18
  (8 shorter events, 0.1 us)
Async XLA Ops:
  0.6 9.4 %copy-start.5 = (s32[2,1024]{1,0:T(2,128)S(1)}, s32[2,1024]{1,0:T(2,128)}, u32[]{:S(2)}) copy-start(s32[2,1024]{1,0:T(2,128)} %param.13) | copy-start | bytes 24580
  0.6 9.6 %copy-start.4 = (bf16[16,128,256]{2,1,0:T(8,128)(2,1)S(1)}, bf16[16,128,256]{2,1,0:T(8,128)(2,1)}, u32[]{:S(2)}) copy-start(bf16[16,128,256]{2,1,0:T(8,128)(2,1)} %param.10) | copy-start | bytes 3145732
  0.7 9.6 %copy-start = (bf16[16,128,256]{2,1,0:T(8,128)(2,1)S(1)}, bf16[16,128,256]{2,1,0:T(8,128)(2,1)}, u32[]{:S(2)}) copy-start(bf16[16,128,256]{2,1,0:T(8,128)(2,1)} %do_ref.3) | copy-start | bytes 3145732
  2.5 19.3 %all-to-all-start = ((bf16[8,64,640]{2,1,0:T(8,128)(2,1)}), bf16[8,64,640]{2,1,0:T(8,128)(2,1)S(1)}, u32[]{:S(2)}, u32[]{:S(2)}) async-start(bf16[8,64,640]{2,1,0:T(8,128)(2,1)} %broadcast_in_dim.6), calls=%async_computation | async-start | bytes 1310720 | tf_op jit(solution)/shard_map/all_to_all | solution.py:173
  10.2 14.7 %copy-start.3 = (f32[2,16,128]{2,1,0:T(8,128)S(1)}, f32[2,16,128]{2,1,0:T(8,128)}, u32[]{:S(2)}) copy-start(f32[2,16,128]{2,1,0:T(8,128)} %lse_ref.3) | copy-start | bytes 49156
  21.9 3.0 %collective-permute-start = (bf16[512,640]{1,0:T(8,128)(2,1)S(1)}, bf16[512,640]{1,0:T(8,128)(2,1)S(1)}, u32[]{:S(2)}, u32[]{:S(2)}) collective-permute-start(bf16[512,640]{1,0:T(8,128)(2,1)S(1)} %bitcast.13), channel_id=1, source_target_pairs={{0,16},{16,0},{32,48},{48,32},{64,80},{80,64},{96,112},{112,96},{1... | collective-permute-start | bytes 1966088 | tf_op jit(solution)/shard_map/ppermute | solution.py:189
  24.9 1.4 %copy-start.1 = (bf16[16,128,384]{2,1,0:T(8,128)(2,1)S(1)}, bf16[16,128,384]{2,1,0:T(8,128)(2,1)}, u32[]{:S(2)}) copy-start(bf16[16,128,384]{2,1,0:T(8,128)(2,1)} %q_ref.3) | copy-start | bytes 4718596
  37.6 2.2 %collective-permute-start.1 = (bf16[512,640]{1,0:T(8,128)(2,1)S(1)}, bf16[512,640]{1,0:T(8,128)(2,1)S(1)}, u32[]{:S(2)}, u32[]{:S(2)}) collective-permute-start(bf16[512,640]{1,0:T(8,128)(2,1)S(1)} %get-tuple-element.12), channel_id=1, source_target_pairs={{0,16},{16,0},{32,48},{48,32},{64,80},{80,64},{96,112},{112,96},{1... | collective-permute-start | bytes 1966088 | tf_op jit(solution)/shard_map/ppermute | solution.py:196
  40.8 18.5 %all-to-all-start.2 = ((bf16[8,64,640]{2,1,0:T(8,128)(2,1)}), bf16[8,64,640]{2,1,0:T(8,128)(2,1)}, u32[]{:S(2)}, u32[]{:S(2)}) async-start(bf16[8,64,640]{2,1,0:T(8,128)(2,1)} %bitcast.16), calls=%async_computation.2 | async-start | bytes 1310720 | tf_op jit(solution)/shard_map/all_to_all | solution.py:198
  45.0 1.4 %copy-start.2 = (bf16[16,128,384]{2,1,0:T(8,128)(2,1)S(1)}, bf16[16,128,384]{2,1,0:T(8,128)(2,1)}, u32[]{:S(2)}) copy-start(bf16[16,128,384]{2,1,0:T(8,128)(2,1)} %q_ref.3) | copy-start | bytes 4718596
  59.3 48.6 %all-to-all-start.1 = ((bf16[8,2,384,128]{3,2,1,0:T(8,128)(2,1)}), bf16[8,2,384,128]{3,2,1,0:T(8,128)(2,1)S(1)}, u32[]{:S(2)}, u32[]{:S(2)}) async-start(bf16[8,2,384,128]{3,2,1,0:T(8,128)(2,1)} %bitcast.5), calls=%async_computation.1 | async-start | bytes 3145728 | tf_op jit(solution)/shard_map/all_to_all | solution.py:193

commit v3 on v2

v3 whole, which is shorter than its diff:
```python
import math

import jax
import jax.numpy as jnp
from jax import lax
from jax.experimental import pallas as pl
from jax.experimental.pallas import tpu as pltpu
from jax.sharding import PartitionSpec as P

DK = 192
DV = 128
QBLK = 64
LANES = 128
GROUPS = 2
WIN = 256
SCALE = 1.0 / math.sqrt(DK)
LOG2E = math.log2(math.e)
KEY_TILE = 256
FAR = (3, -3, 4)
NEAR = (0, 1, -1, 2, -2)
NT = (((1,), (1,)), ((), ()))
NN = (((1,), (0,)), ((), ()))


def dot(a, b, dims):
    return lax.dot_general(a, b, dims, preferred_element_type=jnp.float32)


def key_tiles(own_ref, par_ref):
    half = own_ref.shape[0]
    return [
        (ref, t * KEY_TILE, side * half + t * KEY_TILE)
        for side, ref in enumerate((own_ref, par_ref))
        for t in range(half // KEY_TILE)
    ]


def load_keys(own_ref, par_ref, kz, kt):
    lane = lax.broadcasted_iota(jnp.int32, (KEY_TILE, WIN), 1)
    for group in range(GROUPS):
        keep = (lane < DK) if group == 0 else (lane >= WIN - DK)
        lo = group * LANES
        first = 0 if group == 0 else WIN - DK
        for ref, at, row in key_tiles(own_ref, par_ref):
            k = jnp.where(keep, ref[at:at + KEY_TILE, lo:lo + WIN], jnp.zeros((), jnp.bfloat16))
            kz[group, row:row + KEY_TILE, :] = k
            kt[group, :, row:row + KEY_TILE] = k.T[first:first + DK, :]


def owner_grads(h, per_owner, q_ref, do_ref, own_ref, par_ref, lse_ref, delta_ref, mask_ref, kz, kt, acc_k, acc_v):
    rows = per_owner * q_ref.shape[1]
    result = []
    for group in range(GROUPS):
        lo = group * LANES
        vlo = 3 * LANES + lo
        q = q_ref[pl.ds(h, per_owner), :, lo:lo + WIN].reshape(rows, WIN)
        do = do_ref[pl.ds(h, per_owner), :, lo:lo + DV].reshape(rows, DV)
        lse = jnp.concatenate([lse_ref[group, pl.ds(h + j, 1), :] for j in range(per_owner)], axis=1) * LOG2E
        delta = jnp.concatenate([delta_ref[group, pl.ds(h + j, 1), :] for j in range(per_owner)], axis=1)
        dqt = jnp.zeros((DK, rows), jnp.float32)
        for ref, at, row in key_tiles(own_ref, par_ref):
            s = dot(kz[group, row:row + KEY_TILE, :], q, NT)
            dp = dot(ref[at:at + KEY_TILE, vlo:vlo + DV], do, NT)
            mask = jnp.concatenate([mask_ref[row:row + KEY_TILE, :]] * per_owner, axis=1)
            p = jnp.exp2(s * (SCALE * LOG2E) - lse) * mask
            ds = (p * (dp - delta)).astype(jnp.bfloat16)
            acc_v[group, row:row + KEY_TILE, :] += dot(p.astype(jnp.bfloat16), do, NN)
            acc_k[group, row:row + KEY_TILE, :] += dot(ds, q, NN)
            dqt = dqt + dot(kt[group, :, row:row + KEY_TILE], ds, NN)
        result.append(dqt * SCALE)
    return result


def far_kernel(heads_ref, *refs):
    inputs, (right, left, acc_k, acc_v), (kz, kt, held) = refs[:7], refs[7:11], refs[11:]
    per_owner = right.shape[0]
    load_keys(inputs[2], inputs[3], kz, kt)
    acc_k[...] = jnp.zeros_like(acc_k)
    acc_v[...] = jnp.zeros_like(acc_v)

    def one(i, carry):
        dqt = owner_grads(heads_ref[i], per_owner, *inputs, kz, kt, acc_k, acc_v)
        for group in range(GROUPS):
            for j in range(per_owner):
                held[i, j, group * DK:(group + 1) * DK, :] = dqt[group][:, j * LANES:(j + 1) * LANES].astype(held.dtype)
        return carry

    lax.fori_loop(0, len(FAR), one, 0)
    width = GROUPS * DK
    right[:, :width, :] = held[0]
    left[:, :width, :] = held[1]
    right[:, width:, :] = held[2, :, :DK, :]
    left[:, width:, :] = held[2, :, DK:, :]


def near_kernel(heads_ref, *refs):
    inputs, (in_k, in_v), (near, own_out, par_out), (kz, kt, acc_k, acc_v) = refs[:7], refs[7:9], refs[9:12], refs[12:]
    per_owner = near.shape[1]
    half = own_out.shape[0]
    load_keys(inputs[2], inputs[3], kz, kt)
    acc_k[...] = in_k[...]
    acc_v[...] = in_v[...]

    def one(i, carry):
        dqt = owner_grads(heads_ref[len(FAR) + i], per_owner, *inputs, kz, kt, acc_k, acc_v)
        for group in range(GROUPS):
            for j in range(per_owner):
                near[i, j, group * DK:(group + 1) * DK, :] = dqt[group][:, j * LANES:(j + 1) * LANES]
        return carry

    lax.fori_loop(0, len(NEAR), one, 0)
    low = lax.broadcasted_iota(jnp.int32, (half, LANES), 1) < DK - LANES
    for side, out in enumerate((own_out, par_out)):
        at = side * half
        a = acc_k[0, at:at + half, :] * SCALE
        b = acc_k[1, at:at + half, :] * SCALE
        out[:, :LANES] = a[:, :LANES].astype(out.dtype)
        out[:, LANES:2 * LANES] = jnp.where(low, a[:, LANES:], b[:, :LANES]).astype(out.dtype)
        out[:, 2 * LANES:3 * LANES] = b[:, LANES:].astype(out.dtype)
        for group in range(GROUPS):
            vlo = (3 + group) * LANES
            out[:, vlo:vlo + DV] = acc_v[group, at:at + half, :].astype(out.dtype)


def call(kernel, name, owners, per_owner, outs, scratch, *args):
    half = args[3].shape[0]
    count = args[1].shape[1]
    work = 2 * GROUPS * owners * per_owner * count * 2 * half
    vmem = pl.BlockSpec(memory_space=pltpu.VMEM)
    return pl.pallas_call(
        kernel,
        out_shape=outs,
        in_specs=[pl.BlockSpec(memory_space=pltpu.SMEM)] + [vmem] * (len(args) - 1),
        out_specs=tuple(vmem for _ in outs),
        scratch_shapes=[
            pltpu.VMEM((GROUPS, 2 * half, WIN), jnp.bfloat16),
            pltpu.VMEM((GROUPS, DK, 2 * half), jnp.bfloat16),
            *scratch,
        ],
        cost_estimate=pl.CostEstimate(
            flops=work * (3 * DK + 2 * DV), bytes_accessed=10_000_000, transcendentals=work // 2),
        compiler_params=pltpu.CompilerParams(vmem_limit_bytes=24 * 1024 * 1024),
        name=name,
    )(*args)


def per_device(queries, comp_keys, comp_values, outputs, grad_out, log_sums, visible):
    pb = lax.axis_size("pb")
    ka = lax.axis_size("ka")
    chips = pb // 2
    core = lax.rem(lax.axis_index("pb"), 2)
    me = lax.axis_index("ka")
    same_core = [[2 * i + c for i in range(chips)] for c in range(2)]
    other_core = [(i, i ^ 1) for i in range(pb)]
    rows = comp_keys.shape[0]
    heads, count, width = queries.shape
    per_owner = heads // ka
    f32, bf16 = jnp.float32, jnp.bfloat16

    def along(x, step):
        return lax.ppermute(x, "ka", [(i, (i + step) % ka) for i in range(ka)])

    both = jnp.concatenate([comp_keys, comp_values], axis=1)
    keys = 2 * chips * rows
    half = keys // 2
    own = lax.all_to_all(
        jnp.broadcast_to(both, (chips, *both.shape)), "pb", 0, 0, axis_index_groups=same_core, tiled=True
    ).reshape(half, both.shape[1])
    delta = jnp.stack([
        jnp.sum(
            grad_out[:, :, g * DV:(g + 1) * DV].astype(f32) * outputs[:, :, g * DV:(g + 1) * DV].astype(f32), axis=2
        )
        for g in range(GROUPS)
    ])
    seen = visible.reshape(visible.shape[0], chips, 2, rows)
    seen = jnp.where(core == 0, seen, seen[:, :, ::-1])
    seen = seen.transpose(2, 1, 3, 0).reshape(keys, visible.shape[0])
    mask = jnp.repeat(seen.astype(f32), QBLK, axis=1)
    order = per_owner * ((me + jnp.array(FAR + NEAR, jnp.int32) + ka) % ka)
    own, delta, mask, order = lax.optimization_barrier((own, delta, mask, order))
    par = lax.ppermute(own, "pb", other_core)

    args = (order, queries, grad_out, own, par, log_sums, delta, mask)
    shape = jax.ShapeDtypeStruct
    hops = shape((per_owner, width + DK, count), bf16)
    right, left, acc_k, acc_v = call(
        far_kernel, "far_grads", len(FAR), per_owner,
        (hops, hops, shape((GROUPS, keys, WIN), f32), shape((GROUPS, keys, DV), f32)),
        [pltpu.VMEM((len(FAR), per_owner, width, count), bf16)], *args,
    )
    with jax.named_scope("step1"):
        from_left = along(right, 2)
        from_right = along(left, -2)
    near, own_kv, par_kv = call(
        near_kernel, "near_grads", len(NEAR), per_owner,
        (
            shape((len(NEAR), per_owner, width, count), f32),
            shape((half, both.shape[1]), f32),
            shape((half, both.shape[1]), bf16),
        ),
        [pltpu.VMEM((GROUPS, keys, WIN), f32), pltpu.VMEM((GROUPS, keys, DV), f32)], *args, acc_k, acc_v,
    )
    from_other = lax.ppermute(par_kv, "pb", other_core)

    from_left, from_right = from_left.astype(f32), from_right.astype(f32)
    up1 = near[1] + from_left[:, :width]
    down1 = near[2] + from_right[:, :width]
    up2 = jnp.concatenate([near[3, :, :DK] + from_left[:, width:], near[3, :, DK:]], axis=1)
    down2 = jnp.concatenate([near[4, :, :DK], near[4, :, DK:] + from_right[:, width:]], axis=1)
    with jax.named_scope("step2"):
        arrived = [
            along(x.astype(bf16), step) for x, step in ((up2, 2), (down2, -2), (up1, 1), (down1, -1))
        ]
    chip_sum = (own_kv + from_other.astype(f32)).astype(bf16)
    arrived_kv = lax.all_to_all(
        chip_sum.reshape(chips, rows, both.shape[1]), "pb", 0, 0, axis_index_groups=same_core, tiled=True
    )
    kv = arrived_kv.astype(f32).sum(axis=0)
    dq = near[0] + sum(x.astype(f32) for x in arrived)
    return (dq.transpose(0, 2, 1), kv[:, :width], kv[:, width:])


def solution(mesh):
    return jax.shard_map(
        per_device,
        mesh=mesh,
        in_specs=(
            P(None, "pb", "ga"),
            P(("ka", "pb"), "ga"),
            P(("ka", "pb"), "ga"),
            P(None, "pb", "ga"),
            P(None, "pb", "ga"),
            P("ga", None, "pb"),
            P("pb", "ka"),
        ),
        out_specs=(P("ka", "pb", "ga"), P(("ka", "pb"), "ga"), P(("ka", "pb"), "ga")),
        check_vma=False,
    )
```

time: 109 us -> 83.3 us (0.76)
  waiting for transfers between devices: 52.2 us -> 25.1 us
  Pallas kernels: 24.1 us -> 19 us
  starting transfers between devices: 21.6 us -> 24.5 us
  other arithmetic: 4.01 us -> 5.6 us
  local copies, waits for them, and re-layouts: 6.33 us -> 7.82 us
    all_to_all x1 -> x0, waiting for transfers between devices: 38 us -> none  [per_device(): lax.all_to_all(dqt.reshape(ka, heads // ka, width, count), 'ka', 0, 0, ti...]
    ppermute x0 -> x6, waiting for transfers between devices: none -> 12.6 us  [along(): return lax.ppermute(x, 'ka', [(i, (i + step) % ka) for i in range(ka)])]
    ppermute x0 -> x6, starting transfers between devices: none -> 11.3 us  [along(): return lax.ppermute(x, 'ka', [(i, (i + step) % ka) for i in range(ka)])]
    all_to_all x1 -> x0, starting transfers between devices: 8.18 us -> none  [per_device(): lax.all_to_all(dqt.reshape(ka, heads // ka, width, count), 'ka', 0, 0, ti...]
    pallas_call x2, Pallas kernels: 24.1 us -> 19 us  [call(): pl.pallas_call(kernel, out_shape=outs, in_specs=[pl.BlockSpec(memory_spac...]
    ppermute x1, waiting for transfers between devices: 1.73 us -> 0.01 us  [per_device(): from_other = lax.ppermute(par_kv, 'pb', other_core)]
    unnamed x13 -> x27, local copies, waits for them, and re-layouts: 3.74 us -> 5.19 us
    reduce_sum x3 -> x2, other arithmetic: 2.02 us -> 0.7 us  [the longest x1 0.61 us: per_device(): jnp.sum(grad_out[:, :, g * DV:(g + 1) * DV].astype(f32) * outputs[:, :, g...]
  transfers between devices with their start and end apart: 5 -> 10, of which waited for: 4 -> 4; matrix products, arithmetic and copies ran while one was open for 3% -> 7% of each run, Pallas kernels for 12% -> 14%
where the time goes in v3:
time: 83.3 us; the launch traced here: 82.8 us
  waiting for transfers between devices  25.1 us (30%)
  starting transfers between devices  24.5 us (29%)
  Pallas kernels  19 us (23%)
  local copies, waits for them, and re-layouts  7.82 us (9%)
  other arithmetic  5.6 us (7%)
  between operations  0.87 us (1%)
    pallas_call x2, Pallas kernels, call(): pl.pallas_call(kernel, out_shape=outs, in_specs=[pl.BlockSpec(memory_spac...  19 us
    ppermute x6, waiting for transfers between devices, along(): return lax.ppermute(x, 'ka', [(i, (i + step) % ka) for i in range(ka)])  12.6 us
    ppermute x6, starting transfers between devices, along(): return lax.ppermute(x, 'ka', [(i, (i + step) % ka) for i in range(ka)])  11.3 us
    all_to_all x1, waiting for transfers between devices, per_device(): lax.all_to_all(jnp.broadcast_to(both, (chips, *both.shape)), 'pb', 0, 0,...  10.9 us
    all_to_all x1, starting transfers between devices, per_device(): lax.all_to_all(jnp.broadcast_to(both, (chips, *both.shape)), 'pb', 0, 0,...  7.6 us
    unnamed x27, local copies, waits for them, and re-layouts  5.19 us
    all_to_all x1, starting transfers between devices, per_device(): lax.all_to_all(chip_sum.reshape(chips, rows, both.shape[1]), 'pb', 0, 0,...  3.54 us
  transfers between devices with their start and end apart: 10, of which 4 were waited for; matrix products, arithmetic and copies ran while one was open for 7% of the time, Pallas kernels for 14%

profile of v3, /device:TPU:1, one launch (start us, length us, event | category | flops | bytes accessed | tf_op | source)
XLA Modules:
  0.0 82.8 jit_solution(7268091744445552419)
XLA Ops:
  0.7 1.0 %pad_maximum_fusion.2 = bf16[64,640]{1,0:T(8,128)(2,1)S(1)} fusion(bf16[64,256]{1,0:T(8,128)(2,1)} %param.10, bf16[64,384]{1,0:T(8,128)(2,1)} %param.9), kind=kLoop, calls=%fused_computation.18 | loop fusion | flops 163840 | bytes 163840 | tf_op jit(solution)/shard_map/concatenate | solution.py:163
  1.6 0.9 %broadcast_in_dim.6 = bf16[8,64,640]{2,1,0:T(8,128)(2,1)} broadcast(bf16[64,640]{1,0:T(8,128)(2,1)S(1)} %pad_maximum_fusion.2), dimensions={1,2} | broadcast | bytes 737280 | tf_op jit(solution)/shard_map/broadcast_in_dim | solution.py:167
  2.6 7.6 %all-to-all-start = ((bf16[8,64,640]{2,1,0:T(8,128)(2,1)}), bf16[8,64,640]{2,1,0:T(8,128)(2,1)S(1)}, u32[]{:S(2)}, u32[]{:S(2)}) async-start(bf16[8,64,640]{2,1,0:T(8,128)(2,1)} %broadcast_in_dim.6), calls=%async_computation | async-start | bytes 1310720 | tf_op jit(solution)/shard_map/all_to_all | solution.py:166
  10.4 0.6 multiply_reduce_fusion.1
  11.1 10.9 %all-to-all-done = bf16[8,64,640]{2,1,0:T(8,128)(2,1)S(1)} async-done(((bf16[8,64,640]{2,1,0:T(8,128)(2,1)}), bf16[8,64,640]{2,1,0:T(8,128)(2,1)S(1)}, u32[]{:S(2)}, u32[]{:S(2)}) %all-to-all-start) | async-done | bytes 655392 | tf_op jit(solution)/shard_map/all_to_all | solution.py:166
  22.1 1.3 %collective-permute-start = (bf16[512,640]{1,0:T(8,128)(2,1)S(1)}, bf16[512,640]{1,0:T(8,128)(2,1)S(1)}, u32[]{:S(2)}, u32[]{:S(2)}) collective-permute-start(bf16[512,640]{1,0:T(8,128)(2,1)S(1)} %bitcast.29), channel_id=1, source_target_pairs={{0,16},{16,0},{32,48},{48,32},{64,80},{80,64},{96,112},{112,96},{1... | collective-permute-start | bytes 1966088 | tf_op jit(solution)/shard_map/ppermute | solution.py:181
  23.4 0.2 copy.15.refs_6_
  23.6 1.5 %collective-permute-done.refs_3_ = bf16[512,640]{1,0:T(8,128)(2,1)S(1)} collective-permute-done((bf16[512,640]{1,0:T(8,128)(2,1)S(1)}, bf16[512,640]{1,0:T(8,128)(2,1)S(1)}, u32[]{:S(2)}, u32[]{:S(2)}) %collective-permute-start) | collective-permute-done | bytes 655392 | tf_op jit(solution)/shard_map/ppermute | solution.py:181
  25.1 1.4 %copy-done.3 = bf16[16,128,384]{2,1,0:T(8,128)(2,1)S(1)} copy-done((bf16[16,128,384]{2,1,0:T(8,128)(2,1)S(1)}, bf16[16,128,384]{2,1,0:T(8,128)(2,1)}, u32[]{:S(2)}) %copy-start.3) | copy-done | bytes 1572888
  26.5 7.3 %far_grads.1 = (bf16[2,576,128]{2,1,0:T(8,128)(2,1)S(1)}, bf16[2,576,128]{2,1,0:T(8,128)(2,1)S(1)}, f32[2,1024,256]{2,1,0:T(8,128)S(1)}, f32[2,1024,128]{2,1,0:T(8,128)S(1)}) custom-call(s32[8]{0:T(128)S(1)} %fusion.7.heads_ref, bf16[16,128,384]{2,1,0:T(8,128)(2,1)S(1)} %copy-done.3, bf16[16,128,256]{2,1,0:T(8,128)(2,1)S(1)} %copy-done, ...), custom_call_target="tpu_custom_call" | custom-call | flops 2617245696 | bytes 10000000 | tf_op jit(solution)/shard_map/far_grads/pallas_call | solution.py:130
  33.9 3.1 %collective-permute-start.1 = (bf16[2,576,128]{2,1,0:T(8,128)(2,1)S(1)}, bf16[2,576,128]{2,1,0:T(8,128)(2,1)S(1)}, u32[]{:S(2)}, u32[]{:S(2)}) collective-permute-start(bf16[2,576,128]{2,1,0:T(8,128)(2,1)S(1)} %get-tuple-element.21), channel_id=1, source_target_pairs={{0,4},{2,6},{4,8},{6,10},{8,12},{10,14},{12,0},{14,2},{1,5},{3,7},... | collective-permute-start | bytes 884744 | tf_op jit(solution)/shard_map/step1/ppermute | solution.py:161
  37.0 3.1 %collective-permute-start.3 = (bf16[2,576,128]{2,1,0:T(8,128)(2,1)S(1)}, bf16[2,576,128]{2,1,0:T(8,128)(2,1)S(1)}, u32[]{:S(2)}, u32[]{:S(2)}) collective-permute-start(bf16[2,576,128]{2,1,0:T(8,128)(2,1)S(1)} %get-tuple-element.22), channel_id=1, source_target_pairs={{0,12},{2,14},{4,0},{6,2},{8,4},{10,6},{12,8},{14,10},{1,13},{3,15... | collective-permute-start | bytes 884744 | tf_op jit(solution)/shard_map/step1/ppermute | solution.py:161
  40.1 1.1 %copy-done.2 = bf16[8,64,640]{2,1,0:T(8,128)(2,1)S(1)} copy-done((bf16[8,64,640]{2,1,0:T(8,128)(2,1)S(1)}, bf16[8,64,640]{2,1,0:T(8,128)(2,1)}, u32[]{:S(2)}) %copy-start.2) | copy-done | bytes 655384
  41.2 1.1 %copy-done.5 = bf16[512,640]{1,0:T(8,128)(2,1)S(1)} copy-done((bf16[512,640]{1,0:T(8,128)(2,1)S(1)}, bf16[512,640]{1,0:T(8,128)(2,1)}, u32[]{:S(2)}) %copy-start.5) | copy-done | bytes 655384
  42.3 0.7 copy-done.9
  42.9 11.6 %near_grads.1 = (f32[5,2,384,128]{3,2,1,0:T(8,128)S(1)}, f32[512,640]{1,0:T(8,128)S(1)}, bf16[512,640]{1,0:T(8,128)(2,1)S(1)}) custom-call(s32[8]{0:T(128)S(1)} %copy-done.9, bf16[16,128,384]{2,1,0:T(8,128)(2,1)S(1)} %copy-done.3, bf16[16,128,256]{2,1,0:T(8,128)(2,1)S(1)} %copy-done, bf16[512,640]{1,0:T(8,128)(2,1)S(1)} %bitcast.31, ...), custom_call_target="tpu_custom_call" | custom-call | flops 4362076160 | bytes 10000000 | tf_op jit(solution)/shard_map/near_grads/pallas_call | solution.py:130
  54.6 0.7 collective-permute-start.7
  55.3 0.2 convert.15
  55.6 0.8 fusion.1
  56.5 0.8 collective-permute-start.5
  57.2 1.9 %collective-permute-start.6 = (bf16[2,384,128]{2,1,0:T(8,128)(2,1)}, bf16[2,384,128]{2,1,0:T(8,128)(2,1)S(1)}, u32[]{:S(2)}, u32[]{:S(2)}) collective-permute-start(bf16[2,384,128]{2,1,0:T(8,128)(2,1)} %get-tuple-element.36), channel_id=1, source_target_pairs={{0,14},{2,0},{4,2},{6,4},{8,6},{10,8},{12,10},{14,12},{1,15},{3,1}... | collective-permute-start | bytes 589832 | tf_op jit(solution)/shard_map/step2/ppermute | solution.py:161
  59.2 0.7 pad_maximum_fusion.1
  59.9 1.8 %collective-permute-start.4 = (bf16[2,384,128]{2,1,0:T(8,128)(2,1)}, bf16[2,384,128]{2,1,0:T(8,128)(2,1)}, u32[]{:S(2)}, u32[]{:S(2)}) collective-permute-start(bf16[2,384,128]{2,1,0:T(8,128)(2,1)} %pad_maximum_fusion.1), channel_id=1, source_target_pairs={{0,12},{2,14},{4,0},{6,2},{8,4},{10,6},{12,8},{14,10},{1,13},{3,15... | collective-permute-start | bytes 589832 | tf_op jit(solution)/shard_map/step2/ppermute | solution.py:161
  61.7 1.0 %add_convert_fusion = bf16[512,640]{1,0:T(8,128)(2,1)} fusion(f32[512,640]{1,0:T(8,128)S(1)} %get-tuple-element.23, bf16[512,640]{1,0:T(8,128)(2,1)S(1)} %collective-permute-done.7), kind=kLoop, calls=%fused_computation.1 | loop fusion | flops 983040 | bytes 2621440 | tf_op jit(solution)/shard_map/convert_element_type | solution.py:214
  62.7 3.5 %all-to-all-start.1 = ((bf16[8,64,640]{2,1,0:T(8,128)(2,1)}), bf16[8,64,640]{2,1,0:T(8,128)(2,1)S(1)}, u32[]{:S(2)}, u32[]{:S(2)}) async-start(bf16[8,64,640]{2,1,0:T(8,128)(2,1)} %bitcast.13), calls=%async_computation.1 | async-start | bytes 1310720 | tf_op jit(solution)/shard_map/all_to_all | solution.py:215
  66.3 0.6 collective-permute-start.2
  66.9 5.8 %collective-permute-done.4 = bf16[2,384,128]{2,1,0:T(8,128)(2,1)} collective-permute-done((bf16[2,384,128]{2,1,0:T(8,128)(2,1)}, bf16[2,384,128]{2,1,0:T(8,128)(2,1)}, u32[]{:S(2)}, u32[]{:S(2)}) %collective-permute-start.4) | collective-permute-done | bytes 196640 | tf_op jit(solution)/shard_map/step2/ppermute | solution.py:161
  72.8 6.8 %collective-permute-done.2 = bf16[2,384,128]{2,1,0:T(8,128)(2,1)S(1)} collective-permute-done((bf16[2,384,128]{2,1,0:T(8,128)(2,1)S(1)}, bf16[2,384,128]{2,1,0:T(8,128)(2,1)S(1)}, u32[]{:S(2)}, u32[]{:S(2)}) %collective-permute-start.2) | collective-permute-done | bytes 196640 | tf_op jit(solution)/shard_map/step2/ppermute | solution.py:161
  79.5 1.0 %fusion.2 = f32[2,128,384]{1,2,0:T(8,128)S(1)} fusion(bf16[2,384,128]{2,1,0:T(8,128)(2,1)S(1)} %collective-permute-done.6, bf16[2,384,128]{2,1,0:T(8,128)(2,1)S(1)} %collective-permute-done.5, bf16[2,384,128]{2,1,0:T(8,128)(2,1)} %collective-permute-done.4, bf16[2,384,128]{2,1,0:T(8,128)(2,1)S(1)} %collective-permute-done.2, ...), kind=kLoop, calls=%fused_computation.9 | loop fusion | flops 786432 | bytes 1572864 | tf_op jit(solution)/shard_map/transpose | solution.py:220
  80.6 0.9 %copy.16 = f32[2,128,384]{2,1,0:T(8,128)} copy(f32[2,128,384]{1,2,0:T(8,128)S(1)} %fusion.2) | data formatting | bytes 786432
  81.6 0.6 slice.77
  82.2 0.6 slice.76
  (41 shorter events, 0.5 us)
Async XLA Ops:
  0.6 9.5 %copy-start.11 = (s32[2,1024]{1,0:T(2,128)S(1)}, s32[2,1024]{1,0:T(2,128)}, u32[]{:S(2)}) copy-start(s32[2,1024]{1,0:T(2,128)} %param.14) | copy-start | bytes 24580
  0.6 9.7 %copy-start = (bf16[16,128,256]{2,1,0:T(8,128)(2,1)S(1)}, bf16[16,128,256]{2,1,0:T(8,128)(2,1)}, u32[]{:S(2)}) copy-start(bf16[16,128,256]{2,1,0:T(8,128)(2,1)} %refs_1_.3) | copy-start | bytes 3145732
  0.7 9.7 %copy-start.10 = (bf16[16,128,256]{2,1,0:T(8,128)(2,1)S(1)}, bf16[16,128,256]{2,1,0:T(8,128)(2,1)}, u32[]{:S(2)}) copy-start(bf16[16,128,256]{2,1,0:T(8,128)(2,1)} %param.11) | copy-start | bytes 3145732
  2.6 8.5 %copy-start.12 = (s32[8]{0:T(128)S(1)}, s32[8]{0:T(128)}, u32[]{:S(2)}) copy-start(s32[8]{0:T(128)} %constant.38.clone) | copy-start | bytes 100
  2.6 19.4 %all-to-all-start = ((bf16[8,64,640]{2,1,0:T(8,128)(2,1)}), bf16[8,64,640]{2,1,0:T(8,128)(2,1)S(1)}, u32[]{:S(2)}, u32[]{:S(2)}) async-start(bf16[8,64,640]{2,1,0:T(8,128)(2,1)} %broadcast_in_dim.6), calls=%async_computation | async-start | bytes 1310720 | tf_op jit(solution)/shard_map/all_to_all | solution.py:166
  10.4 14.7 %copy-start.6 = (f32[2,16,128]{2,1,0:T(8,128)S(1)}, f32[2,16,128]{2,1,0:T(8,128)}, u32[]{:S(2)}) copy-start(f32[2,16,128]{2,1,0:T(8,128)} %refs_4_.3) | copy-start | bytes 49156
  11.1 22.8 %copy-start.8 = (s32[8]{0:T(128)}, s32[8]{0:T(128)S(1)}, u32[]{:S(2)}) copy-start(s32[8]{0:T(128)S(1)} %fusion.7.heads_ref) | copy-start | bytes 100
  22.0 11.9 %copy-start.1 = (bf16[8,64,640]{2,1,0:T(8,128)(2,1)}, bf16[8,64,640]{2,1,0:T(8,128)(2,1)S(1)}, u32[]{:S(2)}) copy-start(bf16[8,64,640]{2,1,0:T(8,128)(2,1)S(1)} %all-to-all-done) | copy-start | bytes 1966084
  22.1 3.0 %collective-permute-start = (bf16[512,640]{1,0:T(8,128)(2,1)S(1)}, bf16[512,640]{1,0:T(8,128)(2,1)S(1)}, u32[]{:S(2)}, u32[]{:S(2)}) collective-permute-start(bf16[512,640]{1,0:T(8,128)(2,1)S(1)} %bitcast.29), channel_id=1, source_target_pairs={{0,16},{16,0},{32,48},{48,32},{64,80},{80,64},{96,112},{112,96},{1... | collective-permute-start | bytes 1966088 | tf_op jit(solution)/shard_map/ppermute | solution.py:181
  25.1 1.4 %copy-start.3 = (bf16[16,128,384]{2,1,0:T(8,128)(2,1)S(1)}, bf16[16,128,384]{2,1,0:T(8,128)(2,1)}, u32[]{:S(2)}) copy-start(bf16[16,128,384]{2,1,0:T(8,128)(2,1)} %refs_0_.3) | copy-start | bytes 4718596
  26.5 7.4 %copy-start.4 = (bf16[512,640]{1,0:T(8,128)(2,1)}, bf16[512,640]{1,0:T(8,128)(2,1)S(1)}, u32[]{:S(2)}) copy-start(bf16[512,640]{1,0:T(8,128)(2,1)S(1)} %collective-permute-done.refs_3_) | copy-start | bytes 1966084
  26.5 13.6 %copy-start.7 = (f32[2,16,128]{2,1,0:T(8,128)S(1)}, f32[2,16,128]{2,1,0:T(8,128)}, u32[]{:S(2)}) copy-start(f32[2,16,128]{2,1,0:T(8,128)} %refs_4_.3) | copy-start | bytes 49156
  33.9 21.6 %collective-permute-start.1 = (bf16[2,576,128]{2,1,0:T(8,128)(2,1)S(1)}, bf16[2,576,128]{2,1,0:T(8,128)(2,1)S(1)}, u32[]{:S(2)}, u32[]{:S(2)}) collective-permute-start(bf16[2,576,128]{2,1,0:T(8,128)(2,1)S(1)} %get-tuple-element.21), channel_id=1, source_target_pairs={{0,4},{2,6},{4,8},{6,10},{8,12},{10,14},{12,0},{14,2},{1,5},{3,7},... | collective-permute-start | bytes 884744 | tf_op jit(solution)/shard_map/step1/ppermute | solution.py:161
  37.0 18.6 %collective-permute-start.3 = (bf16[2,576,128]{2,1,0:T(8,128)(2,1)S(1)}, bf16[2,576,128]{2,1,0:T(8,128)(2,1)S(1)}, u32[]{:S(2)}, u32[]{:S(2)}) collective-permute-start(bf16[2,576,128]{2,1,0:T(8,128)(2,1)S(1)} %get-tuple-element.22), channel_id=1, source_target_pairs={{0,12},{2,14},{4,0},{6,2},{8,4},{10,6},{12,8},{14,10},{1,13},{3,15... | collective-permute-start | bytes 884744 | tf_op jit(solution)/shard_map/step1/ppermute | solution.py:161
  40.1 1.1 %copy-start.2 = (bf16[8,64,640]{2,1,0:T(8,128)(2,1)S(1)}, bf16[8,64,640]{2,1,0:T(8,128)(2,1)}, u32[]{:S(2)}) copy-start(bf16[8,64,640]{2,1,0:T(8,128)(2,1)} %copy-done.1) | copy-start | bytes 1966084
  41.2 1.1 %copy-start.5 = (bf16[512,640]{1,0:T(8,128)(2,1)S(1)}, bf16[512,640]{1,0:T(8,128)(2,1)}, u32[]{:S(2)}) copy-start(bf16[512,640]{1,0:T(8,128)(2,1)} %copy-done.4) | copy-start | bytes 1966084
  42.3 0.7 copy-start.9
  54.6 7.1 %collective-permute-start.7 = (bf16[512,640]{1,0:T(8,128)(2,1)S(1)}, bf16[512,640]{1,0:T(8,128)(2,1)S(1)}, u32[]{:S(2)}, u32[]{:S(2)}) collective-permute-start(bf16[512,640]{1,0:T(8,128)(2,1)S(1)} %get-tuple-element.24), channel_id=1, source_target_pairs={{0,16},{16,0},{32,48},{48,32},{64,80},{80,64},{96,112},{112,96},{1... | collective-permute-start | bytes 1966088 | tf_op jit(solution)/shard_map/ppermute | solution.py:203
  56.5 10.5 %collective-permute-start.5 = (bf16[2,384,128]{2,1,0:T(8,128)(2,1)}, bf16[2,384,128]{2,1,0:T(8,128)(2,1)S(1)}, u32[]{:S(2)}, u32[]{:S(2)}) collective-permute-start(bf16[2,384,128]{2,1,0:T(8,128)(2,1)} %get-tuple-element.35), channel_id=1, source_target_pairs={{0,2},{2,4},{4,6},{6,8},{8,10},{10,12},{12,14},{14,0},{1,3},{3,5},... | collective-permute-start | bytes 589832 | tf_op jit(solution)/shard_map/step2/ppermute | solution.py:161
  57.2 9.7 %collective-permute-start.6 = (bf16[2,384,128]{2,1,0:T(8,128)(2,1)}, bf16[2,384,128]{2,1,0:T(8,128)(2,1)S(1)}, u32[]{:S(2)}, u32[]{:S(2)}) collective-permute-start(bf16[2,384,128]{2,1,0:T(8,128)(2,1)} %get-tuple-element.36), channel_id=1, source_target_pairs={{0,14},{2,0},{4,2},{6,4},{8,6},{10,8},{12,10},{14,12},{1,15},{3,1}... | collective-permute-start | bytes 589832 | tf_op jit(solution)/shard_map/step2/ppermute | solution.py:161
  59.9 12.9 %collective-permute-start.4 = (bf16[2,384,128]{2,1,0:T(8,128)(2,1)}, bf16[2,384,128]{2,1,0:T(8,128)(2,1)}, u32[]{:S(2)}, u32[]{:S(2)}) collective-permute-start(bf16[2,384,128]{2,1,0:T(8,128)(2,1)} %pad_maximum_fusion.1), channel_id=1, source_target_pairs={{0,12},{2,14},{4,0},{6,2},{8,4},{10,6},{12,8},{14,10},{1,13},{3,15... | collective-permute-start | bytes 589832 | tf_op jit(solution)/shard_map/step2/ppermute | solution.py:161
  62.7 18.8 %all-to-all-start.1 = ((bf16[8,64,640]{2,1,0:T(8,128)(2,1)}), bf16[8,64,640]{2,1,0:T(8,128)(2,1)S(1)}, u32[]{:S(2)}, u32[]{:S(2)}) async-start(bf16[8,64,640]{2,1,0:T(8,128)(2,1)} %bitcast.13), calls=%async_computation.1 | async-start | bytes 1310720 | tf_op jit(solution)/shard_map/all_to_all | solution.py:215
  66.3 13.2 %collective-permute-start.2 = (bf16[2,384,128]{2,1,0:T(8,128)(2,1)S(1)}, bf16[2,384,128]{2,1,0:T(8,128)(2,1)S(1)}, u32[]{:S(2)}, u32[]{:S(2)}) collective-permute-start(bf16[2,384,128]{2,1,0:T(8,128)(2,1)S(1)} %pad_maximum_fusion), channel_id=1, source_target_pairs={{0,4},{2,6},{4,8},{6,10},{8,12},{10,14},{12,0},{14,2},{1,5},{3,7},... | collective-permute-start | bytes 589832 | tf_op jit(solution)/shard_map/step2/ppermute | solution.py:161

commit v4 on v3

v4 whole, which is shorter than its diff:
```python
import math

import jax
import jax.numpy as jnp
from jax import lax
from jax.experimental import pallas as pl
from jax.experimental.pallas import tpu as pltpu
from jax.sharding import PartitionSpec as P


DK = 192
DV = 128
QBLK = 64
LANES = 128
GROUPS = 2
WIN = 256
SCALE = 1.0 / math.sqrt(DK)
LOG2E = math.log2(math.e)
FAR = (3, 5, 4)
NEAR = (0, 1, 7, 2, 6)
KA = 8
GRANT = 67_000_000
NT = (((1,), (1,)), ((), ()))
NN = (((1,), (0,)), ((), ()))
VMEM = pl.BlockSpec(memory_space=pltpu.VMEM)
HBM = pl.BlockSpec(memory_space=pltpu.HBM)


def dot(a, b, dims):
    return lax.dot_general(a, b, dims, preferred_element_type=jnp.float32)


def pick(i, values):
    result = jnp.int32(values[0])
    for n, value in enumerate(values[1:], 1):
        result = jnp.where(i == n, jnp.int32(value), result)
    return result


def load_keys(copies, kv_buf, kz, vz, kt):
    half = kv_buf.shape[1]
    lane = lax.broadcasted_iota(jnp.int32, (half, WIN), 1)
    for side, copy in enumerate(copies):
        copy.wait()
        at = side * half
        for group in range(GROUPS):
            keep = (lane < DK) if group == 0 else (lane >= WIN - DK)
            lo = group * LANES
            vlo = 3 * LANES + lo
            first = 0 if group == 0 else WIN - DK
            k = jnp.where(keep, kv_buf[side, :, lo:lo + WIN], jnp.zeros((), jnp.bfloat16))
            kz[group, at:at + half, :] = k
            vz[group, at:at + half, :] = kv_buf[side, :, vlo:vlo + DV]
            kt[group, :, at:at + half] = k.T[first:first + DK, :]


def start_copies(owners, h_of, q_hbm, do_hbm, own_hbm, par_hbm, mask_hbm, q_buf, do_buf, kv_buf, mask_buf, sems, others):
    per_owner = q_buf.shape[1]
    keys = [
        pltpu.make_async_copy(own_hbm, kv_buf.at[0], others.at[0]),
        pltpu.make_async_copy(par_hbm, kv_buf.at[1], others.at[1]),
    ]
    mask = pltpu.make_async_copy(mask_hbm, mask_buf, others.at[2])
    for copy in keys:
        copy.start()

    def copies(i, h):
        return (
            pltpu.make_async_copy(q_hbm.at[pl.ds(h, per_owner)], q_buf.at[i], sems.at[0, i]),
            pltpu.make_async_copy(do_hbm.at[pl.ds(h, per_owner)], do_buf.at[i], sems.at[1, i]),
        )

    for i in range(owners):
        for copy in copies(i, h_of(i)):
            copy.start()
        if i == 0:
            mask.start()
    return keys, mask, copies


def group_terms(group, i, h, q_buf, do_buf, lse_ref, delta_ref, mask_ref, kz, vz):
    per_owner, count = q_buf.shape[1:3]
    rows = per_owner * count
    lo = group * LANES
    q = q_buf[i, :, :, lo:lo + WIN].reshape(rows, WIN)
    do = do_buf[i, :, :, lo:lo + DV].reshape(rows, DV)
    lse = jnp.concatenate([lse_ref[group, pl.ds(h + j, 1), :] for j in range(per_owner)], axis=1) * LOG2E
    delta = jnp.concatenate([delta_ref[group, pl.ds(h + j, 1), :] for j in range(per_owner)], axis=1)
    s = dot(kz[group], q, NT)
    dp = dot(vz[group], do, NT)
    p = jnp.exp2(s * (SCALE * LOG2E) - lse) * jnp.concatenate([mask_ref[...]] * per_owner, axis=1)
    ds = (p * (dp - delta)).astype(jnp.bfloat16)
    return q, do, p.astype(jnp.bfloat16), ds


def far_kernel(q_hbm, do_hbm, own_hbm, par_hbm, mask_hbm, lse_ref, delta_ref, right, left,
               q_buf, do_buf, kv_buf, mask_ref, kz, vz, kt, held, sems, others):
    per_owner, _, count = right.shape
    me = lax.axis_index("ka")
    h_of = lambda i: per_owner * lax.rem(me + pick(i, FAR), KA)
    key_copies, mask_copy, copies = start_copies(
        len(FAR), h_of, q_hbm, do_hbm, own_hbm, par_hbm, mask_hbm, q_buf, do_buf, kv_buf, mask_ref, sems, others)
    load_keys(key_copies, kv_buf, kz, vz, kt)
    mask_copy.wait()

    def one(i, carry):
        h = h_of(i)
        for copy in copies(i, h):
            copy.wait()
        for group in range(GROUPS):
            _, _, _, ds = group_terms(group, i, h, q_buf, do_buf, lse_ref, delta_ref, mask_ref, kz, vz)
            dqt = dot(kt[group], ds, NN) * SCALE
            for j in range(per_owner):
                held[i, j, group * DK:(group + 1) * DK, :] = dqt[:, j * count:(j + 1) * count].astype(held.dtype)
        return carry

    lax.fori_loop(0, len(FAR), one, 0)
    width = GROUPS * DK
    right[:, :width, :] = held[0]
    left[:, :width, :] = held[1]
    right[:, width:, :] = held[2, :, :DK, :]
    left[:, width:, :] = held[2, :, DK:, :]


def near_kernel(q_hbm, do_hbm, own_hbm, par_hbm, mask_hbm, lse_ref, delta_ref, after, home, near, own_out, par_out,
                q_buf, do_buf, kv_buf, mask_ref, kz, vz, kt, acc_k, acc_v, near_buf, sems, others):
    del after
    per_owner, _, count = home.shape
    half = own_out.shape[0]
    me = lax.axis_index("ka")
    steps = NEAR + FAR
    h_of = lambda i: per_owner * lax.rem(me + pick(i, steps), KA)
    key_copies, mask_copy, copies = start_copies(
        KA, h_of, q_hbm, do_hbm, own_hbm, par_hbm, mask_hbm, q_buf, do_buf, kv_buf, mask_ref, sems, others)
    load_keys(key_copies, kv_buf, kz, vz, kt)
    mask_copy.wait()
    acc_k[...] = jnp.zeros_like(acc_k)
    acc_v[...] = jnp.zeros_like(acc_v)

    def one(i, query_grads):
        h = h_of(i)
        for copy in copies(i, h):
            copy.wait()
        for group in range(GROUPS):
            q, do, p, ds = group_terms(group, i, h, q_buf, do_buf, lse_ref, delta_ref, mask_ref, kz, vz)
            acc_v[group] += dot(p, do, NN)
            acc_k[group] += dot(ds, q, NN)
            if query_grads is not None:
                dqt = dot(kt[group], ds, NN) * SCALE
                for j in range(per_owner):
                    query_grads(j, slice(group * DK, (group + 1) * DK), dqt[:, j * count:(j + 1) * count])


    def near_one(i, carry):
        def to_near(j, where, value):
            near_buf[i, j, where, :] = value

        one(i, to_near)
        return carry

    def far_one(i, carry):
        one(i, None)
        return carry

    lax.fori_loop(0, len(NEAR), near_one, 0)
    results = (
        pltpu.make_async_copy(near_buf.at[0], home, others.at[0]),
        pltpu.make_async_copy(near_buf.at[pl.ds(1, len(NEAR) - 1)], near, others.at[1]),
    )
    for copy in results:
        copy.start()
    lax.fori_loop(len(NEAR), KA, far_one, 0)
    low = lax.broadcasted_iota(jnp.int32, (half, LANES), 1) < DK - LANES
    for side, out in enumerate((own_out, par_out)):
        at = side * half
        a = acc_k[0, at:at + half, :] * SCALE
        b = acc_k[1, at:at + half, :] * SCALE
        out[:, :LANES] = a[:, :LANES].astype(out.dtype)
        out[:, LANES:2 * LANES] = jnp.where(low, a[:, LANES:], b[:, :LANES]).astype(out.dtype)
        out[:, 2 * LANES:3 * LANES] = b[:, LANES:].astype(out.dtype)
        for group in range(GROUPS):
            vlo = (3 + group) * LANES
            out[:, vlo:vlo + DV] = acc_v[group, at:at + half, :].astype(out.dtype)
    for copy in results:
        copy.wait()


def grads(kernel, owners, matmuls, outs, out_specs, scratch, q, do, own, par, mask, lse, delta, *after):
    heads, count, width = q.shape
    per_owner = heads // KA
    keys = 2 * own.shape[0]
    bf16 = jnp.bfloat16
    return pl.pallas_call(
        kernel,
        out_shape=outs,
        in_specs=[HBM] * 5 + [VMEM] * 2 + [HBM] * len(after),
        out_specs=out_specs,
        scratch_shapes=[
            pltpu.VMEM((owners, per_owner, count, width), bf16),
            pltpu.VMEM((owners, per_owner, count, do.shape[2]), bf16),
            pltpu.VMEM((2, *own.shape), bf16),
            pltpu.VMEM(mask.shape, mask.dtype),
            pltpu.VMEM((GROUPS, keys, WIN), bf16),
            pltpu.VMEM((GROUPS, keys, DV), bf16),
            pltpu.VMEM((GROUPS, DK, keys), bf16),
            *scratch,
            pltpu.SemaphoreType.DMA((2, owners)),
            pltpu.SemaphoreType.DMA((3,)),
        ],
        cost_estimate=pl.CostEstimate(
            flops=2 * GROUPS * owners * per_owner * count * keys * matmuls, bytes_accessed=6_000_000,
            transcendentals=GROUPS * owners * per_owner * count * keys),
        compiler_params=pltpu.CompilerParams(vmem_limit_bytes=GRANT),
    )(q, do, own, par, mask, lse, delta, *after)


def small(kernel, outs, *args, out_specs=None):
    return pl.pallas_call(
        kernel,
        out_shape=outs,
        in_specs=[VMEM] * len(args),
        out_specs=out_specs or tuple(VMEM for _ in outs),
        compiler_params=pltpu.CompilerParams(vmem_limit_bytes=16 * 1024 * 1024),
    )(*args)


def copies_kernel(keys, values, out):
    width = keys.shape[1]
    for i in range(out.shape[0]):
        out[i, :, :width] = keys[...]
        out[i, :, width:] = values[...]


def message_kernel(near, from_left, from_right, up2, down2, up1, down1):
    f32, bf16 = jnp.float32, jnp.bfloat16
    width = up1.shape[1]
    up1[...] = (near[0] + from_left[:, :width, :].astype(f32)).astype(bf16)
    down1[...] = (near[1] + from_right[:, :width, :].astype(f32)).astype(bf16)
    up2[:, :DK, :] = (near[2, :, :DK, :] + from_left[:, width:, :].astype(f32)).astype(bf16)
    up2[:, DK:, :] = near[2, :, DK:, :].astype(bf16)
    down2[:, :DK, :] = near[3, :, :DK, :].astype(bf16)
    down2[:, DK:, :] = (near[3, :, DK:, :] + from_right[:, width:, :].astype(f32)).astype(bf16)


def finish_kernel(home, a, b, c, d, pieces, dq, dk, dv):
    f32 = jnp.float32
    for j in range(home.shape[0]):
        total = home[j] + ((a[j].astype(f32) + b[j].astype(f32)) + (c[j].astype(f32) + d[j].astype(f32)))
        dq[j] = total.T
    kv = pieces[0].astype(f32)
    for i in range(1, pieces.shape[0]):
        kv = kv + pieces[i].astype(f32)
    width = dk.shape[1]
    dk[...] = kv[:, :width]
    dv[...] = kv[:, width:]


def per_device(queries, comp_keys, comp_values, outputs, grad_out, log_sums, visible):
    pb = lax.axis_size("pb")
    ka = lax.axis_size("ka")
    chips = pb // 2
    core = lax.rem(lax.axis_index("pb"), 2)
    same_core = [[2 * i + c for i in range(chips)] for c in range(2)]
    other_core = [(i, i ^ 1) for i in range(pb)]
    rows, width = comp_keys.shape
    both = width + comp_values.shape[1]
    heads, count, _ = queries.shape
    per_owner = heads // ka
    keys = 2 * chips * rows
    half = keys // 2
    f32, bf16 = jnp.float32, jnp.bfloat16
    shape = jax.ShapeDtypeStruct

    def along(x, step):
        return lax.ppermute(x, "ka", [(i, (i + step) % ka) for i in range(ka)])

    (copies,) = small(copies_kernel, (shape((chips, rows, both), bf16),), comp_keys, comp_values)
    own = lax.all_to_all(copies, "pb", 0, 0, axis_index_groups=same_core, tiled=True).reshape(half, both)
    delta = jnp.stack([
        jnp.sum(
            grad_out[:, :, g * DV:(g + 1) * DV].astype(f32) * outputs[:, :, g * DV:(g + 1) * DV].astype(f32), axis=2
        )
        for g in range(GROUPS)
    ])
    seen = visible.reshape(visible.shape[0], chips, 2, rows)
    seen = jnp.where(core == 0, seen, seen[:, :, ::-1])
    seen = seen.transpose(2, 1, 3, 0).reshape(keys, visible.shape[0])
    mask = jnp.repeat(seen.astype(f32), QBLK, axis=1)
    own, delta, mask = lax.optimization_barrier((own, delta, mask))
    par = lax.ppermute(own, "pb", other_core)

    args = (queries, grad_out, own, par, mask, log_sums, delta)
    hops = shape((per_owner, width + DK, count), bf16)
    chunk = (per_owner, width, count)
    right, left = grads(
        far_kernel, len(FAR), 2 * DK + DV, (hops, hops), (VMEM, VMEM), [pltpu.VMEM((len(FAR), *chunk), bf16)], *args
    )
    from_left = along(right, 2)
    from_right = along(left, -2)
    home, near, own_kv, par_kv = grads(
        near_kernel, KA, 3 * DK + 2 * DV,
        (shape(chunk, f32), shape((len(NEAR) - 1, *chunk), f32), shape((half, both), f32), shape((half, both), bf16)),
        (HBM, HBM, VMEM, VMEM),
        [
            pltpu.VMEM((GROUPS, keys, WIN), f32),
            pltpu.VMEM((GROUPS, keys, DV), f32),
            pltpu.VMEM((len(NEAR), *chunk), f32),
        ],
        *args, right,
    )
    from_other = lax.ppermute(par_kv, "pb", other_core)

    messages = small(message_kernel, (shape(chunk, bf16),) * 4, near, from_left, from_right)
    arrived = [along(x, step) for x, step in zip(messages, (2, -2, 1, -1))]
    chip_sum = (own_kv + from_other.astype(f32)).astype(bf16)
    pieces = lax.all_to_all(
        chip_sum.reshape(chips, rows, both), "pb", 0, 0, axis_index_groups=same_core, tiled=True
    )
    return small(
        finish_kernel,
        (shape((per_owner, count, width), f32), shape((rows, width), f32), shape((rows, both - width), f32)),
        home, *arrived, pieces,
    )


def solution(mesh):
    return jax.shard_map(
        per_device,
        mesh=mesh,
        in_specs=(
            P(None, "pb", "ga"),
            P(("ka", "pb"), "ga"),
            P(("ka", "pb"), "ga"),
            P(None, "pb", "ga"),
            P(None, "pb", "ga"),
            P("ga", None, "pb"),
            P("pb", "ka"),
        ),
        out_specs=(P("ka", "pb", "ga"), P(("ka", "pb"), "ga"), P(("ka", "pb"), "ga")),
        check_vma=False,
    )
```

time: 83.3 us -> 95.5 us (1.15)
  waiting for transfers between devices: 25.1 us -> 36.6 us
  Pallas kernels: 19 us -> 24.8 us
  local copies, waits for them, and re-layouts: 7.82 us -> 3.49 us
  other arithmetic: 5.6 us -> 3.68 us
    ppermute x6, waiting for transfers between devices: 12.6 us -> 24.1 us  [along(): return lax.ppermute(x, 'ka', [(i, (i + step) % ka) for i in range(ka)])]
    pallas_call x2 -> x5, Pallas kernels: 19 us -> 24.8 us  [the longest x2 22.9 us: grads(): pl.pallas_call(kernel, out_shape=outs, in_specs=[HBM] * 5 + [VMEM] * 2 +...]
    unnamed x27 -> x18, local copies, waits for them, and re-layouts: 5.19 us -> 1.58 us
    ppermute x1, waiting for transfers between devices: 0.01 us -> 1.93 us  [per_device(): from_other = lax.ppermute(par_kv, 'pb', other_core)]
    concatenate x3 -> x0, other arithmetic: 1.69 us -> none  [the longest x1 0.97 us: per_device(): both = jnp.concatenate([comp_keys, comp_values], axis=1)]
    convert_element_type x1, other arithmetic: 1.03 us -> 2.45 us  [per_device(): chip_sum = (own_kv + from_other.astype(f32)).astype(bf16)]
    slice x2 -> x0, local copies, waits for them, and re-layouts: 1.28 us -> none  [per_device(): return (dq.transpose(0, 2, 1), kv[:, :width], kv[:, width:])]
    all_to_all x2, waiting for transfers between devices: 10.9 us -> 9.71 us  [the longest x1 9.71 us: per_device(): lax.all_to_all(copies, 'pb', 0, 0, axis_index_groups=same_core, tiled=True)]
  transfers between devices with their start and end apart: 10 -> 10, of which waited for: 4 -> 8; matrix products, arithmetic and copies ran while one was open for 7% -> 3% of each run, Pallas kernels for 14% -> 0%
where the time goes in v4:
time: 95.5 us; the launch traced here: 94.8 us
  waiting for transfers between devices  36.6 us (38%)
  starting transfers between devices  25.4 us (27%)
  Pallas kernels  24.8 us (26%)
  other arithmetic  3.68 us (4%)
  local copies, waits for them, and re-layouts  3.49 us (4%)
    ppermute x6, waiting for transfers between devices, along(): return lax.ppermute(x, 'ka', [(i, (i + step) % ka) for i in range(ka)])  24.1 us
    pallas_call x2, Pallas kernels, grads(): pl.pallas_call(kernel, out_shape=outs, in_specs=[HBM] * 5 + [VMEM] * 2 +...  22.9 us
    ppermute x6, starting transfers between devices, along(): return lax.ppermute(x, 'ka', [(i, (i + step) % ka) for i in range(ka)])  12.5 us
    all_to_all x1, waiting for transfers between devices, per_device(): lax.all_to_all(copies, 'pb', 0, 0, axis_index_groups=same_core, tiled=True)  9.71 us
    all_to_all x1, starting transfers between devices, per_device(): lax.all_to_all(copies, 'pb', 0, 0, axis_index_groups=same_core, tiled=True)  7.47 us
    all_to_all x1, starting transfers between devices, per_device(): lax.all_to_all(chip_sum.reshape(chips, rows, both), 'pb', 0, 0, axis_inde...  3.67 us
    convert_element_type x1, other arithmetic, per_device(): chip_sum = (own_kv + from_other.astype(f32)).astype(bf16)  2.45 us
    pallas_call x3, Pallas kernels, small(): pl.pallas_call(kernel, out_shape=outs, in_specs=[VMEM] * len(args), out_s...  1.96 us
  transfers between devices with their start and end apart: 10, of which 8 were waited for; matrix products, arithmetic and copies ran while one was open for 3% of the time, Pallas kernels for 0%

profile of v4, /device:TPU:1, one launch (start us, length us, event | category | flops | bytes accessed | tf_op | source)
XLA Modules:
  0.0 94.8 jit_solution(15726753255011901562)
XLA Ops:
  0.6 0.8 copy-done.2
  1.4 0.8 copy-done.3
  2.2 0.9 shard_map.94
  3.1 7.5 %all-to-all-start = ((bf16[8,64,640]{2,1,0:T(8,128)(2,1)}), bf16[8,64,640]{2,1,0:T(8,128)(2,1)S(1)}, u32[]{:S(2)}, u32[]{:S(2)}) async-start(bf16[8,64,640]{2,1,0:T(8,128)(2,1)} %shard_map.94), calls=%async_computation | async-start | bytes 1310720 | tf_op jit(solution)/shard_map/all_to_all | solution.py:278
  10.6 0.8 reshape.21
  11.4 0.1 convert_element_type.33
  11.5 0.6 multiply_reduce_fusion.1
  12.1 0.6 pad_maximum_fusion.delta_ref
  12.7 9.7 %all-to-all-done = bf16[8,64,640]{2,1,0:T(8,128)(2,1)S(1)} async-done(((bf16[8,64,640]{2,1,0:T(8,128)(2,1)}), bf16[8,64,640]{2,1,0:T(8,128)(2,1)S(1)}, u32[]{:S(2)}, u32[]{:S(2)}) %all-to-all-start) | async-done | bytes 655392 | tf_op jit(solution)/shard_map/all_to_all | solution.py:278
  22.5 1.3 %collective-permute-start = (bf16[512,640]{1,0:T(8,128)(2,1)S(1)}, bf16[512,640]{1,0:T(8,128)(2,1)}, u32[]{:S(2)}, u32[]{:S(2)}) collective-permute-start(bf16[512,640]{1,0:T(8,128)(2,1)S(1)} %bitcast.12), channel_id=1, source_target_pairs={{0,16},{16,0},{32,48},{48,32},{64,80},{80,64},{96,112},{112,96},{1... | collective-permute-start | bytes 1966088 | tf_op jit(solution)/shard_map/ppermute | solution.py:290
  23.8 1.0 %copy.13.mask_hbm = f32[1024,128]{1,0:T(8,128)} copy(f32[1024,128]{0,1:T(8,128)S(1)} %bitcast.11) | data formatting | bytes 1048576 | tf_op jit(solution)/shard_map/optimization_barrier | solution.py:289
  24.8 0.9 collective-permute-done.par_hbm
  25.6 6.6 %shard_map.95 = (bf16[2,576,128]{2,1,0:T(8,128)(2,1)}, bf16[2,576,128]{2,1,0:T(8,128)(2,1)}) custom-call(bf16[16,128,384]{2,1,0:T(8,128)(2,1)} %q_hbm.3, bf16[16,128,256]{2,1,0:T(8,128)(2,1)} %do_hbm.3, bf16[512,640]{1,0:T(8,128)(2,1)} %bitcast.13, bf16[512,640]{1,0:T(8,128)(2,1)} %collective-permute-done.par_hbm, f32[1024,128]{1,0:T(8,128)} %copy.13.mask_hbm, ...), custom_call_target="tpu_custom_call" | custom-call | flops 1610612736 | bytes 6000000 | tf_op jit(solution)/shard_map/pallas_call | solution.py:193
  32.3 16.2 %shard_map.96 = (f32[2,384,128]{2,1,0:T(8,128)}, f32[4,2,384,128]{3,2,1,0:T(8,128)}, f32[512,640]{1,0:T(8,128)}, bf16[512,640]{1,0:T(8,128)(2,1)}) custom-call(bf16[16,128,384]{2,1,0:T(8,128)(2,1)} %q_hbm.3, bf16[16,128,256]{2,1,0:T(8,128)(2,1)} %do_hbm.3, bf16[512,640]{1,0:T(8,128)(2,1)} %bitcast.14, bf16[512,640]{1,0:T(8,128)(2,1)} %collective-permute-done.par_hbm, ...), custom_call_target="tpu_custom_call" | custom-call | flops 6979321856 | bytes 6000000 | tf_op jit(solution)/shard_map/pallas_call | solution.py:193
  48.5 0.5 collective-permute-start.7
  49.0 1.9 %collective-permute-done.7 = bf16[512,640]{1,0:T(8,128)(2,1)S(1)} collective-permute-done((bf16[512,640]{1,0:T(8,128)(2,1)}, bf16[512,640]{1,0:T(8,128)(2,1)S(1)}, u32[]{:S(2)}, u32[]{:S(2)}) %collective-permute-start.7) | collective-permute-done | bytes 655392 | tf_op jit(solution)/shard_map/ppermute | solution.py:311
  50.9 2.4 %add_convert_fusion = bf16[512,640]{1,0:T(8,128)(2,1)} fusion(f32[512,640]{1,0:T(8,128)} %get-tuple-element.27, bf16[512,640]{1,0:T(8,128)(2,1)S(1)} %collective-permute-done.7), kind=kLoop, calls=%fused_computation | loop fusion | flops 983040 | bytes 2621440 | tf_op jit(solution)/shard_map/convert_element_type | solution.py:315
  53.4 3.7 %all-to-all-start.1 = ((bf16[8,64,640]{2,1,0:T(8,128)(2,1)}), bf16[8,64,640]{2,1,0:T(8,128)(2,1)S(1)}, u32[]{:S(2)}, u32[]{:S(2)}) async-start(bf16[8,64,640]{2,1,0:T(8,128)(2,1)} %bitcast.5), calls=%async_computation.1 | async-start | bytes 1310720 | tf_op jit(solution)/shard_map/all_to_all | solution.py:316
  57.1 0.0 copy-start.1
  57.1 3.1 %collective-permute-start.1 = (bf16[2,576,128]{2,1,0:T(8,128)(2,1)S(1)}, bf16[2,576,128]{2,1,0:T(8,128)(2,1)S(1)}, u32[]{:S(2)}, u32[]{:S(2)}) collective-permute-start(bf16[2,576,128]{2,1,0:T(8,128)(2,1)S(1)} %copy-done.8), channel_id=1, source_target_pairs={{0,4},{2,6},{4,8},{6,10},{8,12},{10,14},{12,0},{14,2},{1,5},{3,7},... | collective-permute-start | bytes 884744 | tf_op jit(solution)/shard_map/ppermute | solution.py:275
  60.1 3.1 %collective-permute-start.2 = (bf16[2,576,128]{2,1,0:T(8,128)(2,1)S(1)}, bf16[2,576,128]{2,1,0:T(8,128)(2,1)S(1)}, u32[]{:S(2)}, u32[]{:S(2)}) collective-permute-start(bf16[2,576,128]{2,1,0:T(8,128)(2,1)S(1)} %copy-done.7), channel_id=1, source_target_pairs={{0,12},{2,14},{4,0},{6,2},{8,4},{10,6},{12,8},{14,10},{1,13},{3,15... | collective-permute-start | bytes 884744 | tf_op jit(solution)/shard_map/ppermute | solution.py:275
  63.3 8.9 %collective-permute-done.1.from_left = bf16[2,576,128]{2,1,0:T(8,128)(2,1)S(1)} collective-permute-done((bf16[2,576,128]{2,1,0:T(8,128)(2,1)S(1)}, bf16[2,576,128]{2,1,0:T(8,128)(2,1)S(1)}, u32[]{:S(2)}, u32[]{:S(2)}) %collective-permute-start.1) | collective-permute-done | bytes 294944 | tf_op jit(solution)/shard_map/ppermute | solution.py:275
  72.1 5.6 %collective-permute-done.2.from_right = bf16[2,576,128]{2,1,0:T(8,128)(2,1)S(1)} collective-permute-done((bf16[2,576,128]{2,1,0:T(8,128)(2,1)S(1)}, bf16[2,576,128]{2,1,0:T(8,128)(2,1)S(1)}, u32[]{:S(2)}, u32[]{:S(2)}) %collective-permute-start.2) | collective-permute-done | bytes 294944 | tf_op jit(solution)/shard_map/ppermute | solution.py:275
  77.7 0.1 shard_map.97
  77.8 3.5 %collective-permute-start.3 = (bf16[2,384,128]{2,1,0:T(8,128)(2,1)S(1)}, bf16[2,384,128]{2,1,0:T(8,128)(2,1)S(1)}, u32[]{:S(2)}, u32[]{:S(2)}) collective-permute-start(bf16[2,384,128]{2,1,0:T(8,128)(2,1)S(1)} %get-tuple-element.23), channel_id=1, source_target_pairs={{0,4},{2,6},{4,8},{6,10},{8,12},{10,14},{12,0},{14,2},{1,5},{3,7},... | collective-permute-start | bytes 589832 | tf_op jit(solution)/shard_map/ppermute | solution.py:275
  81.3 0.2 collective-permute-start.4
  81.4 0.0 collective-permute-start.5
  81.5 2.7 %collective-permute-start.6 = (bf16[2,384,128]{2,1,0:T(8,128)(2,1)S(1)}, bf16[2,384,128]{2,1,0:T(8,128)(2,1)S(1)}, u32[]{:S(2)}, u32[]{:S(2)}) collective-permute-start(bf16[2,384,128]{2,1,0:T(8,128)(2,1)S(1)} %get-tuple-element.26), channel_id=1, source_target_pairs={{0,14},{2,0},{4,2},{6,4},{8,6},{10,8},{12,10},{14,12},{1,15},{3,1}... | collective-permute-start | bytes 589832 | tf_op jit(solution)/shard_map/ppermute | solution.py:275
  84.1 5.5 %collective-permute-done.3.a = bf16[2,384,128]{2,1,0:T(8,128)(2,1)S(1)} collective-permute-done((bf16[2,384,128]{2,1,0:T(8,128)(2,1)S(1)}, bf16[2,384,128]{2,1,0:T(8,128)(2,1)S(1)}, u32[]{:S(2)}, u32[]{:S(2)}) %collective-permute-start.3) | collective-permute-done | bytes 196640 | tf_op jit(solution)/shard_map/ppermute | solution.py:275
  89.7 3.9 %collective-permute-done.5.c = bf16[2,384,128]{2,1,0:T(8,128)(2,1)S(1)} collective-permute-done((bf16[2,384,128]{2,1,0:T(8,128)(2,1)S(1)}, bf16[2,384,128]{2,1,0:T(8,128)(2,1)S(1)}, u32[]{:S(2)}, u32[]{:S(2)}) %collective-permute-start.5) | collective-permute-done | bytes 196640 | tf_op jit(solution)/shard_map/ppermute | solution.py:275
  93.6 0.2 collective-permute-done.6.d
  93.8 0.9 shard_map.98
  (20 shorter events, 0.1 us)
Async XLA Ops:
  0.6 0.8 copy-start.2
  1.4 0.8 copy-start.3
  2.2 9.3 %copy-start.4 = (bf16[16,128,256]{2,1,0:T(8,128)(2,1)S(1)}, bf16[16,128,256]{2,1,0:T(8,128)(2,1)}, u32[]{:S(2)}) copy-start(bf16[16,128,256]{2,1,0:T(8,128)(2,1)} %param.10) | copy-start | bytes 3145732
  2.2 9.3 %copy-start.5 = (bf16[16,128,256]{2,1,0:T(8,128)(2,1)S(1)}, bf16[16,128,256]{2,1,0:T(8,128)(2,1)}, u32[]{:S(2)}) copy-start(bf16[16,128,256]{2,1,0:T(8,128)(2,1)} %do_hbm.3) | copy-start | bytes 3145732
  3.1 19.3 %all-to-all-start = ((bf16[8,64,640]{2,1,0:T(8,128)(2,1)}), bf16[8,64,640]{2,1,0:T(8,128)(2,1)S(1)}, u32[]{:S(2)}, u32[]{:S(2)}) async-start(bf16[8,64,640]{2,1,0:T(8,128)(2,1)} %shard_map.94), calls=%async_computation | async-start | bytes 1310720 | tf_op jit(solution)/shard_map/all_to_all | solution.py:278
  22.4 2.4 %copy-start.6 = (bf16[8,64,640]{2,1,0:T(8,128)(2,1)}, bf16[8,64,640]{2,1,0:T(8,128)(2,1)S(1)}, u32[]{:S(2)}) copy-start(bf16[8,64,640]{2,1,0:T(8,128)(2,1)S(1)} %all-to-all-done) | copy-start | bytes 1966084
  22.5 3.2 %collective-permute-start = (bf16[512,640]{1,0:T(8,128)(2,1)S(1)}, bf16[512,640]{1,0:T(8,128)(2,1)}, u32[]{:S(2)}, u32[]{:S(2)}) collective-permute-start(bf16[512,640]{1,0:T(8,128)(2,1)S(1)} %bitcast.12), channel_id=1, source_target_pairs={{0,16},{16,0},{32,48},{48,32},{64,80},{80,64},{96,112},{112,96},{1... | collective-permute-start | bytes 1966088 | tf_op jit(solution)/shard_map/ppermute | solution.py:290
  48.5 2.4 %collective-permute-start.7 = (bf16[512,640]{1,0:T(8,128)(2,1)}, bf16[512,640]{1,0:T(8,128)(2,1)S(1)}, u32[]{:S(2)}, u32[]{:S(2)}) collective-permute-start(bf16[512,640]{1,0:T(8,128)(2,1)} %get-tuple-element.28), channel_id=1, source_target_pairs={{0,16},{16,0},{32,48},{48,32},{64,80},{80,64},{96,112},{112,96},{1... | collective-permute-start | bytes 1966088 | tf_op jit(solution)/shard_map/ppermute | solution.py:311
  50.9 26.8 %copy-start = (f32[4,2,384,128]{3,2,1,0:T(8,128)S(1)}, f32[4,2,384,128]{3,2,1,0:T(8,128)}, u32[]{:S(2)}) copy-start(f32[4,2,384,128]{3,2,1,0:T(8,128)} %get-tuple-element.21.near) | copy-start | bytes 4718596
  53.4 3.7 %copy-start.8 = (bf16[2,576,128]{2,1,0:T(8,128)(2,1)S(1)}, bf16[2,576,128]{2,1,0:T(8,128)(2,1)}, u32[]{:S(2)}) copy-start(bf16[2,576,128]{2,1,0:T(8,128)(2,1)} %get-tuple-element.19.after) | copy-start | bytes 884740
  53.4 6.8 %copy-start.7 = (bf16[2,576,128]{2,1,0:T(8,128)(2,1)S(1)}, bf16[2,576,128]{2,1,0:T(8,128)(2,1)}, u32[]{:S(2)}) copy-start(bf16[2,576,128]{2,1,0:T(8,128)(2,1)} %get-tuple-element.22) | copy-start | bytes 884740
  53.4 40.5 %all-to-all-start.1 = ((bf16[8,64,640]{2,1,0:T(8,128)(2,1)}), bf16[8,64,640]{2,1,0:T(8,128)(2,1)S(1)}, u32[]{:S(2)}, u32[]{:S(2)}) async-start(bf16[8,64,640]{2,1,0:T(8,128)(2,1)} %bitcast.5), calls=%async_computation.1 | async-start | bytes 1310720 | tf_op jit(solution)/shard_map/all_to_all | solution.py:316
  57.1 36.8 %copy-start.1 = (f32[2,384,128]{2,1,0:T(8,128)S(1)}, f32[2,384,128]{2,1,0:T(8,128)}, u32[]{:S(2)}) copy-start(f32[2,384,128]{2,1,0:T(8,128)} %get-tuple-element.20.home) | copy-start | bytes 1179652
  57.1 15.0 %collective-permute-start.1 = (bf16[2,576,128]{2,1,0:T(8,128)(2,1)S(1)}, bf16[2,576,128]{2,1,0:T(8,128)(2,1)S(1)}, u32[]{:S(2)}, u32[]{:S(2)}) collective-permute-start(bf16[2,576,128]{2,1,0:T(8,128)(2,1)S(1)} %copy-done.8), channel_id=1, source_target_pairs={{0,4},{2,6},{4,8},{6,10},{8,12},{10,14},{12,0},{14,2},{1,5},{3,7},... | collective-permute-start | bytes 884744 | tf_op jit(solution)/shard_map/ppermute | solution.py:275
  60.1 17.5 %collective-permute-start.2 = (bf16[2,576,128]{2,1,0:T(8,128)(2,1)S(1)}, bf16[2,576,128]{2,1,0:T(8,128)(2,1)S(1)}, u32[]{:S(2)}, u32[]{:S(2)}) collective-permute-start(bf16[2,576,128]{2,1,0:T(8,128)(2,1)S(1)} %copy-done.7), channel_id=1, source_target_pairs={{0,12},{2,14},{4,0},{6,2},{8,4},{10,6},{12,8},{14,10},{1,13},{3,15... | collective-permute-start | bytes 884744 | tf_op jit(solution)/shard_map/ppermute | solution.py:275
  77.8 11.9 %collective-permute-start.3 = (bf16[2,384,128]{2,1,0:T(8,128)(2,1)S(1)}, bf16[2,384,128]{2,1,0:T(8,128)(2,1)S(1)}, u32[]{:S(2)}, u32[]{:S(2)}) collective-permute-start(bf16[2,384,128]{2,1,0:T(8,128)(2,1)S(1)} %get-tuple-element.23), channel_id=1, source_target_pairs={{0,4},{2,6},{4,8},{6,10},{8,12},{10,14},{12,0},{14,2},{1,5},{3,7},... | collective-permute-start | bytes 589832 | tf_op jit(solution)/shard_map/ppermute | solution.py:275
  81.3 8.4 %collective-permute-start.4 = (bf16[2,384,128]{2,1,0:T(8,128)(2,1)S(1)}, bf16[2,384,128]{2,1,0:T(8,128)(2,1)S(1)}, u32[]{:S(2)}, u32[]{:S(2)}) collective-permute-start(bf16[2,384,128]{2,1,0:T(8,128)(2,1)S(1)} %get-tuple-element.24), channel_id=1, source_target_pairs={{0,12},{2,14},{4,0},{6,2},{8,4},{10,6},{12,8},{14,10},{1,13},{3,15... | collective-permute-start | bytes 589832 | tf_op jit(solution)/shard_map/ppermute | solution.py:275
  81.4 12.1 %collective-permute-start.5 = (bf16[2,384,128]{2,1,0:T(8,128)(2,1)S(1)}, bf16[2,384,128]{2,1,0:T(8,128)(2,1)S(1)}, u32[]{:S(2)}, u32[]{:S(2)}) collective-permute-start(bf16[2,384,128]{2,1,0:T(8,128)(2,1)S(1)} %get-tuple-element.25), channel_id=1, source_target_pairs={{0,2},{2,4},{4,6},{6,8},{8,10},{10,12},{12,14},{14,0},{1,3},{3,5},... | collective-permute-start | bytes 589832 | tf_op jit(solution)/shard_map/ppermute | solution.py:275
  81.5 12.4 %collective-permute-start.6 = (bf16[2,384,128]{2,1,0:T(8,128)(2,1)S(1)}, bf16[2,384,128]{2,1,0:T(8,128)(2,1)S(1)}, u32[]{:S(2)}, u32[]{:S(2)}) collective-permute-start(bf16[2,384,128]{2,1,0:T(8,128)(2,1)S(1)} %get-tuple-element.26), channel_id=1, source_target_pairs={{0,14},{2,0},{4,2},{6,4},{8,6},{10,8},{12,10},{14,12},{1,15},{3,1}... | collective-permute-start | bytes 589832 | tf_op jit(solution)/shard_map/ppermute | solution.py:275

commit v5 on v4

--- a/solution.py
+++ b/solution.py
@@ -37,28 +37,29 @@
     return result
 
 
-def load_keys(copies, kv_buf, kz, vz, kt):
-    half = kv_buf.shape[1]
+def load_keys(copies, kv_buf, kz, kt):
+    half = kv_buf.shape[0] // 2
     lane = lax.broadcasted_iota(jnp.int32, (half, WIN), 1)
+    one = lax.broadcasted_iota(jnp.int32, (DK, WIN), 0)
+    column = lax.broadcasted_iota(jnp.int32, (DK, WIN), 1)
     for side, copy in enumerate(copies):
         copy.wait()
         at = side * half
         for group in range(GROUPS):
-            keep = (lane < DK) if group == 0 else (lane >= WIN - DK)
+            first = 0 if group == 0 else WIN - DK
+            keep = (lane >= first) & (lane < first + DK)
             lo = group * LANES
-            vlo = 3 * LANES + lo
-            first = 0 if group == 0 else WIN - DK
-            k = jnp.where(keep, kv_buf[side, :, lo:lo + WIN], jnp.zeros((), jnp.bfloat16))
+            k = jnp.where(keep, kv_buf[at:at + half, lo:lo + WIN], jnp.zeros((), jnp.bfloat16))
             kz[group, at:at + half, :] = k
-            vz[group, at:at + half, :] = kv_buf[side, :, vlo:vlo + DV]
-            kt[group, :, at:at + half] = k.T[first:first + DK, :]
+            turn = jnp.where(column == one + first, 1.0, 0.0).astype(jnp.bfloat16)
+            kt[group, :, at:at + half] = dot(turn, k, NT).astype(jnp.bfloat16)
 
 
 def start_copies(owners, h_of, q_hbm, do_hbm, own_hbm, par_hbm, mask_hbm, q_buf, do_buf, kv_buf, mask_buf, sems, others):
     per_owner = q_buf.shape[1]
     keys = [
-        pltpu.make_async_copy(own_hbm, kv_buf.at[0], others.at[0]),
-        pltpu.make_async_copy(par_hbm, kv_buf.at[1], others.at[1]),
+        pltpu.make_async_copy(own_hbm, kv_buf.at[pl.ds(0, own_hbm.shape[0])], others.at[0]),
+        pltpu.make_async_copy(par_hbm, kv_buf.at[pl.ds(own_hbm.shape[0], own_hbm.shape[0])], others.at[1]),
     ]
     mask = pltpu.make_async_copy(mask_hbm, mask_buf, others.at[2])
     for copy in keys:
@@ -78,7 +79,7 @@
     return keys, mask, copies
 
 
-def group_terms(group, i, h, q_buf, do_buf, lse_ref, delta_ref, mask_ref, kz, vz):
+def group_terms(group, i, h, q_buf, do_buf, lse_ref, delta_ref, mask_ref, kz, kv_buf):
     per_owner, count = q_buf.shape[1:3]
     rows = per_owner * count
     lo = group * LANES
@@ -87,20 +88,21 @@
     lse = jnp.concatenate([lse_ref[group, pl.ds(h + j, 1), :] for j in range(per_owner)], axis=1) * LOG2E
     delta = jnp.concatenate([delta_ref[group, pl.ds(h + j, 1), :] for j in range(per_owner)], axis=1)
     s = dot(kz[group], q, NT)
-    dp = dot(vz[group], do, NT)
+    vlo = 3 * LANES + lo
+    dp = dot(kv_buf[:, vlo:vlo + DV], do, NT)
     p = jnp.exp2(s * (SCALE * LOG2E) - lse) * jnp.concatenate([mask_ref[...]] * per_owner, axis=1)
     ds = (p * (dp - delta)).astype(jnp.bfloat16)
     return q, do, p.astype(jnp.bfloat16), ds
 
 
 def far_kernel(q_hbm, do_hbm, own_hbm, par_hbm, mask_hbm, lse_ref, delta_ref, right, left,
-               q_buf, do_buf, kv_buf, mask_ref, kz, vz, kt, held, sems, others):
+               q_buf, do_buf, kv_buf, mask_ref, kz, kt, held, sems, others):
     per_owner, _, count = right.shape
     me = lax.axis_index("ka")
     h_of = lambda i: per_owner * lax.rem(me + pick(i, FAR), KA)
     key_copies, mask_copy, copies = start_copies(
         len(FAR), h_of, q_hbm, do_hbm, own_hbm, par_hbm, mask_hbm, q_buf, do_buf, kv_buf, mask_ref, sems, others)
-    load_keys(key_copies, kv_buf, kz, vz, kt)
+    load_keys(key_copies, kv_buf, kz, kt)
     mask_copy.wait()
 
     def one(i, carry):
@@ -108,7 +110,7 @@
         for copy in copies(i, h):
             copy.wait()
         for group in range(GROUPS):
-            _, _, _, ds = group_terms(group, i, h, q_buf, do_buf, lse_ref, delta_ref, mask_ref, kz, vz)
+            _, _, _, ds = group_terms(group, i, h, q_buf, do_buf, lse_ref, delta_ref, mask_ref, kz, kv_buf)
             dqt = dot(kt[group], ds, NN) * SCALE
             for j in range(per_owner):
                 held[i, j, group * DK:(group + 1) * DK, :] = dqt[:, j * count:(j + 1) * count].astype(held.dtype)
@@ -123,7 +125,7 @@
 
 
 def near_kernel(q_hbm, do_hbm, own_hbm, par_hbm, mask_hbm, lse_ref, delta_ref, after, home, near, own_out, par_out,
-                q_buf, do_buf, kv_buf, mask_ref, kz, vz, kt, acc_k, acc_v, near_buf, sems, others):
+                q_buf, do_buf, kv_buf, mask_ref, kz, kt, acc_k, acc_v, near_buf, own_buf, par_buf, sems, others):
     del after
     per_owner, _, count = home.shape
     half = own_out.shape[0]
@@ -132,17 +134,17 @@
     h_of = lambda i: per_owner * lax.rem(me + pick(i, steps), KA)
     key_copies, mask_copy, copies = start_copies(
         KA, h_of, q_hbm, do_hbm, own_hbm, par_hbm, mask_hbm, q_buf, do_buf, kv_buf, mask_ref, sems, others)
-    load_keys(key_copies, kv_buf, kz, vz, kt)
-    mask_copy.wait()
     acc_k[...] = jnp.zeros_like(acc_k)
     acc_v[...] = jnp.zeros_like(acc_v)
+    load_keys(key_copies, kv_buf, kz, kt)
+    mask_copy.wait()
 
     def one(i, query_grads):
         h = h_of(i)
         for copy in copies(i, h):
             copy.wait()
         for group in range(GROUPS):
-            q, do, p, ds = group_terms(group, i, h, q_buf, do_buf, lse_ref, delta_ref, mask_ref, kz, vz)
+            q, do, p, ds = group_terms(group, i, h, q_buf, do_buf, lse_ref, delta_ref, mask_ref, kz, kv_buf)
             acc_v[group] += dot(p, do, NN)
             acc_k[group] += dot(ds, q, NN)
             if query_grads is not None:
@@ -171,16 +173,21 @@
         copy.start()
     lax.fori_loop(len(NEAR), KA, far_one, 0)
     low = lax.broadcasted_iota(jnp.int32, (half, LANES), 1) < DK - LANES
-    for side, out in enumerate((own_out, par_out)):
+    sums = []
+    for side, (out, held) in ((1, (par_out, par_buf)), (0, (own_out, own_buf))):
         at = side * half
         a = acc_k[0, at:at + half, :] * SCALE
         b = acc_k[1, at:at + half, :] * SCALE
-        out[:, :LANES] = a[:, :LANES].astype(out.dtype)
-        out[:, LANES:2 * LANES] = jnp.where(low, a[:, LANES:], b[:, :LANES]).astype(out.dtype)
-        out[:, 2 * LANES:3 * LANES] = b[:, LANES:].astype(out.dtype)
+        held[:, :LANES] = a[:, :LANES].astype(held.dtype)
+        held[:, LANES:2 * LANES] = jnp.where(low, a[:, LANES:], b[:, :LANES]).astype(held.dtype)
+        held[:, 2 * LANES:3 * LANES] = b[:, LANES:].astype(held.dtype)
         for group in range(GROUPS):
             vlo = (3 + group) * LANES
-            out[:, vlo:vlo + DV] = acc_v[group, at:at + half, :].astype(out.dtype)
+            held[:, vlo:vlo + DV] = acc_v[group, at:at + half, :].astype(held.dtype)
+        sums.append(pltpu.make_async_copy(held, out, others.at[2 + side]))
+        sums[-1].start()
+    for copy in sums:
+        copy.wait()
     for copy in results:
         copy.wait()
 
@@ -198,14 +205,13 @@
         scratch_shapes=[
             pltpu.VMEM((owners, per_owner, count, width), bf16),
             pltpu.VMEM((owners, per_owner, count, do.shape[2]), bf16),
-            pltpu.VMEM((2, *own.shape), bf16),
+            pltpu.VMEM((keys, own.shape[1]), bf16),
             pltpu.VMEM(mask.shape, mask.dtype),
             pltpu.VMEM((GROUPS, keys, WIN), bf16),
-            pltpu.VMEM((GROUPS, keys, DV), bf16),
             pltpu.VMEM((GROUPS, DK, keys), bf16),
             *scratch,
             pltpu.SemaphoreType.DMA((2, owners)),
-            pltpu.SemaphoreType.DMA((3,)),
+            pltpu.SemaphoreType.DMA((4,)),
         ],
         cost_estimate=pl.CostEstimate(
             flops=2 * GROUPS * owners * per_owner * count * keys * matmuls, bytes_accessed=6_000_000,
@@ -224,22 +230,56 @@
     )(*args)
 
 
-def copies_kernel(keys, values, out):
+def copies_kernel(keys, values, out, held, sems):
     width = keys.shape[1]
-    for i in range(out.shape[0]):
-        out[i, :, :width] = keys[...]
-        out[i, :, width:] = values[...]
-
-
-def message_kernel(near, from_left, from_right, up2, down2, up1, down1):
-    f32, bf16 = jnp.float32, jnp.bfloat16
+    parts = (
+        pltpu.make_async_copy(keys, held.at[:, pl.ds(0, width)], sems.at[0]),
+        pltpu.make_async_copy(values, held.at[:, pl.ds(width, values.shape[1])], sems.at[1]),
+    )
+    for copy in parts:
+        copy.start()
+    for copy in parts:
+        copy.wait()
+    sends = [pltpu.make_async_copy(held, out.at[i], sems.at[2 + i]) for i in range(out.shape[0])]
+    for copy in sends:
+        copy.start()
+    for copy in sends:
+        copy.wait()
+
+
+def sum_kernel(own, other, out):
+    out[...] = (own[...] + other[...].astype(jnp.float32)).astype(out.dtype)
+
+
+def message_kernel(near, from_left, from_right, up2, down2, up1, down1, near_buf, left_buf, right_buf, held, sems):
+    f32 = jnp.float32
     width = up1.shape[1]
-    up1[...] = (near[0] + from_left[:, :width, :].astype(f32)).astype(bf16)
-    down1[...] = (near[1] + from_right[:, :width, :].astype(f32)).astype(bf16)
-    up2[:, :DK, :] = (near[2, :, :DK, :] + from_left[:, width:, :].astype(f32)).astype(bf16)
-    up2[:, DK:, :] = near[2, :, DK:, :].astype(bf16)
-    down2[:, :DK, :] = near[3, :, :DK, :].astype(bf16)
-    down2[:, DK:, :] = (near[3, :, DK:, :] + from_right[:, width:, :].astype(f32)).astype(bf16)
+    arrivals = (
+        pltpu.make_async_copy(from_left, left_buf, sems.at[0]),
+        pltpu.make_async_copy(from_right, right_buf, sems.at[1]),
+    )
+    terms = [pltpu.make_async_copy(near.at[i], near_buf.at[i], sems.at[2 + i]) for i in range(4)]
+    sends = [pltpu.make_async_copy(held.at[i], out, sems.at[6 + i]) for i, out in enumerate((up1, down1, up2, down2))]
+    for copy in (arrivals[0], terms[2], arrivals[1], terms[3], terms[0], terms[1]):
+        copy.start()
+    for i in (2, 3, 0, 1):
+        terms[i].wait()
+        if i >= 2:
+            arrivals[i - 2].wait()
+        total = near_buf.at[i]
+        if i == 0:
+            held[i] = (total[...] + left_buf[:, :width, :].astype(f32)).astype(held.dtype)
+        elif i == 1:
+            held[i] = (total[...] + right_buf[:, :width, :].astype(f32)).astype(held.dtype)
+        elif i == 2:
+            held[i, :, :DK, :] = (total[:, :DK, :] + left_buf[:, width:, :].astype(f32)).astype(held.dtype)
+            held[i, :, DK:, :] = total[:, DK:, :].astype(held.dtype)
+        else:
+            held[i, :, :DK, :] = total[:, :DK, :].astype(held.dtype)
+            held[i, :, DK:, :] = (total[:, DK:, :] + right_buf[:, width:, :].astype(f32)).astype(held.dtype)
+        sends[i].start()
+    for copy in sends:
+        copy.wait()
 
 
 def finish_kernel(home, a, b, c, d, pieces, dq, dk, dv):
@@ -274,7 +314,15 @@
     def along(x, step):
         return lax.ppermute(x, "ka", [(i, (i + step) % ka) for i in range(ka)])
 
-    (copies,) = small(copies_kernel, (shape((chips, rows, both), bf16),), comp_keys, comp_values)
+    copies = pl.pallas_call(
+        copies_kernel,
+        out_shape=shape((chips, rows, both), bf16),
+        in_specs=[HBM, HBM],
+        out_specs=HBM,
+        scratch_shapes=[pltpu.VMEM((rows, both), bf16), pltpu.SemaphoreType.DMA((2 + chips,))],
+        compiler_params=pltpu.CompilerParams(vmem_limit_bytes=GRANT),
+        name="copies",
+    )(comp_keys, comp_values)
     own = lax.all_to_all(copies, "pb", 0, 0, axis_index_groups=same_core, tiled=True).reshape(half, both)
     delta = jnp.stack([
         jnp.sum(
@@ -300,22 +348,50 @@
     home, near, own_kv, par_kv = grads(
         near_kernel, KA, 3 * DK + 2 * DV,
         (shape(chunk, f32), shape((len(NEAR) - 1, *chunk), f32), shape((half, both), f32), shape((half, both), bf16)),
-        (HBM, HBM, VMEM, VMEM),
+        (HBM, HBM, HBM, HBM),
         [
             pltpu.VMEM((GROUPS, keys, WIN), f32),
             pltpu.VMEM((GROUPS, keys, DV), f32),
             pltpu.VMEM((len(NEAR), *chunk), f32),
+            pltpu.VMEM((half, both), f32),
+            pltpu.VMEM((half, both), bf16),
         ],
         *args, right,
     )
     from_other = lax.ppermute(par_kv, "pb", other_core)
 
-    messages = small(message_kernel, (shape(chunk, bf16),) * 4, near, from_left, from_right)
-    arrived = [along(x, step) for x, step in zip(messages, (2, -2, 1, -1))]
-    chip_sum = (own_kv + from_other.astype(f32)).astype(bf16)
-    pieces = lax.all_to_all(
-        chip_sum.reshape(chips, rows, both), "pb", 0, 0, axis_index_groups=same_core, tiled=True
-    )
+    up2, down2, up1, down1 = pl.pallas_call(
+        message_kernel,
+        out_shape=(shape(chunk, bf16),) * 4,
+        in_specs=[HBM] * 3,
+        out_specs=(HBM,) * 4,
+        scratch_shapes=[
+            pltpu.VMEM(near.shape, f32),
+            pltpu.VMEM(hops.shape, bf16),
+            pltpu.VMEM(hops.shape, bf16),
+            pltpu.VMEM((4, *chunk), bf16),
+            pltpu.SemaphoreType.DMA((10,)),
+        ],
+        compiler_params=pltpu.CompilerParams(vmem_limit_bytes=GRANT),
+        name="messages",
+    )(near, from_left, from_right)
+    from_up2 = along(up2, 2)
+    from_down2 = along(down2, -2)
+    from_up1 = along(up1, 1)
+    from_down1 = along(down1, -1)
+    blocks = 4
+    block = pl.BlockSpec((half // blocks, both), lambda i: (i, 0))
+    chip_sum = pl.pallas_call(
+        sum_kernel,
+        out_shape=shape((half, both), bf16),
+        grid=(blocks,),
+        in_specs=[block, block],
+        out_specs=block,
+        compiler_params=pltpu.CompilerParams(vmem_limit_bytes=GRANT),
+        name="chip_sum",
+    )(own_kv, from_other)
+    pieces = lax.all_to_all(chip_sum.reshape(chips, rows, both), "pb", 0, 0, axis_index_groups=same_core, tiled=True)
+    arrived = (from_up2, from_down2, from_up1, from_down1)
     return small(
         finish_kernel,
         (shape((per_owner, count, width), f32), shape((rows, width), f32), shape((rows, both - width), f32)),

time: 95.5 us -> 101 us (1.058)
  Pallas kernels: 24.8 us -> 32.4 us
  local copies, waits for them, and re-layouts: 3.49 us -> 2.22 us
  other arithmetic: 3.68 us -> 2.43 us
    pallas_call x0 -> x3, Pallas kernels: none -> 7.51 us  [the longest x1 3.44 us: per_device(): pl.pallas_call(sum_kernel, out_shape=shape((half, both), bf16), grid=(blo...]
    convert_element_type x1 -> x0, other arithmetic: 2.45 us -> none  [per_device(): chip_sum = (own_kv + from_other.astype(f32)).astype(bf16)]
    reduce_sum x1, other arithmetic: 0.61 us -> 1.82 us  [per_device(): jnp.sum(grad_out[:, :, g * DV:(g + 1) * DV].astype(f32) * outputs[:, :, g...]
    pallas_call x3 -> x1, Pallas kernels: 1.96 us -> 2.03 us  [small(): pl.pallas_call(kernel, out_shape=outs, in_specs=[VMEM] * len(args), out_s...]
  transfers between devices with their start and end apart: 10 -> 10, of which waited for: 8 -> 8; matrix products, arithmetic and copies ran while one was open for 3% -> 4% of each run, Pallas kernels for 0% -> 2%
where the time goes in v5:
time: 101 us
  waiting for transfers between devices  36.9 us (37%)
  Pallas kernels  32.4 us (32%)
  starting transfers between devices  26.1 us (26%)
  other arithmetic  2.43 us (2%)
  local copies, waits for them, and re-layouts  2.22 us (2%)
    ppermute x6, waiting for transfers between devices, along(): return lax.ppermute(x, 'ka', [(i, (i + step) % ka) for i in range(ka)])  24.8 us
    pallas_call x2, Pallas kernels, grads(): pl.pallas_call(kernel, out_shape=outs, in_specs=[HBM] * 5 + [VMEM] * 2 +...  22.8 us
    ppermute x6, starting transfers between devices, along(): return lax.ppermute(x, 'ka', [(i, (i + step) % ka) for i in range(ka)])  12.5 us
    all_to_all x1, waiting for transfers between devices, per_device(): lax.all_to_all(copies, 'pb', 0, 0, axis_index_groups=same_core, tiled=True)  9.21 us
    all_to_all x1, starting transfers between devices, per_device(): lax.all_to_all(copies, 'pb', 0, 0, axis_index_groups=same_core, tiled=True)  7.61 us
    all_to_all x1, starting transfers between devices, per_device(): lax.all_to_all(chip_sum.reshape(chips, rows, both), 'pb', 0, 0, axis_inde...  4.2 us
    pallas_call x1, Pallas kernels, per_device(): pl.pallas_call(sum_kernel, out_shape=shape((half, both), bf16), grid=(blo...  3.44 us
    pallas_call x1, Pallas kernels, per_device(): pl.pallas_call(message_kernel, out_shape=(shape(chunk, bf16),) * 4, in_sp...  2.33 us
  transfers between devices with their start and end apart: 10, of which 8 were waited for; matrix products, arithmetic and copies ran while one was open for 4% of the time, Pallas kernels for 2%

profile of v5, /device:TPU:1, one launch (start us, length us, event | category | flops | bytes accessed | tf_op | source)
XLA Modules:
  0.0 100.7 jit_solution(17744024751191042779)
XLA Ops:
  0.6 1.7 %copies.1 = bf16[8,64,640]{2,1,0:T(8,128)(2,1)} custom-call(bf16[64,384]{1,0:T(8,128)(2,1)} %keys.1, bf16[64,256]{1,0:T(8,128)(2,1)} %values.1), custom_call_target="tpu_custom_call" | custom-call | tf_op jit(solution)/shard_map/copies/pallas_call | solution.py:317
  2.4 0.0 copy-start.1
  2.4 7.6 %all-to-all-start = ((bf16[8,64,640]{2,1,0:T(8,128)(2,1)}), bf16[8,64,640]{2,1,0:T(8,128)(2,1)S(1)}, u32[]{:S(2)}, u32[]{:S(2)}) async-start(bf16[8,64,640]{2,1,0:T(8,128)(2,1)} %copies.1), calls=%async_computation | async-start | bytes 1310720 | tf_op jit(solution)/shard_map/all_to_all | solution.py:326
  10.0 0.1 reshape.21
  10.1 0.1 convert_element_type.27
  10.2 1.8 %multiply_reduce_fusion.1 = (f32[16,128]{1,0:T(8,128)S(1)}, f32[16,128]{1,0:T(8,128)S(1)}) fusion(bf16[16,128,256]{2,1,0:T(8,128)(2,1)S(1)} %copy-done.1, bf16[16,128,256]{2,1,0:T(8,128)(2,1)} %do_hbm.3), kind=kLoop, calls=%fused_computation.1 | loop fusion | flops 2093056 | bytes 2113536 | tf_op jit(solution)/shard_map/reduce_sum | solution.py:328
  12.0 0.6 pad_maximum_fusion.delta_ref
  12.6 9.2 %all-to-all-done = bf16[8,64,640]{2,1,0:T(8,128)(2,1)S(1)} async-done(((bf16[8,64,640]{2,1,0:T(8,128)(2,1)}), bf16[8,64,640]{2,1,0:T(8,128)(2,1)S(1)}, u32[]{:S(2)}, u32[]{:S(2)}) %all-to-all-start) | async-done | bytes 655392 | tf_op jit(solution)/shard_map/all_to_all | solution.py:326
  21.9 1.3 %collective-permute-start = (bf16[512,640]{1,0:T(8,128)(2,1)S(1)}, bf16[512,640]{1,0:T(8,128)(2,1)}, u32[]{:S(2)}, u32[]{:S(2)}) collective-permute-start(bf16[512,640]{1,0:T(8,128)(2,1)S(1)} %bitcast.13), channel_id=1, source_target_pairs={{0,16},{16,0},{32,48},{48,32},{64,80},{80,64},{96,112},{112,96},{1... | collective-permute-start | bytes 1966088 | tf_op jit(solution)/shard_map/ppermute | solution.py:338
  23.2 1.0 copy.13.mask_hbm
  24.2 0.9 collective-permute-done.par_hbm
  25.1 6.7 %shard_map.94 = (bf16[2,576,128]{2,1,0:T(8,128)(2,1)}, bf16[2,576,128]{2,1,0:T(8,128)(2,1)}) custom-call(bf16[16,128,384]{2,1,0:T(8,128)(2,1)} %q_hbm.3, bf16[16,128,256]{2,1,0:T(8,128)(2,1)} %do_hbm.3, bf16[512,640]{1,0:T(8,128)(2,1)} %bitcast.14, bf16[512,640]{1,0:T(8,128)(2,1)} %collective-permute-done.par_hbm, f32[1024,128]{1,0:T(8,128)} %copy.13.mask_hbm, ...), custom_call_target="tpu_custom_call" | custom-call | flops 1610612736 | bytes 6000000 | tf_op jit(solution)/shard_map/pallas_call | solution.py:200
  31.8 16.1 %shard_map.95 = (f32[2,384,128]{2,1,0:T(8,128)}, f32[4,2,384,128]{3,2,1,0:T(8,128)}, f32[512,640]{1,0:T(8,128)}, bf16[512,640]{1,0:T(8,128)(2,1)}) custom-call(bf16[16,128,384]{2,1,0:T(8,128)(2,1)} %q_hbm.3, bf16[16,128,256]{2,1,0:T(8,128)(2,1)} %do_hbm.3, bf16[512,640]{1,0:T(8,128)(2,1)} %bitcast.15, bf16[512,640]{1,0:T(8,128)(2,1)} %collective-permute-done.par_hbm, ...), custom_call_target="tpu_custom_call" | custom-call | flops 6979321856 | bytes 6000000 | tf_op jit(solution)/shard_map/pallas_call | solution.py:200
  47.9 0.5 collective-permute-start.7
  48.4 2.1 %collective-permute-done.7.other = bf16[512,640]{1,0:T(8,128)(2,1)} collective-permute-done((bf16[512,640]{1,0:T(8,128)(2,1)}, bf16[512,640]{1,0:T(8,128)(2,1)}, u32[]{:S(2)}, u32[]{:S(2)}) %collective-permute-start.7) | collective-permute-done | bytes 655392 | tf_op jit(solution)/shard_map/ppermute | solution.py:361
  50.4 3.4 %chip_sum.1 = bf16[512,640]{1,0:T(8,128)(2,1)} custom-call(f32[512,640]{1,0:T(8,128)} %get-tuple-element.27.own, bf16[512,640]{1,0:T(8,128)(2,1)} %collective-permute-done.7.other), custom_call_target="tpu_custom_call" | custom-call | tf_op jit(solution)/shard_map/chip_sum/pallas_call | solution.py:384
  53.9 4.2 %all-to-all-start.1 = ((bf16[8,64,640]{2,1,0:T(8,128)(2,1)}), bf16[8,64,640]{2,1,0:T(8,128)(2,1)}, u32[]{:S(2)}, u32[]{:S(2)}) async-start(bf16[8,64,640]{2,1,0:T(8,128)(2,1)} %bitcast.11), calls=%async_computation.1 | async-start | bytes 1310720 | tf_op jit(solution)/shard_map/all_to_all | solution.py:393
  58.1 3.1 %collective-permute-start.1 = (bf16[2,576,128]{2,1,0:T(8,128)(2,1)}, bf16[2,576,128]{2,1,0:T(8,128)(2,1)}, u32[]{:S(2)}, u32[]{:S(2)}) collective-permute-start(bf16[2,576,128]{2,1,0:T(8,128)(2,1)} %get-tuple-element.19.after), channel_id=1, source_target_pairs={{0,4},{2,6},{4,8},{6,10},{8,12},{10,14},{12,0},{14,2},{1,5},{3,7},... | collective-permute-start | bytes 884744 | tf_op jit(solution)/shard_map/ppermute | solution.py:315
  61.2 3.1 %collective-permute-start.2 = (bf16[2,576,128]{2,1,0:T(8,128)(2,1)}, bf16[2,576,128]{2,1,0:T(8,128)(2,1)}, u32[]{:S(2)}, u32[]{:S(2)}) collective-permute-start(bf16[2,576,128]{2,1,0:T(8,128)(2,1)} %get-tuple-element.22), channel_id=1, source_target_pairs={{0,12},{2,14},{4,0},{6,2},{8,4},{10,6},{12,8},{14,10},{1,13},{3,15... | collective-permute-start | bytes 884744 | tf_op jit(solution)/shard_map/ppermute | solution.py:315
  64.3 9.3 %collective-permute-done.1.from_left = bf16[2,576,128]{2,1,0:T(8,128)(2,1)} collective-permute-done((bf16[2,576,128]{2,1,0:T(8,128)(2,1)}, bf16[2,576,128]{2,1,0:T(8,128)(2,1)}, u32[]{:S(2)}, u32[]{:S(2)}) %collective-permute-start.1) | collective-permute-done | bytes 294944 | tf_op jit(solution)/shard_map/ppermute | solution.py:315
  73.5 5.5 %collective-permute-done.2.from_right = bf16[2,576,128]{2,1,0:T(8,128)(2,1)} collective-permute-done((bf16[2,576,128]{2,1,0:T(8,128)(2,1)}, bf16[2,576,128]{2,1,0:T(8,128)(2,1)}, u32[]{:S(2)}, u32[]{:S(2)}) %collective-permute-start.2) | collective-permute-done | bytes 294944 | tf_op jit(solution)/shard_map/ppermute | solution.py:315
  79.0 2.3 %messages.1 = (bf16[2,384,128]{2,1,0:T(8,128)(2,1)}, bf16[2,384,128]{2,1,0:T(8,128)(2,1)}, bf16[2,384,128]{2,1,0:T(8,128)(2,1)}, bf16[2,384,128]{2,1,0:T(8,128)(2,1)}) custom-call(f32[4,2,384,128]{3,2,1,0:T(8,128)} %get-tuple-element.21.near, bf16[2,576,128]{2,1,0:T(8,128)(2,1)} %collective-permute-done.1.from_left, ...), custom_call_target="tpu_custom_call" | custom-call | tf_op jit(solution)/shard_map/messages/pallas_call | solution.py:363
  81.3 3.6 %collective-permute-start.3 = (bf16[2,384,128]{2,1,0:T(8,128)(2,1)}, bf16[2,384,128]{2,1,0:T(8,128)(2,1)S(1)}, u32[]{:S(2)}, u32[]{:S(2)}) collective-permute-start(bf16[2,384,128]{2,1,0:T(8,128)(2,1)} %get-tuple-element.23), channel_id=1, source_target_pairs={{0,4},{2,6},{4,8},{6,10},{8,12},{10,14},{12,0},{14,2},{1,5},{3,7},... | collective-permute-start | bytes 589832 | tf_op jit(solution)/shard_map/ppermute | solution.py:315
  84.9 0.1 collective-permute-start.4
  85.0 2.7 %collective-permute-start.6 = (bf16[2,384,128]{2,1,0:T(8,128)(2,1)}, bf16[2,384,128]{2,1,0:T(8,128)(2,1)S(1)}, u32[]{:S(2)}, u32[]{:S(2)}) collective-permute-start(bf16[2,384,128]{2,1,0:T(8,128)(2,1)} %get-tuple-element.26), channel_id=1, source_target_pairs={{0,14},{2,0},{4,2},{6,4},{8,6},{10,8},{12,10},{14,12},{1,15},{3,1}... | collective-permute-start | bytes 589832 | tf_op jit(solution)/shard_map/ppermute | solution.py:315
  87.7 5.8 %collective-permute-done.3.a = bf16[2,384,128]{2,1,0:T(8,128)(2,1)S(1)} collective-permute-done((bf16[2,384,128]{2,1,0:T(8,128)(2,1)}, bf16[2,384,128]{2,1,0:T(8,128)(2,1)S(1)}, u32[]{:S(2)}, u32[]{:S(2)}) %collective-permute-start.3) | collective-permute-done | bytes 196640 | tf_op jit(solution)/shard_map/ppermute | solution.py:315
  93.4 0.0 collective-permute-done.4.b
  93.4 3.9 %collective-permute-done.5.c = bf16[2,384,128]{2,1,0:T(8,128)(2,1)S(1)} collective-permute-done((bf16[2,384,128]{2,1,0:T(8,128)(2,1)}, bf16[2,384,128]{2,1,0:T(8,128)(2,1)S(1)}, u32[]{:S(2)}, u32[]{:S(2)}) %collective-permute-start.5) | collective-permute-done | bytes 196640 | tf_op jit(solution)/shard_map/ppermute | solution.py:315
  97.3 0.4 collective-permute-done.6.d
  97.7 0.0 all-to-all-done.1.pieces
  97.7 1.0 copy-done
  98.7 2.0 %shard_map.96 = (f32[2,128,384]{2,1,0:T(8,128)}, f32[64,384]{1,0:T(8,128)}, f32[64,256]{1,0:T(8,128)}) custom-call(f32[2,384,128]{2,1,0:T(8,128)S(1)} %copy-done, bf16[2,384,128]{2,1,0:T(8,128)(2,1)S(1)} %collective-permute-done.3.a, bf16[2,384,128]{2,1,0:T(8,128)(2,1)S(1)} %collective-permute-done.4.b, bf16[2,384,128]{2,1,0:T(8,128)(2,1)S(1)} %collective-permute-done.5.c, ...), custom_call_target="tpu_custom_call" | custom-call | tf_op jit(solution)/shard_map/pallas_call | solution.py:224
  (10 shorter events, 0.1 us)
Async XLA Ops:
  0.6 9.4 %copy-start.3 = (s32[2,1024]{1,0:T(2,128)S(1)}, s32[2,1024]{1,0:T(2,128)}, u32[]{:S(2)}) copy-start(s32[2,1024]{1,0:T(2,128)} %param.13) | copy-start | bytes 24580
  2.4 7.8 %copy-start.1 = (bf16[16,128,256]{2,1,0:T(8,128)(2,1)S(1)}, bf16[16,128,256]{2,1,0:T(8,128)(2,1)}, u32[]{:S(2)}) copy-start(bf16[16,128,256]{2,1,0:T(8,128)(2,1)} %param.10) | copy-start | bytes 3145732
  2.4 19.4 %all-to-all-start = ((bf16[8,64,640]{2,1,0:T(8,128)(2,1)}), bf16[8,64,640]{2,1,0:T(8,128)(2,1)S(1)}, u32[]{:S(2)}, u32[]{:S(2)}) async-start(bf16[8,64,640]{2,1,0:T(8,128)(2,1)} %copies.1), calls=%async_computation | async-start | bytes 1310720 | tf_op jit(solution)/shard_map/all_to_all | solution.py:326
  21.8 2.4 %copy-start.2 = (bf16[8,64,640]{2,1,0:T(8,128)(2,1)}, bf16[8,64,640]{2,1,0:T(8,128)(2,1)S(1)}, u32[]{:S(2)}) copy-start(bf16[8,64,640]{2,1,0:T(8,128)(2,1)S(1)} %all-to-all-done) | copy-start | bytes 1966084
  21.9 3.2 %collective-permute-start = (bf16[512,640]{1,0:T(8,128)(2,1)S(1)}, bf16[512,640]{1,0:T(8,128)(2,1)}, u32[]{:S(2)}, u32[]{:S(2)}) collective-permute-start(bf16[512,640]{1,0:T(8,128)(2,1)S(1)} %bitcast.13), channel_id=1, source_target_pairs={{0,16},{16,0},{32,48},{48,32},{64,80},{80,64},{96,112},{112,96},{1... | collective-permute-start | bytes 1966088 | tf_op jit(solution)/shard_map/ppermute | solution.py:338
  47.9 2.5 %collective-permute-start.7 = (bf16[512,640]{1,0:T(8,128)(2,1)}, bf16[512,640]{1,0:T(8,128)(2,1)}, u32[]{:S(2)}, u32[]{:S(2)}) collective-permute-start(bf16[512,640]{1,0:T(8,128)(2,1)} %get-tuple-element.28), channel_id=1, source_target_pairs={{0,16},{16,0},{32,48},{48,32},{64,80},{80,64},{96,112},{112,96},{1... | collective-permute-start | bytes 1966088 | tf_op jit(solution)/shard_map/ppermute | solution.py:361
  53.9 43.8 %all-to-all-start.1 = ((bf16[8,64,640]{2,1,0:T(8,128)(2,1)}), bf16[8,64,640]{2,1,0:T(8,128)(2,1)}, u32[]{:S(2)}, u32[]{:S(2)}) async-start(bf16[8,64,640]{2,1,0:T(8,128)(2,1)} %bitcast.11), calls=%async_computation.1 | async-start | bytes 1310720 | tf_op jit(solution)/shard_map/all_to_all | solution.py:393
  58.1 15.4 %collective-permute-start.1 = (bf16[2,576,128]{2,1,0:T(8,128)(2,1)}, bf16[2,576,128]{2,1,0:T(8,128)(2,1)}, u32[]{:S(2)}, u32[]{:S(2)}) collective-permute-start(bf16[2,576,128]{2,1,0:T(8,128)(2,1)} %get-tuple-element.19.after), channel_id=1, source_target_pairs={{0,4},{2,6},{4,8},{6,10},{8,12},{10,14},{12,0},{14,2},{1,5},{3,7},... | collective-permute-start | bytes 884744 | tf_op jit(solution)/shard_map/ppermute | solution.py:315
  61.2 17.8 %collective-permute-start.2 = (bf16[2,576,128]{2,1,0:T(8,128)(2,1)}, bf16[2,576,128]{2,1,0:T(8,128)(2,1)}, u32[]{:S(2)}, u32[]{:S(2)}) collective-permute-start(bf16[2,576,128]{2,1,0:T(8,128)(2,1)} %get-tuple-element.22), channel_id=1, source_target_pairs={{0,12},{2,14},{4,0},{6,2},{8,4},{10,6},{12,8},{14,10},{1,13},{3,15... | collective-permute-start | bytes 884744 | tf_op jit(solution)/shard_map/ppermute | solution.py:315
  81.3 12.1 %collective-permute-start.3 = (bf16[2,384,128]{2,1,0:T(8,128)(2,1)}, bf16[2,384,128]{2,1,0:T(8,128)(2,1)S(1)}, u32[]{:S(2)}, u32[]{:S(2)}) collective-permute-start(bf16[2,384,128]{2,1,0:T(8,128)(2,1)} %get-tuple-element.23), channel_id=1, source_target_pairs={{0,4},{2,6},{4,8},{6,10},{8,12},{10,14},{12,0},{14,2},{1,5},{3,7},... | collective-permute-start | bytes 589832 | tf_op jit(solution)/shard_map/ppermute | solution.py:315
  84.9 8.6 %collective-permute-start.4 = (bf16[2,384,128]{2,1,0:T(8,128)(2,1)}, bf16[2,384,128]{2,1,0:T(8,128)(2,1)S(1)}, u32[]{:S(2)}, u32[]{:S(2)}) collective-permute-start(bf16[2,384,128]{2,1,0:T(8,128)(2,1)} %get-tuple-element.24), channel_id=1, source_target_pairs={{0,12},{2,14},{4,0},{6,2},{8,4},{10,6},{12,8},{14,10},{1,13},{3,15... | collective-permute-start | bytes 589832 | tf_op jit(solution)/shard_map/ppermute | solution.py:315
  85.0 12.3 %collective-permute-start.5 = (bf16[2,384,128]{2,1,0:T(8,128)(2,1)}, bf16[2,384,128]{2,1,0:T(8,128)(2,1)S(1)}, u32[]{:S(2)}, u32[]{:S(2)}) collective-permute-start(bf16[2,384,128]{2,1,0:T(8,128)(2,1)} %get-tuple-element.25), channel_id=1, source_target_pairs={{0,2},{2,4},{4,6},{6,8},{8,10},{10,12},{12,14},{14,0},{1,3},{3,5},... | collective-permute-start | bytes 589832 | tf_op jit(solution)/shard_map/ppermute | solution.py:315
  85.0 12.7 %collective-permute-start.6 = (bf16[2,384,128]{2,1,0:T(8,128)(2,1)}, bf16[2,384,128]{2,1,0:T(8,128)(2,1)S(1)}, u32[]{:S(2)}, u32[]{:S(2)}) collective-permute-start(bf16[2,384,128]{2,1,0:T(8,128)(2,1)} %get-tuple-element.26), channel_id=1, source_target_pairs={{0,14},{2,0},{4,2},{6,4},{8,6},{10,8},{12,10},{14,12},{1,15},{3,1}... | collective-permute-start | bytes 589832 | tf_op jit(solution)/shard_map/ppermute | solution.py:315
  97.7 1.0 copy-start

commit v6 on v4

v6 whole, which is shorter than its diff:
```python
import math

import jax
import jax.numpy as jnp
from jax import lax
from jax.experimental import pallas as pl
from jax.experimental.pallas import tpu as pltpu
from jax.sharding import PartitionSpec as P


DK = 192
DV = 128
QBLK = 64
LANES = 128
GROUPS = 2
WIN = 256
SCALE = 1.0 / math.sqrt(DK)
LOG2E = math.log2(math.e)
FAR = (3, 5, 4)
NEAR = (0, 1, 7, 2, 6)
KA = 8
GRANT = 20 * 1024 * 1024
NT = (((1,), (1,)), ((), ()))
NN = (((1,), (0,)), ((), ()))
VMEM = pl.BlockSpec(memory_space=pltpu.VMEM)
HBM = pl.BlockSpec(memory_space=pltpu.HBM)


def dot(a, b, dims):
    return lax.dot_general(a, b, dims, preferred_element_type=jnp.float32)


def pick(i, values):
    result = jnp.int32(values[0])
    for n, value in enumerate(values[1:], 1):
        result = jnp.where(i == n, jnp.int32(value), result)
    return result


def load_keys(own_ref, par_ref, kz, vz, kt):
    half = own_ref.shape[0]
    lane = lax.broadcasted_iota(jnp.int32, (half, WIN), 1)
    one = lax.broadcasted_iota(jnp.int32, (DK, WIN), 0)
    column = lax.broadcasted_iota(jnp.int32, (DK, WIN), 1)
    for side, ref in enumerate((own_ref, par_ref)):
        at = side * half
        for group in range(GROUPS):
            first = 0 if group == 0 else WIN - DK
            keep = (lane >= first) & (lane < first + DK)
            lo = group * LANES
            vlo = 3 * LANES + lo
            k = jnp.where(keep, ref[:, lo:lo + WIN], jnp.zeros((), jnp.bfloat16))
            kz[group, at:at + half, :] = k
            vz[group, at:at + half, :] = ref[:, vlo:vlo + DV]
            turn = jnp.where(column == one + first, 1.0, 0.0).astype(jnp.bfloat16)
            kt[group, :, at:at + half] = dot(turn, k, NT).astype(jnp.bfloat16)


def group_terms(group, h, per_owner, q_ref, do_ref, mask_ref, lse_ref, delta_ref, kz, vz):
    rows = per_owner * q_ref.shape[1]
    lo = group * LANES
    q = q_ref[pl.ds(h, per_owner), :, lo:lo + WIN].reshape(rows, WIN)
    do = do_ref[pl.ds(h, per_owner), :, lo:lo + DV].reshape(rows, DV)
    lse = jnp.concatenate([lse_ref[group, pl.ds(h + j, 1), :] for j in range(per_owner)], axis=1) * LOG2E
    delta = jnp.concatenate([delta_ref[group, pl.ds(h + j, 1), :] for j in range(per_owner)], axis=1)
    s = dot(kz[group], q, NT)
    dp = dot(vz[group], do, NT)
    p = jnp.exp2(s * (SCALE * LOG2E) - lse) * jnp.concatenate([mask_ref[...]] * per_owner, axis=1)
    ds = (p * (dp - delta)).astype(jnp.bfloat16)
    return q, do, p.astype(jnp.bfloat16), ds


def far_kernel(q_ref, do_ref, mask_ref, lse_ref, delta_ref, own_ref, par_ref, right, left, kz, vz, kt, held):
    per_owner, _, count = right.shape
    me = lax.axis_index("ka")
    load_keys(own_ref, par_ref, kz, vz, kt)

    def one(i, carry):
        h = per_owner * lax.rem(me + pick(i, FAR), KA)
        for group in range(GROUPS):
            ds = group_terms(group, h, per_owner, q_ref, do_ref, mask_ref, lse_ref, delta_ref, kz, vz)[3]
            dqt = dot(kt[group], ds, NN) * SCALE
            for j in range(per_owner):
                held[i, j, group * DK:(group + 1) * DK, :] = dqt[:, j * count:(j + 1) * count].astype(held.dtype)
        return carry

    lax.fori_loop(0, len(FAR), one, 0)
    width = GROUPS * DK
    right[:, :width, :] = held[0]
    left[:, :width, :] = held[1]
    right[:, width:, :] = held[2, :, :DK, :]
    left[:, width:, :] = held[2, :, DK:, :]


def near_kernel(q_ref, do_ref, mask_ref, lse_ref, delta_ref, kz, vz, kt, near, own_out, par_out, acc_k, acc_v):
    _, per_owner, _, count = near.shape
    half = own_out.shape[0]
    me = lax.axis_index("ka")
    steps = NEAR + FAR
    acc_k[...] = jnp.zeros_like(acc_k)
    acc_v[...] = jnp.zeros_like(acc_v)

    def one(i, query_grads):
        h = per_owner * lax.rem(me + pick(i, steps), KA)
        for group in range(GROUPS):
            q, do, p, ds = group_terms(group, h, per_owner, q_ref, do_ref, mask_ref, lse_ref, delta_ref, kz, vz)
            acc_v[group] += dot(p, do, NN)
            acc_k[group] += dot(ds, q, NN)
            if query_grads:
                dqt = dot(kt[group], ds, NN) * SCALE
                for j in range(per_owner):
                    near[i, j, group * DK:(group + 1) * DK, :] = dqt[:, j * count:(j + 1) * count]

    def near_one(i, carry):
        one(i, True)
        return carry

    def far_one(i, carry):
        one(i, False)
        return carry

    lax.fori_loop(0, len(NEAR), near_one, 0)
    lax.fori_loop(len(NEAR), KA, far_one, 0)
    low = lax.broadcasted_iota(jnp.int32, (half, LANES), 1) < DK - LANES
    for side, out in enumerate((own_out, par_out)):
        at = side * half
        a = acc_k[0, at:at + half, :] * SCALE
        b = acc_k[1, at:at + half, :] * SCALE
        out[:, :LANES] = a[:, :LANES].astype(out.dtype)
        out[:, LANES:2 * LANES] = jnp.where(low, a[:, LANES:], b[:, :LANES]).astype(out.dtype)
        out[:, 2 * LANES:3 * LANES] = b[:, LANES:].astype(out.dtype)
        for group in range(GROUPS):
            vlo = (3 + group) * LANES
            out[:, vlo:vlo + DV] = acc_v[group, at:at + half, :].astype(out.dtype)


def grads(kernel, owners, matmuls, outs, scratch, *args):
    heads, count, _ = args[0].shape
    keys = args[2].shape[0]
    terms = GROUPS * owners * (heads // KA) * count * keys
    return pl.pallas_call(
        kernel,
        out_shape=outs,
        in_specs=[VMEM] * len(args),
        out_specs=tuple(VMEM for _ in outs),
        scratch_shapes=scratch,
        cost_estimate=pl.CostEstimate(flops=2 * terms * matmuls, bytes_accessed=6_000_000, transcendentals=terms),
        compiler_params=pltpu.CompilerParams(vmem_limit_bytes=GRANT),
    )(*args)


def small(kernel, outs, *args):
    return pl.pallas_call(
        kernel,
        out_shape=outs,
        in_specs=[VMEM] * len(args),
        out_specs=tuple(VMEM for _ in outs),
        compiler_params=pltpu.CompilerParams(vmem_limit_bytes=GRANT),
    )(*args)


def copies_kernel(keys, values, out, held, sems):
    width = keys.shape[1]
    parts = (
        pltpu.make_async_copy(keys, held.at[:, pl.ds(0, width)], sems.at[0]),
        pltpu.make_async_copy(values, held.at[:, pl.ds(width, values.shape[1])], sems.at[1]),
    )
    for copy in parts:
        copy.start()
    for copy in parts:
        copy.wait()
    sends = [pltpu.make_async_copy(held, out.at[i], sems.at[2 + i]) for i in range(out.shape[0])]
    for copy in sends:
        copy.start()
    for copy in sends:
        copy.wait()


def message_kernel(near, from_left, from_right, up2, down2, up1, down1):
    f32, bf16 = jnp.float32, jnp.bfloat16
    width = up1.shape[1]
    up1[...] = (near[1] + from_left[:, :width, :].astype(f32)).astype(bf16)
    down1[...] = (near[2] + from_right[:, :width, :].astype(f32)).astype(bf16)
    up2[:, :DK, :] = (near[3, :, :DK, :] + from_left[:, width:, :].astype(f32)).astype(bf16)
    up2[:, DK:, :] = near[3, :, DK:, :].astype(bf16)
    down2[:, :DK, :] = near[4, :, :DK, :].astype(bf16)
    down2[:, DK:, :] = (near[4, :, DK:, :] + from_right[:, width:, :].astype(f32)).astype(bf16)


def finish_kernel(near, a, b, c, d, pieces, dq, dk, dv):
    f32 = jnp.float32
    for j in range(near.shape[1]):
        total = near[0, j] + ((a[j].astype(f32) + b[j].astype(f32)) + (c[j].astype(f32) + d[j].astype(f32)))
        dq[j] = total.T
    kv = pieces[0].astype(f32)
    for i in range(1, pieces.shape[0]):
        kv = kv + pieces[i].astype(f32)
    width = dk.shape[1]
    dk[...] = kv[:, :width]
    dv[...] = kv[:, width:]


def per_device(queries, comp_keys, comp_values, outputs, grad_out, log_sums, visible):
    pb = lax.axis_size("pb")
    ka = lax.axis_size("ka")
    chips = pb // 2
    core = lax.rem(lax.axis_index("pb"), 2)
    same_core = [[2 * i + c for i in range(chips)] for c in range(2)]
    other_core = [(i, i ^ 1) for i in range(pb)]
    rows, width = comp_keys.shape
    both = width + comp_values.shape[1]
    heads, count, _ = queries.shape
    per_owner = heads // ka
    keys = 2 * chips * rows
    half = keys // 2
    f32, bf16 = jnp.float32, jnp.bfloat16
    shape = jax.ShapeDtypeStruct

    def along(x, step):
        return lax.ppermute(x, "ka", [(i, (i + step) % ka) for i in range(ka)])

    copies = pl.pallas_call(
        copies_kernel,
        out_shape=shape((chips, rows, both), bf16),
        in_specs=[HBM, HBM],
        out_specs=HBM,
        scratch_shapes=[pltpu.VMEM((rows, both), bf16), pltpu.SemaphoreType.DMA((2 + chips,))],
        compiler_params=pltpu.CompilerParams(vmem_limit_bytes=GRANT),
        name="copies",
    )(comp_keys, comp_values)
    own = lax.all_to_all(copies, "pb", 0, 0, axis_index_groups=same_core, tiled=True).reshape(half, both)
    delta = jnp.stack([
        jnp.sum(
            grad_out[:, :, g * DV:(g + 1) * DV].astype(f32) * outputs[:, :, g * DV:(g + 1) * DV].astype(f32), axis=2
        )
        for g in range(GROUPS)
    ])
    seen = visible.reshape(visible.shape[0], chips, 2, rows)
    seen = jnp.where(core == 0, seen, seen[:, :, ::-1])
    seen = seen.transpose(2, 1, 3, 0).reshape(keys, visible.shape[0])
    mask = jnp.repeat(seen.astype(f32), QBLK, axis=1)
    own, delta, mask = lax.optimization_barrier((own, delta, mask))
    par = lax.ppermute(own, "pb", other_core)

    args = (queries, grad_out, mask, log_sums, delta)
    hops = shape((per_owner, width + DK, count), bf16)
    chunk = (per_owner, width, count)
    right, left, kz, vz, kt = grads(
        far_kernel, len(FAR), 2 * DK + DV,
        (
            hops, hops, shape((GROUPS, keys, WIN), bf16), shape((GROUPS, keys, DV), bf16),
            shape((GROUPS, DK, keys), bf16),
        ),
        [pltpu.VMEM((len(FAR), *chunk), bf16)], *args, own, par,
    )
    from_left = along(right, 2)
    from_right = along(left, -2)
    near, own_kv, par_kv = grads(
        near_kernel, KA, 3 * DK + 2 * DV,
        (shape((len(NEAR), *chunk), f32), shape((half, both), f32), shape((half, both), bf16)),
        [pltpu.VMEM((GROUPS, keys, WIN), f32), pltpu.VMEM((GROUPS, keys, DV), f32)], *args, kz, vz, kt,
    )
    from_other = lax.ppermute(par_kv, "pb", other_core)

    up2, down2, up1, down1 = small(message_kernel, (shape(chunk, bf16),) * 4, near, from_left, from_right)
    from_up2 = along(up2, 2)
    from_down2 = along(down2, -2)
    from_up1 = along(up1, 1)
    from_down1 = along(down1, -1)
    chip_sum = (own_kv + from_other.astype(f32)).astype(bf16)
    pieces = lax.all_to_all(chip_sum.reshape(chips, rows, both), "pb", 0, 0, axis_index_groups=same_core, tiled=True)
    arrived = (from_up2, from_down2, from_up1, from_down1)
    return small(
        finish_kernel,
        (shape((per_owner, count, width), f32), shape((rows, width), f32), shape((rows, both - width), f32)),
        near, *arrived, pieces,
    )


def solution(mesh):
    return jax.shard_map(
        per_device,
        mesh=mesh,
        in_specs=(
            P(None, "pb", "ga"),
            P(("ka", "pb"), "ga"),
            P(("ka", "pb"), "ga"),
            P(None, "pb", "ga"),
            P(None, "pb", "ga"),
            P("ga", None, "pb"),
            P("pb", "ka"),
        ),
        out_specs=(P("ka", "pb", "ga"), P(("ka", "pb"), "ga"), P(("ka", "pb"), "ga")),
        check_vma=False,
    )
```

time: 95.5 us -> 89.9 us (0.941)
  Pallas kernels: 24.8 us -> 17.6 us
  local copies, waits for them, and re-layouts: 3.49 us -> 7.46 us
  other arithmetic: 3.68 us -> 1.6 us
    pallas_call x2 -> x3, Pallas kernels: 22.9 us -> 16.5 us  [the longest x2 15.6 us: grads(): pl.pallas_call(kernel, out_shape=outs, in_specs=[VMEM] * len(args), out_s...]
    unnamed x18 -> x22, local copies, waits for them, and re-layouts: 1.58 us -> 4.51 us
    convert_element_type x1, other arithmetic: 2.45 us -> 0.97 us  [per_device(): chip_sum = (own_kv + from_other.astype(f32)).astype(bf16)]
    pallas_call x3 -> x2, Pallas kernels: 1.96 us -> 1.06 us  [small(): pl.pallas_call(kernel, out_shape=outs, in_specs=[VMEM] * len(args), out_s...]
where the time goes in v6:
time: 89.9 us; the launch traced here: 89.4 us
  waiting for transfers between devices  36.6 us (41%)
  starting transfers between devices  25.4 us (28%)
  Pallas kernels  17.6 us (20%)
  local copies, waits for them, and re-layouts  7.46 us (8%)
  other arithmetic  1.6 us (2%)
    ppermute x6, waiting for transfers between devices, along(): return lax.ppermute(x, 'ka', [(i, (i + step) % ka) for i in range(ka)])  24.1 us
    pallas_call x2, Pallas kernels, grads(): pl.pallas_call(kernel, out_shape=outs, in_specs=[VMEM] * len(args), out_s...  15.6 us
    ppermute x6, starting transfers between devices, along(): return lax.ppermute(x, 'ka', [(i, (i + step) % ka) for i in range(ka)])  12.5 us
    all_to_all x1, waiting for transfers between devices, per_device(): lax.all_to_all(copies, 'pb', 0, 0, axis_index_groups=same_core, tiled=True)  10.3 us
    all_to_all x1, starting transfers between devices, per_device(): lax.all_to_all(copies, 'pb', 0, 0, axis_index_groups=same_core, tiled=True)  7.48 us
    unnamed x22, local copies, waits for them, and re-layouts  4.51 us
    all_to_all x1, starting transfers between devices, per_device(): lax.all_to_all(chip_sum.reshape(chips, rows, both), 'pb', 0, 0, axis_inde...  3.67 us
  transfers between devices with their start and end apart: 10, of which 8 were waited for; matrix products, arithmetic and copies ran while one was open for 3% of the time, Pallas kernels for 0%

profile of v6, /device:TPU:1, one launch (start us, length us, event | category | flops | bytes accessed | tf_op | source)
XLA Modules:
  0.0 89.4 jit_solution(16255455323130064424)
XLA Ops:
  0.7 0.9 copy-done.1
  1.5 0.8 copy-done.2
  2.3 1.0 %copies.1 = bf16[8,64,640]{2,1,0:T(8,128)(2,1)} custom-call(bf16[64,384]{1,0:T(8,128)(2,1)S(1)} %copy-done.1, bf16[64,256]{1,0:T(8,128)(2,1)S(1)} %copy-done.2), custom_call_target="tpu_custom_call" | custom-call | tf_op jit(solution)/shard_map/copies/pallas_call | solution.py:222
  3.3 7.5 %all-to-all-start = ((bf16[8,64,640]{2,1,0:T(8,128)(2,1)}), bf16[8,64,640]{2,1,0:T(8,128)(2,1)S(1)}, u32[]{:S(2)}, u32[]{:S(2)}) async-start(bf16[8,64,640]{2,1,0:T(8,128)(2,1)} %copies.1), calls=%async_computation | async-start | bytes 1310720 | tf_op jit(solution)/shard_map/all_to_all | solution.py:231
  10.7 0.8 reshape.21
  11.6 0.6 multiply_reduce_fusion.1
  12.3 10.3 %all-to-all-done = bf16[8,64,640]{2,1,0:T(8,128)(2,1)S(1)} async-done(((bf16[8,64,640]{2,1,0:T(8,128)(2,1)}), bf16[8,64,640]{2,1,0:T(8,128)(2,1)S(1)}, u32[]{:S(2)}, u32[]{:S(2)}) %all-to-all-start) | async-done | bytes 655392 | tf_op jit(solution)/shard_map/all_to_all | solution.py:231
  22.6 0.9 broadcast_in_dim.3
  23.4 1.2 %collective-permute-start = (bf16[512,640]{1,0:T(8,128)(2,1)S(1)}, bf16[512,640]{1,0:T(8,128)(2,1)S(1)}, u32[]{:S(2)}, u32[]{:S(2)}) collective-permute-start(bf16[512,640]{1,0:T(8,128)(2,1)S(1)} %bitcast.11), channel_id=1, source_target_pairs={{0,16},{16,0},{32,48},{48,32},{64,80},{80,64},{96,112},{112,96},{1... | collective-permute-start | bytes 1966088 | tf_op jit(solution)/shard_map/ppermute | solution.py:243
  24.7 1.2 %copy.13.mask_ref = f32[1024,128]{1,0:T(8,128)S(1)} copy(f32[1024,128]{0,1:T(8,128)} %bitcast.14) | data formatting | bytes 1048576 | tf_op jit(solution)/shard_map/optimization_barrier | solution.py:242
  25.9 0.5 collective-permute-done.par_ref
  26.4 1.4 %copy-done.3 = bf16[16,128,384]{2,1,0:T(8,128)(2,1)S(1)} copy-done((bf16[16,128,384]{2,1,0:T(8,128)(2,1)S(1)}, bf16[16,128,384]{2,1,0:T(8,128)(2,1)}, u32[]{:S(2)}) %copy-start.3) | copy-done | bytes 1572888
  27.8 3.9 %shard_map.94 = (bf16[2,576,128]{2,1,0:T(8,128)(2,1)S(1)}, bf16[2,576,128]{2,1,0:T(8,128)(2,1)S(1)}, bf16[2,1024,256]{2,1,0:T(8,128)(2,1)S(1)}, bf16[2,1024,128]...) custom-call(bf16[16,128,384]{2,1,0:T(8,128)(2,1)S(1)} %copy-done.3, bf16[16,128,256]{2,1,0:T(8,128)(2,1)S(1)} %copy-done, ...), custom_call_target="tpu_custom_call" | custom-call | flops 1610612736 | bytes 6000000 | tf_op jit(solution)/shard_map/pallas_call | solution.py:141
  31.7 0.7 copy-done.4
  32.4 0.7 copy-done.6
  33.2 11.7 %shard_map.95 = (f32[5,2,384,128]{3,2,1,0:T(8,128)S(1)}, f32[512,640]{1,0:T(8,128)S(1)}, bf16[512,640]{1,0:T(8,128)(2,1)S(1)}) custom-call(bf16[16,128,384]{2,1,0:T(8,128)(2,1)S(1)} %copy-done.3, bf16[16,128,256]{2,1,0:T(8,128)(2,1)S(1)} %copy-done, f32[1024,128]{1,0:T(8,128)S(1)} %copy.13.mask_ref, f32[2,16,128]{2,1,0:T(8,128)S(1)} %copy-done.9, ...), custom_call_target="tpu_custom_call" | custom-call | flops 6979321856 | bytes 6000000 | tf_op jit(solution)/shard_map/pallas_call | solution.py:141
  44.9 0.5 collective-permute-start.7
  45.3 1.7 %collective-permute-done.7 = bf16[512,640]{1,0:T(8,128)(2,1)S(1)} collective-permute-done((bf16[512,640]{1,0:T(8,128)(2,1)S(1)}, bf16[512,640]{1,0:T(8,128)(2,1)S(1)}, u32[]{:S(2)}, u32[]{:S(2)}) %collective-permute-start.7) | collective-permute-done | bytes 655392 | tf_op jit(solution)/shard_map/ppermute | solution.py:263
  47.0 1.0 %add_convert_fusion = bf16[512,640]{1,0:T(8,128)(2,1)} fusion(f32[512,640]{1,0:T(8,128)S(1)} %get-tuple-element.31, bf16[512,640]{1,0:T(8,128)(2,1)S(1)} %collective-permute-done.7), kind=kLoop, calls=%fused_computation | loop fusion | flops 983040 | bytes 2621440 | tf_op jit(solution)/shard_map/convert_element_type | solution.py:270
  48.0 3.7 %all-to-all-start.1 = ((bf16[8,64,640]{2,1,0:T(8,128)(2,1)}), bf16[8,64,640]{2,1,0:T(8,128)(2,1)S(1)}, u32[]{:S(2)}, u32[]{:S(2)}) async-start(bf16[8,64,640]{2,1,0:T(8,128)(2,1)} %bitcast.13), calls=%async_computation.1 | async-start | bytes 1310720 | tf_op jit(solution)/shard_map/all_to_all | solution.py:271
  51.7 3.1 %collective-permute-start.1 = (bf16[2,576,128]{2,1,0:T(8,128)(2,1)S(1)}, bf16[2,576,128]{2,1,0:T(8,128)(2,1)S(1)}, u32[]{:S(2)}, u32[]{:S(2)}) collective-permute-start(bf16[2,576,128]{2,1,0:T(8,128)(2,1)S(1)} %copy-done.7), channel_id=1, source_target_pairs={{0,4},{2,6},{4,8},{6,10},{8,12},{10,14},{12,0},{14,2},{1,5},{3,7},... | collective-permute-start | bytes 884744 | tf_op jit(solution)/shard_map/ppermute | solution.py:220
  54.8 3.1 %collective-permute-start.2 = (bf16[2,576,128]{2,1,0:T(8,128)(2,1)S(1)}, bf16[2,576,128]{2,1,0:T(8,128)(2,1)S(1)}, u32[]{:S(2)}, u32[]{:S(2)}) collective-permute-start(bf16[2,576,128]{2,1,0:T(8,128)(2,1)S(1)} %copy-done.5), channel_id=1, source_target_pairs={{0,12},{2,14},{4,0},{6,2},{8,4},{10,6},{12,8},{14,10},{1,13},{3,15... | collective-permute-start | bytes 884744 | tf_op jit(solution)/shard_map/ppermute | solution.py:220
  57.9 8.9 %collective-permute-done.1.from_left = bf16[2,576,128]{2,1,0:T(8,128)(2,1)S(1)} collective-permute-done((bf16[2,576,128]{2,1,0:T(8,128)(2,1)S(1)}, bf16[2,576,128]{2,1,0:T(8,128)(2,1)S(1)}, u32[]{:S(2)}, u32[]{:S(2)}) %collective-permute-start.1) | collective-permute-done | bytes 294944 | tf_op jit(solution)/shard_map/ppermute | solution.py:220
  66.8 5.6 %collective-permute-done.2.from_right = bf16[2,576,128]{2,1,0:T(8,128)(2,1)S(1)} collective-permute-done((bf16[2,576,128]{2,1,0:T(8,128)(2,1)S(1)}, bf16[2,576,128]{2,1,0:T(8,128)(2,1)S(1)}, u32[]{:S(2)}, u32[]{:S(2)}) %collective-permute-start.2) | collective-permute-done | bytes 294944 | tf_op jit(solution)/shard_map/ppermute | solution.py:220
  72.3 0.1 shard_map.96
  72.4 3.5 %collective-permute-start.3 = (bf16[2,384,128]{2,1,0:T(8,128)(2,1)S(1)}, bf16[2,384,128]{2,1,0:T(8,128)(2,1)S(1)}, u32[]{:S(2)}, u32[]{:S(2)}) collective-permute-start(bf16[2,384,128]{2,1,0:T(8,128)(2,1)S(1)} %get-tuple-element.27), channel_id=1, source_target_pairs={{0,4},{2,6},{4,8},{6,10},{8,12},{10,14},{12,0},{14,2},{1,5},{3,7},... | collective-permute-start | bytes 589832 | tf_op jit(solution)/shard_map/ppermute | solution.py:220
  75.9 0.2 collective-permute-start.4
  76.1 2.7 %collective-permute-start.6 = (bf16[2,384,128]{2,1,0:T(8,128)(2,1)S(1)}, bf16[2,384,128]{2,1,0:T(8,128)(2,1)S(1)}, u32[]{:S(2)}, u32[]{:S(2)}) collective-permute-start(bf16[2,384,128]{2,1,0:T(8,128)(2,1)S(1)} %get-tuple-element.30), channel_id=1, source_target_pairs={{0,14},{2,0},{4,2},{6,4},{8,6},{10,8},{12,10},{14,12},{1,15},{3,1}... | collective-permute-start | bytes 589832 | tf_op jit(solution)/shard_map/ppermute | solution.py:220
  78.8 5.5 %collective-permute-done.3.a = bf16[2,384,128]{2,1,0:T(8,128)(2,1)S(1)} collective-permute-done((bf16[2,384,128]{2,1,0:T(8,128)(2,1)S(1)}, bf16[2,384,128]{2,1,0:T(8,128)(2,1)S(1)}, u32[]{:S(2)}, u32[]{:S(2)}) %collective-permute-start.3) | collective-permute-done | bytes 196640 | tf_op jit(solution)/shard_map/ppermute | solution.py:220
  84.3 3.9 %collective-permute-done.5.c = bf16[2,384,128]{2,1,0:T(8,128)(2,1)S(1)} collective-permute-done((bf16[2,384,128]{2,1,0:T(8,128)(2,1)S(1)}, bf16[2,384,128]{2,1,0:T(8,128)(2,1)S(1)}, u32[]{:S(2)}, u32[]{:S(2)}) %collective-permute-start.5) | collective-permute-done | bytes 196640 | tf_op jit(solution)/shard_map/ppermute | solution.py:220
  88.2 0.2 collective-permute-done.6.d
  88.5 0.9 %shard_map.97 = (f32[2,128,384]{2,1,0:T(8,128)}, f32[64,384]{1,0:T(8,128)}, f32[64,256]{1,0:T(8,128)}) custom-call(f32[5,2,384,128]{3,2,1,0:T(8,128)S(1)} %get-tuple-element.24.near, bf16[2,384,128]{2,1,0:T(8,128)(2,1)S(1)} %collective-permute-done.3.a, bf16[2,384,128]{2,1,0:T(8,128)(2,1)S(1)} %collective-permute-done.4.b, ...), custom_call_target="tpu_custom_call" | custom-call | tf_op jit(solution)/shard_map/pallas_call | solution.py:153
  (24 shorter events, 0.1 us)
Async XLA Ops:
  0.6 11.0 %copy-start = (bf16[16,128,256]{2,1,0:T(8,128)(2,1)S(1)}, bf16[16,128,256]{2,1,0:T(8,128)(2,1)}, u32[]{:S(2)}) copy-start(bf16[16,128,256]{2,1,0:T(8,128)(2,1)} %do_ref.3) | copy-start | bytes 3145732
  0.6 0.9 copy-start.1
  1.5 0.8 copy-start.2
  2.3 9.3 %copy-start.10 = (bf16[16,128,256]{2,1,0:T(8,128)(2,1)S(1)}, bf16[16,128,256]{2,1,0:T(8,128)(2,1)}, u32[]{:S(2)}) copy-start(bf16[16,128,256]{2,1,0:T(8,128)(2,1)} %param.10) | copy-start | bytes 3145732
  3.3 19.3 %all-to-all-start = ((bf16[8,64,640]{2,1,0:T(8,128)(2,1)}), bf16[8,64,640]{2,1,0:T(8,128)(2,1)S(1)}, u32[]{:S(2)}, u32[]{:S(2)}) async-start(bf16[8,64,640]{2,1,0:T(8,128)(2,1)} %copies.1), calls=%async_computation | async-start | bytes 1310720 | tf_op jit(solution)/shard_map/all_to_all | solution.py:231
  12.3 14.1 %copy-start.8 = (f32[2,16,128]{2,1,0:T(8,128)S(1)}, f32[2,16,128]{2,1,0:T(8,128)}, u32[]{:S(2)}) copy-start(f32[2,16,128]{2,1,0:T(8,128)} %lse_ref.3) | copy-start | bytes 49156
  23.4 3.0 %collective-permute-start = (bf16[512,640]{1,0:T(8,128)(2,1)S(1)}, bf16[512,640]{1,0:T(8,128)(2,1)S(1)}, u32[]{:S(2)}, u32[]{:S(2)}) collective-permute-start(bf16[512,640]{1,0:T(8,128)(2,1)S(1)} %bitcast.11), channel_id=1, source_target_pairs={{0,16},{16,0},{32,48},{48,32},{64,80},{80,64},{96,112},{112,96},{1... | collective-permute-start | bytes 1966088 | tf_op jit(solution)/shard_map/ppermute | solution.py:243
  26.4 1.4 %copy-start.3 = (bf16[16,128,384]{2,1,0:T(8,128)(2,1)S(1)}, bf16[16,128,384]{2,1,0:T(8,128)(2,1)}, u32[]{:S(2)}) copy-start(bf16[16,128,384]{2,1,0:T(8,128)(2,1)} %q_ref.3) | copy-start | bytes 4718596
  27.8 5.4 %copy-start.9 = (f32[2,16,128]{2,1,0:T(8,128)S(1)}, f32[2,16,128]{2,1,0:T(8,128)}, u32[]{:S(2)}) copy-start(f32[2,16,128]{2,1,0:T(8,128)} %lse_ref.3) | copy-start | bytes 49156
  31.7 0.7 copy-start.4
  32.4 0.7 copy-start.6
  44.9 2.2 %collective-permute-start.7 = (bf16[512,640]{1,0:T(8,128)(2,1)S(1)}, bf16[512,640]{1,0:T(8,128)(2,1)S(1)}, u32[]{:S(2)}, u32[]{:S(2)}) collective-permute-start(bf16[512,640]{1,0:T(8,128)(2,1)S(1)} %get-tuple-element.32), channel_id=1, source_target_pairs={{0,16},{16,0},{32,48},{48,32},{64,80},{80,64},{96,112},{112,96},{1... | collective-permute-start | bytes 1966088 | tf_op jit(solution)/shard_map/ppermute | solution.py:263
  48.0 3.7 %copy-start.7 = (bf16[2,576,128]{2,1,0:T(8,128)(2,1)S(1)}, bf16[2,576,128]{2,1,0:T(8,128)(2,1)}, u32[]{:S(2)}) copy-start(bf16[2,576,128]{2,1,0:T(8,128)(2,1)} %copy-done.6) | copy-start | bytes 884740
  48.0 6.8 %copy-start.5 = (bf16[2,576,128]{2,1,0:T(8,128)(2,1)S(1)}, bf16[2,576,128]{2,1,0:T(8,128)(2,1)}, u32[]{:S(2)}) copy-start(bf16[2,576,128]{2,1,0:T(8,128)(2,1)} %copy-done.4) | copy-start | bytes 884740
  48.0 40.5 %all-to-all-start.1 = ((bf16[8,64,640]{2,1,0:T(8,128)(2,1)}), bf16[8,64,640]{2,1,0:T(8,128)(2,1)S(1)}, u32[]{:S(2)}, u32[]{:S(2)}) async-start(bf16[8,64,640]{2,1,0:T(8,128)(2,1)} %bitcast.13), calls=%async_computation.1 | async-start | bytes 1310720 | tf_op jit(solution)/shard_map/all_to_all | solution.py:271
  51.7 15.1 %collective-permute-start.1 = (bf16[2,576,128]{2,1,0:T(8,128)(2,1)S(1)}, bf16[2,576,128]{2,1,0:T(8,128)(2,1)S(1)}, u32[]{:S(2)}, u32[]{:S(2)}) collective-permute-start(bf16[2,576,128]{2,1,0:T(8,128)(2,1)S(1)} %copy-done.7), channel_id=1, source_target_pairs={{0,4},{2,6},{4,8},{6,10},{8,12},{10,14},{12,0},{14,2},{1,5},{3,7},... | collective-permute-start | bytes 884744 | tf_op jit(solution)/shard_map/ppermute | solution.py:220
  54.8 17.5 %collective-permute-start.2 = (bf16[2,576,128]{2,1,0:T(8,128)(2,1)S(1)}, bf16[2,576,128]{2,1,0:T(8,128)(2,1)S(1)}, u32[]{:S(2)}, u32[]{:S(2)}) collective-permute-start(bf16[2,576,128]{2,1,0:T(8,128)(2,1)S(1)} %copy-done.5), channel_id=1, source_target_pairs={{0,12},{2,14},{4,0},{6,2},{8,4},{10,6},{12,8},{14,10},{1,13},{3,15... | collective-permute-start | bytes 884744 | tf_op jit(solution)/shard_map/ppermute | solution.py:220
  72.4 11.9 %collective-permute-start.3 = (bf16[2,384,128]{2,1,0:T(8,128)(2,1)S(1)}, bf16[2,384,128]{2,1,0:T(8,128)(2,1)S(1)}, u32[]{:S(2)}, u32[]{:S(2)}) collective-permute-start(bf16[2,384,128]{2,1,0:T(8,128)(2,1)S(1)} %get-tuple-element.27), channel_id=1, source_target_pairs={{0,4},{2,6},{4,8},{6,10},{8,12},{10,14},{12,0},{14,2},{1,5},{3,7},... | collective-permute-start | bytes 589832 | tf_op jit(solution)/shard_map/ppermute | solution.py:220
  75.9 8.4 %collective-permute-start.4 = (bf16[2,384,128]{2,1,0:T(8,128)(2,1)S(1)}, bf16[2,384,128]{2,1,0:T(8,128)(2,1)S(1)}, u32[]{:S(2)}, u32[]{:S(2)}) collective-permute-start(bf16[2,384,128]{2,1,0:T(8,128)(2,1)S(1)} %get-tuple-element.28), channel_id=1, source_target_pairs={{0,12},{2,14},{4,0},{6,2},{8,4},{10,6},{12,8},{14,10},{1,13},{3,15... | collective-permute-start | bytes 589832 | tf_op jit(solution)/shard_map/ppermute | solution.py:220
  76.1 12.1 %collective-permute-start.5 = (bf16[2,384,128]{2,1,0:T(8,128)(2,1)S(1)}, bf16[2,384,128]{2,1,0:T(8,128)(2,1)S(1)}, u32[]{:S(2)}, u32[]{:S(2)}) collective-permute-start(bf16[2,384,128]{2,1,0:T(8,128)(2,1)S(1)} %get-tuple-element.29), channel_id=1, source_target_pairs={{0,2},{2,4},{4,6},{6,8},{8,10},{10,12},{12,14},{14,0},{1,3},{3,5},... | collective-permute-start | bytes 589832 | tf_op jit(solution)/shard_map/ppermute | solution.py:220
  76.1 12.4 %collective-permute-start.6 = (bf16[2,384,128]{2,1,0:T(8,128)(2,1)S(1)}, bf16[2,384,128]{2,1,0:T(8,128)(2,1)S(1)}, u32[]{:S(2)}, u32[]{:S(2)}) collective-permute-start(bf16[2,384,128]{2,1,0:T(8,128)(2,1)S(1)} %get-tuple-element.30), channel_id=1, source_target_pairs={{0,14},{2,0},{4,2},{6,4},{8,6},{10,8},{12,10},{14,12},{1,15},{3,1}... | collective-permute-start | bytes 589832 | tf_op jit(solution)/shard_map/ppermute | solution.py:220

commit v7 on v6

--- a/solution.py
+++ b/solution.py
@@ -37,54 +37,72 @@
     return result
 
 
-def load_keys(own_ref, par_ref, kz, vz, kt):
-    half = own_ref.shape[0]
+def load_keys(ref, at, kz, vz, kt):
+    half = ref.shape[0]
     lane = lax.broadcasted_iota(jnp.int32, (half, WIN), 1)
     one = lax.broadcasted_iota(jnp.int32, (DK, WIN), 0)
     column = lax.broadcasted_iota(jnp.int32, (DK, WIN), 1)
-    for side, ref in enumerate((own_ref, par_ref)):
-        at = side * half
-        for group in range(GROUPS):
-            first = 0 if group == 0 else WIN - DK
-            keep = (lane >= first) & (lane < first + DK)
-            lo = group * LANES
-            vlo = 3 * LANES + lo
-            k = jnp.where(keep, ref[:, lo:lo + WIN], jnp.zeros((), jnp.bfloat16))
-            kz[group, at:at + half, :] = k
-            vz[group, at:at + half, :] = ref[:, vlo:vlo + DV]
-            turn = jnp.where(column == one + first, 1.0, 0.0).astype(jnp.bfloat16)
-            kt[group, :, at:at + half] = dot(turn, k, NT).astype(jnp.bfloat16)
-
-
-def group_terms(group, h, per_owner, q_ref, do_ref, mask_ref, lse_ref, delta_ref, kz, vz):
+    for group in range(GROUPS):
+        first = 0 if group == 0 else WIN - DK
+        keep = (lane >= first) & (lane < first + DK)
+        lo = group * LANES
+        vlo = 3 * LANES + lo
+        k = jnp.where(keep, ref[:, lo:lo + WIN], jnp.zeros((), jnp.bfloat16))
+        kz[group, at:at + half, :] = k
+        vz[group, at:at + half, :] = ref[:, vlo:vlo + DV]
+        turn = jnp.where(column == one + first, 1.0, 0.0).astype(jnp.bfloat16)
+        kt[group, :, at:at + half] = dot(turn, k, NT).astype(jnp.bfloat16)
+
+
+def group_terms(group, keys, h, q_at, per_owner, q_ref, do_ref, mask_ref, lse_ref, delta_ref, kz, vz):
     rows = per_owner * q_ref.shape[1]
     lo = group * LANES
-    q = q_ref[pl.ds(h, per_owner), :, lo:lo + WIN].reshape(rows, WIN)
+    q = q_ref[pl.ds(q_at, per_owner), :, lo:lo + WIN].reshape(rows, WIN)
     do = do_ref[pl.ds(h, per_owner), :, lo:lo + DV].reshape(rows, DV)
     lse = jnp.concatenate([lse_ref[group, pl.ds(h + j, 1), :] for j in range(per_owner)], axis=1) * LOG2E
     delta = jnp.concatenate([delta_ref[group, pl.ds(h + j, 1), :] for j in range(per_owner)], axis=1)
-    s = dot(kz[group], q, NT)
-    dp = dot(vz[group], do, NT)
-    p = jnp.exp2(s * (SCALE * LOG2E) - lse) * jnp.concatenate([mask_ref[...]] * per_owner, axis=1)
+    s = dot(kz[group, keys, :], q, NT)
+    dp = dot(vz[group, keys, :], do, NT)
+    p = jnp.exp2(s * (SCALE * LOG2E) - lse) * jnp.concatenate([mask_ref[keys, :]] * per_owner, axis=1)
     ds = (p * (dp - delta)).astype(jnp.bfloat16)
     return q, do, p.astype(jnp.bfloat16), ds
 
 
-def far_kernel(q_ref, do_ref, mask_ref, lse_ref, delta_ref, own_ref, par_ref, right, left, kz, vz, kt, held):
-    per_owner, _, count = right.shape
+def far_terms(side, args, key_ref, kz, vz, kt, emit):
+    per_owner = args[0].shape[0] // len(FAR)
+    count = args[0].shape[1]
+    half = key_ref.shape[0]
+    at = side * half
     me = lax.axis_index("ka")
-    load_keys(own_ref, par_ref, kz, vz, kt)
+    load_keys(key_ref, at, kz, vz, kt)
 
     def one(i, carry):
         h = per_owner * lax.rem(me + pick(i, FAR), KA)
         for group in range(GROUPS):
-            ds = group_terms(group, h, per_owner, q_ref, do_ref, mask_ref, lse_ref, delta_ref, kz, vz)[3]
-            dqt = dot(kt[group], ds, NN) * SCALE
+            ds = group_terms(group, slice(at, at + half), h, per_owner * i, per_owner, *args, kz, vz)[3]
+            dqt = dot(kt[group, :, at:at + half], ds, NN)
             for j in range(per_owner):
-                held[i, j, group * DK:(group + 1) * DK, :] = dqt[:, j * count:(j + 1) * count].astype(held.dtype)
+                emit(i, j, slice(group * DK, (group + 1) * DK), dqt[:, j * count:(j + 1) * count])
         return carry
 
     lax.fori_loop(0, len(FAR), one, 0)
+
+
+def far_own_kernel(q_ref, do_ref, mask_ref, lse_ref, delta_ref, own_ref, partial, kz, vz, kt):
+    def emit(i, j, where, value):
+        partial[i, j, where, :] = value
+
+    far_terms(0, (q_ref, do_ref, mask_ref, lse_ref, delta_ref), own_ref, kz, vz, kt, emit)
+
+
+def far_par_kernel(q_ref, do_ref, mask_ref, lse_ref, delta_ref, par_ref, partial, in_kz, in_vz, in_kt,
+                   right, left, kz, vz, kt, held):
+    del in_kz, in_vz, in_kt
+
+    def emit(i, j, where, value):
+        held[i, j, where, :] = ((partial[i, j, where, :] + value) * SCALE).astype(held.dtype)
+
+    far_terms(1, (q_ref, do_ref, mask_ref, lse_ref, delta_ref), par_ref, kz, vz, kt, emit)
     width = GROUPS * DK
     right[:, :width, :] = held[0]
     left[:, :width, :] = held[1]
@@ -103,7 +121,8 @@
     def one(i, query_grads):
         h = per_owner * lax.rem(me + pick(i, steps), KA)
         for group in range(GROUPS):
-            q, do, p, ds = group_terms(group, h, per_owner, q_ref, do_ref, mask_ref, lse_ref, delta_ref, kz, vz)
+            q, do, p, ds = group_terms(
+                group, slice(None), h, h, per_owner, q_ref, do_ref, mask_ref, lse_ref, delta_ref, kz, vz)
             acc_v[group] += dot(p, do, NN)
             acc_k[group] += dot(ds, q, NN)
             if query_grads:
@@ -134,16 +153,15 @@
             out[:, vlo:vlo + DV] = acc_v[group, at:at + half, :].astype(out.dtype)
 
 
-def grads(kernel, owners, matmuls, outs, scratch, *args):
-    heads, count, _ = args[0].shape
-    keys = args[2].shape[0]
-    terms = GROUPS * owners * (heads // KA) * count * keys
+def grads(kernel, rows, keys, matmuls, outs, scratch, *args, aliases=None):
+    terms = GROUPS * rows * keys
     return pl.pallas_call(
         kernel,
         out_shape=outs,
         in_specs=[VMEM] * len(args),
         out_specs=tuple(VMEM for _ in outs),
         scratch_shapes=scratch,
+        input_output_aliases=aliases or {},
         cost_estimate=pl.CostEstimate(flops=2 * terms * matmuls, bytes_accessed=6_000_000, transcendentals=terms),
         compiler_params=pltpu.CompilerParams(vmem_limit_bytes=GRANT),
     )(*args)
@@ -225,7 +243,7 @@
         in_specs=[HBM, HBM],
         out_specs=HBM,
         scratch_shapes=[pltpu.VMEM((rows, both), bf16), pltpu.SemaphoreType.DMA((2 + chips,))],
-        compiler_params=pltpu.CompilerParams(vmem_limit_bytes=GRANT),
+        compiler_params=pltpu.CompilerParams(vmem_limit_bytes=67_000_000),
         name="copies",
     )(comp_keys, comp_values)
     own = lax.all_to_all(copies, "pb", 0, 0, axis_index_groups=same_core, tiled=True).reshape(half, both)
@@ -239,26 +257,34 @@
     seen = jnp.where(core == 0, seen, seen[:, :, ::-1])
     seen = seen.transpose(2, 1, 3, 0).reshape(keys, visible.shape[0])
     mask = jnp.repeat(seen.astype(f32), QBLK, axis=1)
-    own, delta, mask = lax.optimization_barrier((own, delta, mask))
+    me = lax.axis_index("ka")
+    far_q = jnp.concatenate([
+        lax.dynamic_slice_in_dim(queries, per_owner * lax.rem(me + step, ka), per_owner, 0) for step in FAR
+    ])
+    own, delta, mask, far_q = lax.optimization_barrier((own, delta, mask, far_q))
     par = lax.ppermute(own, "pb", other_core)
 
-    args = (queries, grad_out, mask, log_sums, delta)
+    rest = (grad_out, mask, log_sums, delta)
     hops = shape((per_owner, width + DK, count), bf16)
     chunk = (per_owner, width, count)
+    key_forms = (
+        shape((GROUPS, keys, WIN), bf16), shape((GROUPS, keys, DV), bf16), shape((GROUPS, DK, keys), bf16)
+    )
+    far_rows = len(FAR) * per_owner * count
+    partial, kz, vz, kt = grads(
+        far_own_kernel, far_rows, half, 2 * DK + DV, (shape((len(FAR), *chunk), f32), *key_forms), [],
+        far_q, *rest, own,
+    )
     right, left, kz, vz, kt = grads(
-        far_kernel, len(FAR), 2 * DK + DV,
-        (
-            hops, hops, shape((GROUPS, keys, WIN), bf16), shape((GROUPS, keys, DV), bf16),
-            shape((GROUPS, DK, keys), bf16),
-        ),
-        [pltpu.VMEM((len(FAR), *chunk), bf16)], *args, own, par,
+        far_par_kernel, far_rows, half, 2 * DK + DV, (hops, hops, *key_forms),
+        [pltpu.VMEM((len(FAR), *chunk), bf16)], far_q, *rest, par, partial, kz, vz, kt, aliases={7: 2, 8: 3, 9: 4},
     )
     from_left = along(right, 2)
     from_right = along(left, -2)
     near, own_kv, par_kv = grads(
-        near_kernel, KA, 3 * DK + 2 * DV,
+        near_kernel, heads * count, keys, 3 * DK + 2 * DV,
         (shape((len(NEAR), *chunk), f32), shape((half, both), f32), shape((half, both), bf16)),
-        [pltpu.VMEM((GROUPS, keys, WIN), f32), pltpu.VMEM((GROUPS, keys, DV), f32)], *args, kz, vz, kt,
+        [pltpu.VMEM((GROUPS, keys, WIN), f32), pltpu.VMEM((GROUPS, keys, DV), f32)], queries, *rest, kz, vz, kt,
     )
     from_other = lax.ppermute(par_kv, "pb", other_core)
 

time: 89.9 us -> 88.5 us (0.984)
  local copies, waits for them, and re-layouts: 7.46 us -> 1.64 us
  Pallas kernels: 17.6 us -> 22.5 us
  waiting for transfers between devices: 36.6 us -> 35 us
  other arithmetic: 1.6 us -> 2.89 us
    unnamed x22 -> x18, local copies, waits for them, and re-layouts: 4.51 us -> 0.05 us
    pallas_call x2 -> x3, Pallas kernels: 15.6 us -> 19.7 us  [grads(): pl.pallas_call(kernel, out_shape=outs, in_specs=[VMEM] * len(args), out_s...]
    all_to_all x1, waiting for transfers between devices: 10.3 us -> 8.6 us  [per_device(): lax.all_to_all(copies, 'pb', 0, 0, axis_index_groups=same_core, tiled=True)]
    reduce_sum x1, other arithmetic: 0.61 us -> 1.82 us  [per_device(): jnp.sum(grad_out[:, :, g * DV:(g + 1) * DV].astype(f32) * outputs[:, :, g...]
    dynamic_slice x0 -> x1, local copies, waits for them, and re-layouts: none -> 1.19 us  [per_device(): lax.dynamic_slice_in_dim(queries, per_owner * lax.rem(me + step, ka), per...]
    optimization_barrier x1, local copies, waits for them, and re-layouts: 1.23 us -> 0.19 us  [per_device(): lax.optimization_barrier((own, delta, mask, far_q))]
  transfers between devices with their start and end apart: 10 -> 10, of which waited for: 8 -> 7; matrix products, arithmetic and copies ran while one was open for 3% -> 4% of each run, Pallas kernels for 0% -> 5%
where the time goes in v7:
time: 88.5 us; the launch traced here: 88.1 us
  waiting for transfers between devices  35 us (40%)
  starting transfers between devices  25.2 us (28%)
  Pallas kernels  22.5 us (25%)
  other arithmetic  2.89 us (3%)
  local copies, waits for them, and re-layouts  1.64 us (2%)
    ppermute x6, waiting for transfers between devices, along(): return lax.ppermute(x, 'ka', [(i, (i + step) % ka) for i in range(ka)])  24.3 us
    pallas_call x3, Pallas kernels, grads(): pl.pallas_call(kernel, out_shape=outs, in_specs=[VMEM] * len(args), out_s...  19.7 us
    ppermute x6, starting transfers between devices, along(): return lax.ppermute(x, 'ka', [(i, (i + step) % ka) for i in range(ka)])  12.5 us
    all_to_all x1, waiting for transfers between devices, per_device(): lax.all_to_all(copies, 'pb', 0, 0, axis_index_groups=same_core, tiled=True)  8.6 us
    all_to_all x1, starting transfers between devices, per_device(): lax.all_to_all(copies, 'pb', 0, 0, axis_index_groups=same_core, tiled=True)  7.61 us
    all_to_all x1, starting transfers between devices, per_device(): lax.all_to_all(chip_sum.reshape(chips, rows, both), 'pb', 0, 0, axis_inde...  3.67 us
    ppermute x1, waiting for transfers between devices, per_device(): from_other = lax.ppermute(par_kv, 'pb', other_core)  2.08 us
    reduce_sum x1, other arithmetic, per_device(): jnp.sum(grad_out[:, :, g * DV:(g + 1) * DV].astype(f32) * outputs[:, :, g...  1.82 us
  transfers between devices with their start and end apart: 10, of which 7 were waited for; matrix products, arithmetic and copies ran while one was open for 4% of the time, Pallas kernels for 5%

profile of v7, /device:TPU:1, one launch (start us, length us, event | category | flops | bytes accessed | tf_op | source)
XLA Modules:
  0.0 88.1 jit_solution(7622618174612386428)
XLA Ops:
  0.6 1.7 %copies.1 = bf16[8,64,640]{2,1,0:T(8,128)(2,1)} custom-call(bf16[64,384]{1,0:T(8,128)(2,1)} %keys.1, bf16[64,256]{1,0:T(8,128)(2,1)} %values.1), custom_call_target="tpu_custom_call" | custom-call | tf_op jit(solution)/shard_map/copies/pallas_call | solution.py:240
  2.4 0.0 copy-start
  2.4 7.6 %all-to-all-start = ((bf16[8,64,640]{2,1,0:T(8,128)(2,1)}), bf16[8,64,640]{2,1,0:T(8,128)(2,1)}, u32[]{:S(2)}, u32[]{:S(2)}) async-start(bf16[8,64,640]{2,1,0:T(8,128)(2,1)} %copies.1), calls=%async_computation | async-start | bytes 1310720 | tf_op jit(solution)/shard_map/all_to_all | solution.py:249
  10.0 0.1 reshape.21
  10.2 0.1 convert_element_type.33
  10.2 1.8 %multiply_reduce_fusion.1 = (f32[16,128]{1,0:T(8,128)S(1)}, f32[16,128]{1,0:T(8,128)S(1)}) fusion(bf16[16,128,256]{2,1,0:T(8,128)(2,1)} %param.10, bf16[16,128,256]{2,1,0:T(8,128)(2,1)S(1)} %copy-done), kind=kLoop, calls=%fused_computation.2 | loop fusion | flops 2093056 | bytes 2113536 | tf_op jit(solution)/shard_map/reduce_sum | solution.py:251
  12.1 1.2 %constant_dynamic-slice_fusion.2 = (bf16[2,128,384]{2,1,0:T(8,128)(2,1)S(1)}, bf16[2,128,384]{2,1,0:T(8,128)(2,1)S(1)}, bf16[2,128,384]{2,1,0:T(8,128)(2,1)S(1)}) fusion(bf16[16,128,384]{2,1,0:T(8,128)(2,1)} %q_ref.1, s32[]{:T(128)S(6)} %select_n.19, s32[]{:T(128)S(6)} %select_n.20, s32[]{:T(128)S(6)} %select_n.21), kind=kLoop, calls=%fused_computation.10 | loop fusion | bytes 1179660 | tf_op jit(solution)/shard_map/dynamic_slice | solution.py:262
  13.3 0.1 pad_maximum_fusion.q_ref
  13.4 8.6 %all-to-all-done = bf16[8,64,640]{2,1,0:T(8,128)(2,1)} async-done(((bf16[8,64,640]{2,1,0:T(8,128)(2,1)}), bf16[8,64,640]{2,1,0:T(8,128)(2,1)}, u32[]{:S(2)}, u32[]{:S(2)}) %all-to-all-start) | async-done | bytes 655392 | tf_op jit(solution)/shard_map/all_to_all | solution.py:249
  22.0 1.3 %collective-permute-start = (bf16[512,640]{1,0:T(8,128)(2,1)}, bf16[512,640]{1,0:T(8,128)(2,1)}, u32[]{:S(2)}, u32[]{:S(2)}) collective-permute-start(bf16[512,640]{1,0:T(8,128)(2,1)} %bitcast.own_ref), channel_id=1, source_target_pairs={{0,16},{16,0},{32,48},{48,32},{64,80},{80,64},{96,112},{112,96},{1... | collective-permute-start | bytes 1966088 | tf_op jit(solution)/shard_map/ppermute | solution.py:265
  23.3 0.2 copy.17.mask_ref
  23.5 3.9 %shard_map.94 = (f32[3,2,384,128]{3,2,1,0:T(8,128)S(1)}, bf16[2,1024,256]{2,1,0:T(8,128)(2,1)S(1)}, bf16[2,1024,128]{2,1,0:T(8,128)(2,1)S(1)}, bf16[2,192,1024]{2,1,0:T(8,128)(2,1)S(1)}) custom-call(bf16[6,128,384]{2,1,0:T(8,128)(2,1)S(1)} %pad_maximum_fusion.q_ref, bf16[16,128,256]{2,1,0:T(8,128)(2,1)S(1)} %copy-done, f32[1024,128]{1,0:T(8,128)S(1)} %copy.17.mask_ref, ...), custom_call_target="tpu_custom_call" | custom-call | flops 805306368 | bytes 6000000 | tf_op jit(solution)/shard_map/pallas_call | solution.py:158
  27.5 0.0 copy-start.1
  27.5 0.0 copy-start.3
  27.5 4.1 %shard_map.95 = (bf16[2,576,128]{2,1,0:T(8,128)(2,1)S(1)}, bf16[2,576,128]{2,1,0:T(8,128)(2,1)S(1)}, bf16[2,1024,256]{2,1,0:T(8,128)(2,1)S(1)}, bf16[2,1024,128]...) custom-call(bf16[6,128,384]{2,1,0:T(8,128)(2,1)S(1)} %pad_maximum_fusion.q_r, ...), custom_call_target="tpu_custom_call", output_to_operand_aliasing={{2}: (7, {}), {3}: (8, {}), {4}: (9, {})} | custom-call | flops 805306368 | bytes 6000000 | tf_op jit(solution)/shard_map/pallas_call | solution.py:158
  31.6 11.7 %shard_map.96 = (f32[5,2,384,128]{3,2,1,0:T(8,128)S(1)}, f32[512,640]{1,0:T(8,128)S(1)}, bf16[512,640]{1,0:T(8,128)(2,1)S(1)}) custom-call(bf16[16,128,384]{2,1,0:T(8,128)(2,1)S(1)} %copy-done.1, bf16[16,128,256]{2,1,0:T(8,128)(2,1)S(1)} %copy-done, f32[1024,128]{1,0:T(8,128)S(1)} %copy.17.mask_ref, f32[2,16,128]{2,1,0:T(8,128)S(1)} %copy-done.3, ...), custom_call_target="tpu_custom_call" | custom-call | flops 6979321856 | bytes 6000000 | tf_op jit(solution)/shard_map/pallas_call | solution.py:158
  43.4 0.1 collective-permute-start.7
  43.5 2.1 %collective-permute-done.7 = bf16[512,640]{1,0:T(8,128)(2,1)S(1)} collective-permute-done((bf16[512,640]{1,0:T(8,128)(2,1)S(1)}, bf16[512,640]{1,0:T(8,128)(2,1)S(1)}, u32[]{:S(2)}, u32[]{:S(2)}) %collective-permute-start.7) | collective-permute-done | bytes 655392 | tf_op jit(solution)/shard_map/ppermute | solution.py:289
  45.5 1.0 %add_convert_fusion = bf16[512,640]{1,0:T(8,128)(2,1)} fusion(f32[512,640]{1,0:T(8,128)S(1)} %get-tuple-element.41, bf16[512,640]{1,0:T(8,128)(2,1)S(1)} %collective-permute-done.7), kind=kLoop, calls=%fused_computation | loop fusion | flops 983040 | bytes 2621440 | tf_op jit(solution)/shard_map/convert_element_type | solution.py:296
  46.5 3.7 %all-to-all-start.1 = ((bf16[8,64,640]{2,1,0:T(8,128)(2,1)}), bf16[8,64,640]{2,1,0:T(8,128)(2,1)S(1)}, u32[]{:S(2)}, u32[]{:S(2)}) async-start(bf16[8,64,640]{2,1,0:T(8,128)(2,1)} %bitcast.11), calls=%async_computation.1 | async-start | bytes 1310720 | tf_op jit(solution)/shard_map/all_to_all | solution.py:297
  50.2 3.1 %collective-permute-start.1 = (bf16[2,576,128]{2,1,0:T(8,128)(2,1)S(1)}, bf16[2,576,128]{2,1,0:T(8,128)(2,1)S(1)}, u32[]{:S(2)}, u32[]{:S(2)}) collective-permute-start(bf16[2,576,128]{2,1,0:T(8,128)(2,1)S(1)} %copy-done.7), channel_id=1, source_target_pairs={{0,4},{2,6},{4,8},{6,10},{8,12},{10,14},{12,0},{14,2},{1,5},{3,7},... | collective-permute-start | bytes 884744 | tf_op jit(solution)/shard_map/ppermute | solution.py:238
  53.3 3.1 %collective-permute-start.2 = (bf16[2,576,128]{2,1,0:T(8,128)(2,1)S(1)}, bf16[2,576,128]{2,1,0:T(8,128)(2,1)S(1)}, u32[]{:S(2)}, u32[]{:S(2)}) collective-permute-start(bf16[2,576,128]{2,1,0:T(8,128)(2,1)S(1)} %copy-done.5), channel_id=1, source_target_pairs={{0,12},{2,14},{4,0},{6,2},{8,4},{10,6},{12,8},{14,10},{1,13},{3,15... | collective-permute-start | bytes 884744 | tf_op jit(solution)/shard_map/ppermute | solution.py:238
  56.4 9.1 %collective-permute-done.1.from_left = bf16[2,576,128]{2,1,0:T(8,128)(2,1)S(1)} collective-permute-done((bf16[2,576,128]{2,1,0:T(8,128)(2,1)S(1)}, bf16[2,576,128]{2,1,0:T(8,128)(2,1)S(1)}, u32[]{:S(2)}, u32[]{:S(2)}) %collective-permute-start.1) | collective-permute-done | bytes 294944 | tf_op jit(solution)/shard_map/ppermute | solution.py:238
  65.5 5.3 %collective-permute-done.2.from_right = bf16[2,576,128]{2,1,0:T(8,128)(2,1)S(1)} collective-permute-done((bf16[2,576,128]{2,1,0:T(8,128)(2,1)S(1)}, bf16[2,576,128]{2,1,0:T(8,128)(2,1)S(1)}, u32[]{:S(2)}, u32[]{:S(2)}) %collective-permute-start.2) | collective-permute-done | bytes 294944 | tf_op jit(solution)/shard_map/ppermute | solution.py:238
  70.8 0.1 shard_map.97
  70.9 3.6 %collective-permute-start.3 = (bf16[2,384,128]{2,1,0:T(8,128)(2,1)S(1)}, bf16[2,384,128]{2,1,0:T(8,128)(2,1)S(1)}, u32[]{:S(2)}, u32[]{:S(2)}) collective-permute-start(bf16[2,384,128]{2,1,0:T(8,128)(2,1)S(1)} %get-tuple-element.37), channel_id=1, source_target_pairs={{0,4},{2,6},{4,8},{6,10},{8,12},{10,14},{12,0},{14,2},{1,5},{3,7},... | collective-permute-start | bytes 589832 | tf_op jit(solution)/shard_map/ppermute | solution.py:238
  74.5 0.1 collective-permute-start.4
  74.6 2.7 %collective-permute-start.6 = (bf16[2,384,128]{2,1,0:T(8,128)(2,1)S(1)}, bf16[2,384,128]{2,1,0:T(8,128)(2,1)S(1)}, u32[]{:S(2)}, u32[]{:S(2)}) collective-permute-start(bf16[2,384,128]{2,1,0:T(8,128)(2,1)S(1)} %get-tuple-element.40), channel_id=1, source_target_pairs={{0,14},{2,0},{4,2},{6,4},{8,6},{10,8},{12,10},{14,12},{1,15},{3,1}... | collective-permute-start | bytes 589832 | tf_op jit(solution)/shard_map/ppermute | solution.py:238
  77.3 5.5 %collective-permute-done.3.a = bf16[2,384,128]{2,1,0:T(8,128)(2,1)S(1)} collective-permute-done((bf16[2,384,128]{2,1,0:T(8,128)(2,1)S(1)}, bf16[2,384,128]{2,1,0:T(8,128)(2,1)S(1)}, u32[]{:S(2)}, u32[]{:S(2)}) %collective-permute-start.3) | collective-permute-done | bytes 196640 | tf_op jit(solution)/shard_map/ppermute | solution.py:238
  82.8 4.0 %collective-permute-done.5.c = bf16[2,384,128]{2,1,0:T(8,128)(2,1)S(1)} collective-permute-done((bf16[2,384,128]{2,1,0:T(8,128)(2,1)S(1)}, bf16[2,384,128]{2,1,0:T(8,128)(2,1)S(1)}, u32[]{:S(2)}, u32[]{:S(2)}) %collective-permute-start.5) | collective-permute-done | bytes 196640 | tf_op jit(solution)/shard_map/ppermute | solution.py:238
  86.7 0.4 collective-permute-done.6.d
  87.1 0.9 %shard_map.98 = (f32[2,128,384]{2,1,0:T(8,128)}, f32[64,384]{1,0:T(8,128)}, f32[64,256]{1,0:T(8,128)}) custom-call(f32[5,2,384,128]{3,2,1,0:T(8,128)S(1)} %get-tuple-element.34.near, bf16[2,384,128]{2,1,0:T(8,128)(2,1)S(1)} %collective-permute-done.3.a, bf16[2,384,128]{2,1,0:T(8,128)(2,1)S(1)} %collective-permute-done.4.b, ...), custom_call_target="tpu_custom_call" | custom-call | tf_op jit(solution)/shard_map/pallas_call | solution.py:171
  (23 shorter events, 0.1 us)
Async XLA Ops:
  0.6 9.4 %copy-start.8 = (s32[2,1024]{1,0:T(2,128)S(1)}, s32[2,1024]{1,0:T(2,128)}, u32[]{:S(2)}) copy-start(s32[2,1024]{1,0:T(2,128)} %param.13) | copy-start | bytes 24580
  2.4 7.8 %copy-start = (bf16[16,128,256]{2,1,0:T(8,128)(2,1)S(1)}, bf16[16,128,256]{2,1,0:T(8,128)(2,1)}, u32[]{:S(2)}) copy-start(bf16[16,128,256]{2,1,0:T(8,128)(2,1)} %do_ref.5) | copy-start | bytes 3145732
  2.4 19.6 %all-to-all-start = ((bf16[8,64,640]{2,1,0:T(8,128)(2,1)}), bf16[8,64,640]{2,1,0:T(8,128)(2,1)}, u32[]{:S(2)}, u32[]{:S(2)}) async-start(bf16[8,64,640]{2,1,0:T(8,128)(2,1)} %copies.1), calls=%async_computation | async-start | bytes 1310720 | tf_op jit(solution)/shard_map/all_to_all | solution.py:249
  13.3 10.3 %copy-start.2 = (f32[2,16,128]{2,1,0:T(8,128)S(1)}, f32[2,16,128]{2,1,0:T(8,128)}, u32[]{:S(2)}) copy-start(f32[2,16,128]{2,1,0:T(8,128)} %lse_ref.5) | copy-start | bytes 49156
  22.0 5.5 %collective-permute-start = (bf16[512,640]{1,0:T(8,128)(2,1)}, bf16[512,640]{1,0:T(8,128)(2,1)}, u32[]{:S(2)}, u32[]{:S(2)}) collective-permute-start(bf16[512,640]{1,0:T(8,128)(2,1)} %bitcast.own_ref), channel_id=1, source_target_pairs={{0,16},{16,0},{32,48},{48,32},{64,80},{80,64},{96,112},{112,96},{1... | collective-permute-start | bytes 1966088 | tf_op jit(solution)/shard_map/ppermute | solution.py:265
  27.5 4.2 %copy-start.1 = (bf16[16,128,384]{2,1,0:T(8,128)(2,1)S(1)}, bf16[16,128,384]{2,1,0:T(8,128)(2,1)}, u32[]{:S(2)}) copy-start(bf16[16,128,384]{2,1,0:T(8,128)(2,1)} %q_ref.1) | copy-start | bytes 4718596
  27.5 4.2 %copy-start.3 = (f32[2,16,128]{2,1,0:T(8,128)S(1)}, f32[2,16,128]{2,1,0:T(8,128)}, u32[]{:S(2)}) copy-start(f32[2,16,128]{2,1,0:T(8,128)} %lse_ref.5) | copy-start | bytes 49156
  31.6 11.7 %copy-start.4 = (bf16[2,576,128]{2,1,0:T(8,128)(2,1)}, bf16[2,576,128]{2,1,0:T(8,128)(2,1)S(1)}, u32[]{:S(2)}) copy-start(bf16[2,576,128]{2,1,0:T(8,128)(2,1)S(1)} %get-tuple-element.36) | copy-start | bytes 884740
  31.6 11.7 %copy-start.6 = (bf16[2,576,128]{2,1,0:T(8,128)(2,1)}, bf16[2,576,128]{2,1,0:T(8,128)(2,1)S(1)}, u32[]{:S(2)}) copy-start(bf16[2,576,128]{2,1,0:T(8,128)(2,1)S(1)} %get-tuple-element.35) | copy-start | bytes 884740
  43.4 2.2 %collective-permute-start.7 = (bf16[512,640]{1,0:T(8,128)(2,1)S(1)}, bf16[512,640]{1,0:T(8,128)(2,1)S(1)}, u32[]{:S(2)}, u32[]{:S(2)}) collective-permute-start(bf16[512,640]{1,0:T(8,128)(2,1)S(1)} %get-tuple-element.42), channel_id=1, source_target_pairs={{0,16},{16,0},{32,48},{48,32},{64,80},{80,64},{96,112},{112,96},{1... | collective-permute-start | bytes 1966088 | tf_op jit(solution)/shard_map/ppermute | solution.py:289
  46.5 3.7 %copy-start.7 = (bf16[2,576,128]{2,1,0:T(8,128)(2,1)S(1)}, bf16[2,576,128]{2,1,0:T(8,128)(2,1)}, u32[]{:S(2)}) copy-start(bf16[2,576,128]{2,1,0:T(8,128)(2,1)} %copy-done.6) | copy-start | bytes 884740
  46.5 6.8 %copy-start.5 = (bf16[2,576,128]{2,1,0:T(8,128)(2,1)S(1)}, bf16[2,576,128]{2,1,0:T(8,128)(2,1)}, u32[]{:S(2)}) copy-start(bf16[2,576,128]{2,1,0:T(8,128)(2,1)} %copy-done.4) | copy-start | bytes 884740
  46.5 40.6 %all-to-all-start.1 = ((bf16[8,64,640]{2,1,0:T(8,128)(2,1)}), bf16[8,64,640]{2,1,0:T(8,128)(2,1)S(1)}, u32[]{:S(2)}, u32[]{:S(2)}) async-start(bf16[8,64,640]{2,1,0:T(8,128)(2,1)} %bitcast.11), calls=%async_computation.1 | async-start | bytes 1310720 | tf_op jit(solution)/shard_map/all_to_all | solution.py:297
  50.2 15.3 %collective-permute-start.1 = (bf16[2,576,128]{2,1,0:T(8,128)(2,1)S(1)}, bf16[2,576,128]{2,1,0:T(8,128)(2,1)S(1)}, u32[]{:S(2)}, u32[]{:S(2)}) collective-permute-start(bf16[2,576,128]{2,1,0:T(8,128)(2,1)S(1)} %copy-done.7), channel_id=1, source_target_pairs={{0,4},{2,6},{4,8},{6,10},{8,12},{10,14},{12,0},{14,2},{1,5},{3,7},... | collective-permute-start | bytes 884744 | tf_op jit(solution)/shard_map/ppermute | solution.py:238
  53.3 17.5 %collective-permute-start.2 = (bf16[2,576,128]{2,1,0:T(8,128)(2,1)S(1)}, bf16[2,576,128]{2,1,0:T(8,128)(2,1)S(1)}, u32[]{:S(2)}, u32[]{:S(2)}) collective-permute-start(bf16[2,576,128]{2,1,0:T(8,128)(2,1)S(1)} %copy-done.5), channel_id=1, source_target_pairs={{0,12},{2,14},{4,0},{6,2},{8,4},{10,6},{12,8},{14,10},{1,13},{3,15... | collective-permute-start | bytes 884744 | tf_op jit(solution)/shard_map/ppermute | solution.py:238
  70.9 11.8 %collective-permute-start.3 = (bf16[2,384,128]{2,1,0:T(8,128)(2,1)S(1)}, bf16[2,384,128]{2,1,0:T(8,128)(2,1)S(1)}, u32[]{:S(2)}, u32[]{:S(2)}) collective-permute-start(bf16[2,384,128]{2,1,0:T(8,128)(2,1)S(1)} %get-tuple-element.37), channel_id=1, source_target_pairs={{0,4},{2,6},{4,8},{6,10},{8,12},{10,14},{12,0},{14,2},{1,5},{3,7},... | collective-permute-start | bytes 589832 | tf_op jit(solution)/shard_map/ppermute | solution.py:238
  74.5 8.3 %collective-permute-start.4 = (bf16[2,384,128]{2,1,0:T(8,128)(2,1)S(1)}, bf16[2,384,128]{2,1,0:T(8,128)(2,1)S(1)}, u32[]{:S(2)}, u32[]{:S(2)}) collective-permute-start(bf16[2,384,128]{2,1,0:T(8,128)(2,1)S(1)} %get-tuple-element.38), channel_id=1, source_target_pairs={{0,12},{2,14},{4,0},{6,2},{8,4},{10,6},{12,8},{14,10},{1,13},{3,15... | collective-permute-start | bytes 589832 | tf_op jit(solution)/shard_map/ppermute | solution.py:238
  74.6 12.1 %collective-permute-start.5 = (bf16[2,384,128]{2,1,0:T(8,128)(2,1)S(1)}, bf16[2,384,128]{2,1,0:T(8,128)(2,1)S(1)}, u32[]{:S(2)}, u32[]{:S(2)}) collective-permute-start(bf16[2,384,128]{2,1,0:T(8,128)(2,1)S(1)} %get-tuple-element.39), channel_id=1, source_target_pairs={{0,2},{2,4},{4,6},{6,8},{8,10},{10,12},{12,14},{14,0},{1,3},{3,5},... | collective-permute-start | bytes 589832 | tf_op jit(solution)/shard_map/ppermute | solution.py:238
  74.6 12.5 %collective-permute-start.6 = (bf16[2,384,128]{2,1,0:T(8,128)(2,1)S(1)}, bf16[2,384,128]{2,1,0:T(8,128)(2,1)S(1)}, u32[]{:S(2)}, u32[]{:S(2)}) collective-permute-start(bf16[2,384,128]{2,1,0:T(8,128)(2,1)S(1)} %get-tuple-element.40), channel_id=1, source_target_pairs={{0,14},{2,0},{4,2},{6,4},{8,6},{10,8},{12,10},{14,12},{1,15},{3,1}... | collective-permute-start | bytes 589832 | tf_op jit(solution)/shard_map/ppermute | solution.py:238

commit v8 on v6

--- a/solution.py
+++ b/solution.py
@@ -19,6 +19,7 @@
 FAR = (3, 5, 4)
 NEAR = (0, 1, 7, 2, 6)
 KA = 8
+COPIES_GRANT = 67_000_000
 GRANT = 20 * 1024 * 1024
 NT = (((1,), (1,)), ((), ()))
 NN = (((1,), (0,)), ((), ()))
@@ -56,10 +57,10 @@
             kt[group, :, at:at + half] = dot(turn, k, NT).astype(jnp.bfloat16)
 
 
-def group_terms(group, h, per_owner, q_ref, do_ref, mask_ref, lse_ref, delta_ref, kz, vz):
+def group_terms(group, h, q_at, per_owner, q_ref, do_ref, mask_ref, lse_ref, delta_ref, kz, vz):
     rows = per_owner * q_ref.shape[1]
     lo = group * LANES
-    q = q_ref[pl.ds(h, per_owner), :, lo:lo + WIN].reshape(rows, WIN)
+    q = q_ref[pl.ds(q_at, per_owner), :, lo:lo + WIN].reshape(rows, WIN)
     do = do_ref[pl.ds(h, per_owner), :, lo:lo + DV].reshape(rows, DV)
     lse = jnp.concatenate([lse_ref[group, pl.ds(h + j, 1), :] for j in range(per_owner)], axis=1) * LOG2E
     delta = jnp.concatenate([delta_ref[group, pl.ds(h + j, 1), :] for j in range(per_owner)], axis=1)
@@ -78,7 +79,8 @@
     def one(i, carry):
         h = per_owner * lax.rem(me + pick(i, FAR), KA)
         for group in range(GROUPS):
-            ds = group_terms(group, h, per_owner, q_ref, do_ref, mask_ref, lse_ref, delta_ref, kz, vz)[3]
+            ds = group_terms(
+                group, h, per_owner * i, per_owner, q_ref, do_ref, mask_ref, lse_ref, delta_ref, kz, vz)[3]
             dqt = dot(kt[group], ds, NN) * SCALE
             for j in range(per_owner):
                 held[i, j, group * DK:(group + 1) * DK, :] = dqt[:, j * count:(j + 1) * count].astype(held.dtype)
@@ -103,7 +105,7 @@
     def one(i, query_grads):
         h = per_owner * lax.rem(me + pick(i, steps), KA)
         for group in range(GROUPS):
-            q, do, p, ds = group_terms(group, h, per_owner, q_ref, do_ref, mask_ref, lse_ref, delta_ref, kz, vz)
+            q, do, p, ds = group_terms(group, h, h, per_owner, q_ref, do_ref, mask_ref, lse_ref, delta_ref, kz, vz)
             acc_v[group] += dot(p, do, NN)
             acc_k[group] += dot(ds, q, NN)
             if query_grads:
@@ -134,10 +136,8 @@
             out[:, vlo:vlo + DV] = acc_v[group, at:at + half, :].astype(out.dtype)
 
 
-def grads(kernel, owners, matmuls, outs, scratch, *args):
-    heads, count, _ = args[0].shape
-    keys = args[2].shape[0]
-    terms = GROUPS * owners * (heads // KA) * count * keys
+def grads(kernel, rows, keys, matmuls, outs, scratch, *args):
+    terms = GROUPS * rows * keys
     return pl.pallas_call(
         kernel,
         out_shape=outs,
@@ -225,7 +225,7 @@
         in_specs=[HBM, HBM],
         out_specs=HBM,
         scratch_shapes=[pltpu.VMEM((rows, both), bf16), pltpu.SemaphoreType.DMA((2 + chips,))],
-        compiler_params=pltpu.CompilerParams(vmem_limit_bytes=GRANT),
+        compiler_params=pltpu.CompilerParams(vmem_limit_bytes=COPIES_GRANT),
         name="copies",
     )(comp_keys, comp_values)
     own = lax.all_to_all(copies, "pb", 0, 0, axis_index_groups=same_core, tiled=True).reshape(half, both)
@@ -239,26 +239,30 @@
     seen = jnp.where(core == 0, seen, seen[:, :, ::-1])
     seen = seen.transpose(2, 1, 3, 0).reshape(keys, visible.shape[0])
     mask = jnp.repeat(seen.astype(f32), QBLK, axis=1)
-    own, delta, mask = lax.optimization_barrier((own, delta, mask))
+    me = lax.axis_index("ka")
+    far_q = jnp.concatenate([
+        lax.dynamic_slice_in_dim(queries, per_owner * lax.rem(me + step, ka), per_owner, 0) for step in FAR
+    ])
+    own, delta, mask, far_q = lax.optimization_barrier((own, delta, mask, far_q))
     par = lax.ppermute(own, "pb", other_core)
 
-    args = (queries, grad_out, mask, log_sums, delta)
+    args = (grad_out, mask, log_sums, delta)
     hops = shape((per_owner, width + DK, count), bf16)
     chunk = (per_owner, width, count)
     right, left, kz, vz, kt = grads(
-        far_kernel, len(FAR), 2 * DK + DV,
+        far_kernel, len(FAR) * per_owner * count, keys, 2 * DK + DV,
         (
             hops, hops, shape((GROUPS, keys, WIN), bf16), shape((GROUPS, keys, DV), bf16),
             shape((GROUPS, DK, keys), bf16),
         ),
-        [pltpu.VMEM((len(FAR), *chunk), bf16)], *args, own, par,
+        [pltpu.VMEM((len(FAR), *chunk), bf16)], far_q, *args, own, par,
     )
     from_left = along(right, 2)
     from_right = along(left, -2)
     near, own_kv, par_kv = grads(
-        near_kernel, KA, 3 * DK + 2 * DV,
+        near_kernel, heads * count, keys, 3 * DK + 2 * DV,
         (shape((len(NEAR), *chunk), f32), shape((half, both), f32), shape((half, both), bf16)),
-        [pltpu.VMEM((GROUPS, keys, WIN), f32), pltpu.VMEM((GROUPS, keys, DV), f32)], *args, kz, vz, kt,
+        [pltpu.VMEM((GROUPS, keys, WIN), f32), pltpu.VMEM((GROUPS, keys, DV), f32)], queries, *args, kz, vz, kt,
     )
     from_other = lax.ppermute(par_kv, "pb", other_core)
 

time: 89.9 us -> 87.7 us (0.976)
  local copies, waits for them, and re-layouts: 7.46 us -> 4.91 us
  waiting for transfers between devices: 36.6 us -> 34.8 us
  other arithmetic: 1.6 us -> 2.87 us
    unnamed x22 -> x18, local copies, waits for them, and re-layouts: 4.51 us -> 1.47 us
    all_to_all x1, waiting for transfers between devices: 10.3 us -> 8.49 us  [per_device(): lax.all_to_all(copies, 'pb', 0, 0, axis_index_groups=same_core, tiled=True)]
    reduce_sum x1, other arithmetic: 0.61 us -> 1.82 us  [per_device(): jnp.sum(grad_out[:, :, g * DV:(g + 1) * DV].astype(f32) * outputs[:, :, g...]
    dynamic_slice x0 -> x1, local copies, waits for them, and re-layouts: none -> 1.19 us  [per_device(): lax.dynamic_slice_in_dim(queries, per_owner * lax.rem(me + step, ka), per...]
  transfers between devices with their start and end apart: 10 -> 10, of which waited for: 8 -> 8; matrix products, arithmetic and copies ran while one was open for 3% -> 5% of each run, Pallas kernels for 0% -> 0%
where the time goes in v8:
time: 87.7 us; the launch traced here: 87.3 us
  waiting for transfers between devices  34.8 us (40%)
  starting transfers between devices  25.5 us (29%)
  Pallas kernels  18.4 us (21%)
  local copies, waits for them, and re-layouts  4.91 us (6%)
  other arithmetic  2.87 us (3%)
    ppermute x6, waiting for transfers between devices, along(): return lax.ppermute(x, 'ka', [(i, (i + step) % ka) for i in range(ka)])  24.1 us
    pallas_call x2, Pallas kernels, grads(): pl.pallas_call(kernel, out_shape=outs, in_specs=[VMEM] * len(args), out_s...  15.6 us
    ppermute x6, starting transfers between devices, along(): return lax.ppermute(x, 'ka', [(i, (i + step) % ka) for i in range(ka)])  12.5 us
    all_to_all x1, waiting for transfers between devices, per_device(): lax.all_to_all(copies, 'pb', 0, 0, axis_index_groups=same_core, tiled=True)  8.49 us
    all_to_all x1, starting transfers between devices, per_device(): lax.all_to_all(copies, 'pb', 0, 0, axis_index_groups=same_core, tiled=True)  7.61 us
    all_to_all x1, starting transfers between devices, per_device(): lax.all_to_all(chip_sum.reshape(chips, rows, both), 'pb', 0, 0, axis_inde...  3.67 us
    reduce_sum x1, other arithmetic, per_device(): jnp.sum(grad_out[:, :, g * DV:(g + 1) * DV].astype(f32) * outputs[:, :, g...  1.82 us
  transfers between devices with their start and end apart: 10, of which 8 were waited for; matrix products, arithmetic and copies ran while one was open for 5% of the time, Pallas kernels for 0%

profile of v8, /device:TPU:1, one launch (start us, length us, event | category | flops | bytes accessed | tf_op | source)
XLA Modules:
  0.0 87.3 jit_solution(10829005429503068774)
XLA Ops:
  0.6 1.7 %copies.1 = bf16[8,64,640]{2,1,0:T(8,128)(2,1)} custom-call(bf16[64,384]{1,0:T(8,128)(2,1)} %keys.1, bf16[64,256]{1,0:T(8,128)(2,1)} %values.1), custom_call_target="tpu_custom_call" | custom-call | tf_op jit(solution)/shard_map/copies/pallas_call | solution.py:222
  2.4 7.6 %all-to-all-start = ((bf16[8,64,640]{2,1,0:T(8,128)(2,1)}), bf16[8,64,640]{2,1,0:T(8,128)(2,1)S(1)}, u32[]{:S(2)}, u32[]{:S(2)}) async-start(bf16[8,64,640]{2,1,0:T(8,128)(2,1)} %copies.1), calls=%async_computation | async-start | bytes 1310720 | tf_op jit(solution)/shard_map/all_to_all | solution.py:231
  10.0 0.1 reshape.21
  10.1 0.1 convert_element_type.33
  10.2 1.8 %multiply_reduce_fusion.1 = (f32[16,128]{1,0:T(8,128)S(1)}, f32[16,128]{1,0:T(8,128)S(1)}) fusion(bf16[16,128,256]{2,1,0:T(8,128)(2,1)} %param.10, bf16[16,128,256]{2,1,0:T(8,128)(2,1)S(1)} %copy-done), kind=kLoop, calls=%fused_computation.2 | loop fusion | flops 2093056 | bytes 2113536 | tf_op jit(solution)/shard_map/reduce_sum | solution.py:233
  12.1 1.2 %constant_dynamic-slice_fusion.2 = (bf16[2,128,384]{2,1,0:T(8,128)(2,1)S(1)}, bf16[2,128,384]{2,1,0:T(8,128)(2,1)S(1)}, bf16[2,128,384]{2,1,0:T(8,128)(2,1)S(1)}) fusion(bf16[16,128,384]{2,1,0:T(8,128)(2,1)} %q_ref.1, s32[]{:T(128)S(6)} %select_n.19, s32[]{:T(128)S(6)} %select_n.20, s32[]{:T(128)S(6)} %select_n.21), kind=kLoop, calls=%fused_computation.10 | loop fusion | bytes 1179660 | tf_op jit(solution)/shard_map/dynamic_slice | solution.py:244
  13.3 0.1 pad_maximum_fusion.q_ref
  13.4 8.5 %all-to-all-done = bf16[8,64,640]{2,1,0:T(8,128)(2,1)S(1)} async-done(((bf16[8,64,640]{2,1,0:T(8,128)(2,1)}), bf16[8,64,640]{2,1,0:T(8,128)(2,1)S(1)}, u32[]{:S(2)}, u32[]{:S(2)}) %all-to-all-start) | async-done | bytes 655392 | tf_op jit(solution)/shard_map/all_to_all | solution.py:231
  21.8 0.8 broadcast_in_dim.3
  22.7 1.2 %collective-permute-start = (bf16[512,640]{1,0:T(8,128)(2,1)S(1)}, bf16[512,640]{1,0:T(8,128)(2,1)S(1)}, u32[]{:S(2)}, u32[]{:S(2)}) collective-permute-start(bf16[512,640]{1,0:T(8,128)(2,1)S(1)} %bitcast.11), channel_id=1, source_target_pairs={{0,16},{16,0},{32,48},{48,32},{64,80},{80,64},{96,112},{112,96},{1... | collective-permute-start | bytes 1966088 | tf_op jit(solution)/shard_map/ppermute | solution.py:247
  23.9 1.2 %copy.13.mask_ref = f32[1024,128]{1,0:T(8,128)S(1)} copy(f32[1024,128]{0,1:T(8,128)} %bitcast.14) | data formatting | bytes 1048576 | tf_op jit(solution)/shard_map/optimization_barrier | solution.py:246
  25.2 0.5 collective-permute-done.par_ref
  25.7 3.9 %shard_map.94 = (bf16[2,576,128]{2,1,0:T(8,128)(2,1)S(1)}, bf16[2,576,128]{2,1,0:T(8,128)(2,1)S(1)}, bf16[2,1024,256]{2,1,0:T(8,128)(2,1)S(1)}, bf16[2,1024,128]...) custom-call(bf16[6,128,384]{2,1,0:T(8,128)(2,1)S(1)} %pad_maximum_fusion.q_ref, bf16[16,128,256]{2,1,0:T(8,128)(2,1)S(1)} %copy-done, ...), custom_call_target="tpu_custom_call" | custom-call | flops 1610612736 | bytes 6000000 | tf_op jit(solution)/shard_map/pallas_call | solution.py:141
  29.6 0.7 copy-done.2
  30.3 0.7 copy-done.4
  31.0 11.7 %shard_map.95 = (f32[5,2,384,128]{3,2,1,0:T(8,128)S(1)}, f32[512,640]{1,0:T(8,128)S(1)}, bf16[512,640]{1,0:T(8,128)(2,1)S(1)}) custom-call(bf16[16,128,384]{2,1,0:T(8,128)(2,1)S(1)} %copy-done.1, bf16[16,128,256]{2,1,0:T(8,128)(2,1)S(1)} %copy-done, f32[1024,128]{1,0:T(8,128)S(1)} %copy.13.mask_ref, f32[2,16,128]{2,1,0:T(8,128)S(1)} %copy-done.7, ...), custom_call_target="tpu_custom_call" | custom-call | flops 6979321856 | bytes 6000000 | tf_op jit(solution)/shard_map/pallas_call | solution.py:141
  42.7 0.5 collective-permute-start.7
  43.2 1.7 %collective-permute-done.7 = bf16[512,640]{1,0:T(8,128)(2,1)S(1)} collective-permute-done((bf16[512,640]{1,0:T(8,128)(2,1)S(1)}, bf16[512,640]{1,0:T(8,128)(2,1)S(1)}, u32[]{:S(2)}, u32[]{:S(2)}) %collective-permute-start.7) | collective-permute-done | bytes 655392 | tf_op jit(solution)/shard_map/ppermute | solution.py:267
  44.9 1.0 %add_convert_fusion = bf16[512,640]{1,0:T(8,128)(2,1)} fusion(f32[512,640]{1,0:T(8,128)S(1)} %get-tuple-element.33, bf16[512,640]{1,0:T(8,128)(2,1)S(1)} %collective-permute-done.7), kind=kLoop, calls=%fused_computation | loop fusion | flops 983040 | bytes 2621440 | tf_op jit(solution)/shard_map/convert_element_type | solution.py:274
  45.9 3.7 %all-to-all-start.1 = ((bf16[8,64,640]{2,1,0:T(8,128)(2,1)}), bf16[8,64,640]{2,1,0:T(8,128)(2,1)S(1)}, u32[]{:S(2)}, u32[]{:S(2)}) async-start(bf16[8,64,640]{2,1,0:T(8,128)(2,1)} %bitcast.13), calls=%async_computation.1 | async-start | bytes 1310720 | tf_op jit(solution)/shard_map/all_to_all | solution.py:275
  49.6 3.1 %collective-permute-start.1 = (bf16[2,576,128]{2,1,0:T(8,128)(2,1)S(1)}, bf16[2,576,128]{2,1,0:T(8,128)(2,1)S(1)}, u32[]{:S(2)}, u32[]{:S(2)}) collective-permute-start(bf16[2,576,128]{2,1,0:T(8,128)(2,1)S(1)} %copy-done.5), channel_id=1, source_target_pairs={{0,4},{2,6},{4,8},{6,10},{8,12},{10,14},{12,0},{14,2},{1,5},{3,7},... | collective-permute-start | bytes 884744 | tf_op jit(solution)/shard_map/ppermute | solution.py:220
  52.6 3.1 %collective-permute-start.2 = (bf16[2,576,128]{2,1,0:T(8,128)(2,1)S(1)}, bf16[2,576,128]{2,1,0:T(8,128)(2,1)S(1)}, u32[]{:S(2)}, u32[]{:S(2)}) collective-permute-start(bf16[2,576,128]{2,1,0:T(8,128)(2,1)S(1)} %copy-done.3), channel_id=1, source_target_pairs={{0,12},{2,14},{4,0},{6,2},{8,4},{10,6},{12,8},{14,10},{1,13},{3,15... | collective-permute-start | bytes 884744 | tf_op jit(solution)/shard_map/ppermute | solution.py:220
  55.8 8.8 %collective-permute-done.1.from_left = bf16[2,576,128]{2,1,0:T(8,128)(2,1)S(1)} collective-permute-done((bf16[2,576,128]{2,1,0:T(8,128)(2,1)S(1)}, bf16[2,576,128]{2,1,0:T(8,128)(2,1)S(1)}, u32[]{:S(2)}, u32[]{:S(2)}) %collective-permute-start.1) | collective-permute-done | bytes 294944 | tf_op jit(solution)/shard_map/ppermute | solution.py:220
  64.6 5.6 %collective-permute-done.2.from_right = bf16[2,576,128]{2,1,0:T(8,128)(2,1)S(1)} collective-permute-done((bf16[2,576,128]{2,1,0:T(8,128)(2,1)S(1)}, bf16[2,576,128]{2,1,0:T(8,128)(2,1)S(1)}, u32[]{:S(2)}, u32[]{:S(2)}) %collective-permute-start.2) | collective-permute-done | bytes 294944 | tf_op jit(solution)/shard_map/ppermute | solution.py:220
  70.2 0.1 shard_map.96
  70.3 3.5 %collective-permute-start.3 = (bf16[2,384,128]{2,1,0:T(8,128)(2,1)S(1)}, bf16[2,384,128]{2,1,0:T(8,128)(2,1)S(1)}, u32[]{:S(2)}, u32[]{:S(2)}) collective-permute-start(bf16[2,384,128]{2,1,0:T(8,128)(2,1)S(1)} %get-tuple-element.29), channel_id=1, source_target_pairs={{0,4},{2,6},{4,8},{6,10},{8,12},{10,14},{12,0},{14,2},{1,5},{3,7},... | collective-permute-start | bytes 589832 | tf_op jit(solution)/shard_map/ppermute | solution.py:220
  73.8 0.2 collective-permute-start.4
  73.9 2.7 %collective-permute-start.6 = (bf16[2,384,128]{2,1,0:T(8,128)(2,1)S(1)}, bf16[2,384,128]{2,1,0:T(8,128)(2,1)S(1)}, u32[]{:S(2)}, u32[]{:S(2)}) collective-permute-start(bf16[2,384,128]{2,1,0:T(8,128)(2,1)S(1)} %get-tuple-element.32), channel_id=1, source_target_pairs={{0,14},{2,0},{4,2},{6,4},{8,6},{10,8},{12,10},{14,12},{1,15},{3,1}... | collective-permute-start | bytes 589832 | tf_op jit(solution)/shard_map/ppermute | solution.py:220
  76.6 5.5 %collective-permute-done.3.a = bf16[2,384,128]{2,1,0:T(8,128)(2,1)S(1)} collective-permute-done((bf16[2,384,128]{2,1,0:T(8,128)(2,1)S(1)}, bf16[2,384,128]{2,1,0:T(8,128)(2,1)S(1)}, u32[]{:S(2)}, u32[]{:S(2)}) %collective-permute-start.3) | collective-permute-done | bytes 196640 | tf_op jit(solution)/shard_map/ppermute | solution.py:220
  82.2 3.9 %collective-permute-done.5.c = bf16[2,384,128]{2,1,0:T(8,128)(2,1)S(1)} collective-permute-done((bf16[2,384,128]{2,1,0:T(8,128)(2,1)S(1)}, bf16[2,384,128]{2,1,0:T(8,128)(2,1)S(1)}, u32[]{:S(2)}, u32[]{:S(2)}) %collective-permute-start.5) | collective-permute-done | bytes 196640 | tf_op jit(solution)/shard_map/ppermute | solution.py:220
  86.1 0.3 collective-permute-done.6.d
  86.3 0.9 %shard_map.97 = (f32[2,128,384]{2,1,0:T(8,128)}, f32[64,384]{1,0:T(8,128)}, f32[64,256]{1,0:T(8,128)}) custom-call(f32[5,2,384,128]{3,2,1,0:T(8,128)S(1)} %get-tuple-element.26.near, bf16[2,384,128]{2,1,0:T(8,128)(2,1)S(1)} %collective-permute-done.3.a, bf16[2,384,128]{2,1,0:T(8,128)(2,1)S(1)} %collective-permute-done.4.b, ...), custom_call_target="tpu_custom_call" | custom-call | tf_op jit(solution)/shard_map/pallas_call | solution.py:153
  (22 shorter events, 0.1 us)
Async XLA Ops:
  0.6 9.4 %copy-start.8 = (s32[2,1024]{1,0:T(2,128)S(1)}, s32[2,1024]{1,0:T(2,128)}, u32[]{:S(2)}) copy-start(s32[2,1024]{1,0:T(2,128)} %param.13) | copy-start | bytes 24580
  2.4 7.8 %copy-start = (bf16[16,128,256]{2,1,0:T(8,128)(2,1)S(1)}, bf16[16,128,256]{2,1,0:T(8,128)(2,1)}, u32[]{:S(2)}) copy-start(bf16[16,128,256]{2,1,0:T(8,128)(2,1)} %do_ref.3) | copy-start | bytes 3145732
  2.4 19.4 %all-to-all-start = ((bf16[8,64,640]{2,1,0:T(8,128)(2,1)}), bf16[8,64,640]{2,1,0:T(8,128)(2,1)S(1)}, u32[]{:S(2)}, u32[]{:S(2)}) async-start(bf16[8,64,640]{2,1,0:T(8,128)(2,1)} %copies.1), calls=%async_computation | async-start | bytes 1310720 | tf_op jit(solution)/shard_map/all_to_all | solution.py:231
  13.3 12.4 %copy-start.6 = (f32[2,16,128]{2,1,0:T(8,128)S(1)}, f32[2,16,128]{2,1,0:T(8,128)}, u32[]{:S(2)}) copy-start(f32[2,16,128]{2,1,0:T(8,128)} %lse_ref.3) | copy-start | bytes 49156
  22.7 3.0 %collective-permute-start = (bf16[512,640]{1,0:T(8,128)(2,1)S(1)}, bf16[512,640]{1,0:T(8,128)(2,1)S(1)}, u32[]{:S(2)}, u32[]{:S(2)}) collective-permute-start(bf16[512,640]{1,0:T(8,128)(2,1)S(1)} %bitcast.11), channel_id=1, source_target_pairs={{0,16},{16,0},{32,48},{48,32},{64,80},{80,64},{96,112},{112,96},{1... | collective-permute-start | bytes 1966088 | tf_op jit(solution)/shard_map/ppermute | solution.py:247
  25.2 5.9 %copy-start.1 = (bf16[16,128,384]{2,1,0:T(8,128)(2,1)S(1)}, bf16[16,128,384]{2,1,0:T(8,128)(2,1)}, u32[]{:S(2)}) copy-start(bf16[16,128,384]{2,1,0:T(8,128)(2,1)} %q_ref.1) | copy-start | bytes 4718596
  25.2 5.9 %copy-start.7 = (f32[2,16,128]{2,1,0:T(8,128)S(1)}, f32[2,16,128]{2,1,0:T(8,128)}, u32[]{:S(2)}) copy-start(f32[2,16,128]{2,1,0:T(8,128)} %lse_ref.3) | copy-start | bytes 49156
  29.6 0.7 copy-start.2
  30.3 0.7 copy-start.4
  42.7 2.2 %collective-permute-start.7 = (bf16[512,640]{1,0:T(8,128)(2,1)S(1)}, bf16[512,640]{1,0:T(8,128)(2,1)S(1)}, u32[]{:S(2)}, u32[]{:S(2)}) collective-permute-start(bf16[512,640]{1,0:T(8,128)(2,1)S(1)} %get-tuple-element.34), channel_id=1, source_target_pairs={{0,16},{16,0},{32,48},{48,32},{64,80},{80,64},{96,112},{112,96},{1... | collective-permute-start | bytes 1966088 | tf_op jit(solution)/shard_map/ppermute | solution.py:267
  45.9 3.7 %copy-start.5 = (bf16[2,576,128]{2,1,0:T(8,128)(2,1)S(1)}, bf16[2,576,128]{2,1,0:T(8,128)(2,1)}, u32[]{:S(2)}) copy-start(bf16[2,576,128]{2,1,0:T(8,128)(2,1)} %copy-done.4) | copy-start | bytes 884740
  45.9 6.8 %copy-start.3 = (bf16[2,576,128]{2,1,0:T(8,128)(2,1)S(1)}, bf16[2,576,128]{2,1,0:T(8,128)(2,1)}, u32[]{:S(2)}) copy-start(bf16[2,576,128]{2,1,0:T(8,128)(2,1)} %copy-done.2) | copy-start | bytes 884740
  45.9 40.5 %all-to-all-start.1 = ((bf16[8,64,640]{2,1,0:T(8,128)(2,1)}), bf16[8,64,640]{2,1,0:T(8,128)(2,1)S(1)}, u32[]{:S(2)}, u32[]{:S(2)}) async-start(bf16[8,64,640]{2,1,0:T(8,128)(2,1)} %bitcast.13), calls=%async_computation.1 | async-start | bytes 1310720 | tf_op jit(solution)/shard_map/all_to_all | solution.py:275
  49.6 15.0 %collective-permute-start.1 = (bf16[2,576,128]{2,1,0:T(8,128)(2,1)S(1)}, bf16[2,576,128]{2,1,0:T(8,128)(2,1)S(1)}, u32[]{:S(2)}, u32[]{:S(2)}) collective-permute-start(bf16[2,576,128]{2,1,0:T(8,128)(2,1)S(1)} %copy-done.5), channel_id=1, source_target_pairs={{0,4},{2,6},{4,8},{6,10},{8,12},{10,14},{12,0},{14,2},{1,5},{3,7},... | collective-permute-start | bytes 884744 | tf_op jit(solution)/shard_map/ppermute | solution.py:220
  52.6 17.5 %collective-permute-start.2 = (bf16[2,576,128]{2,1,0:T(8,128)(2,1)S(1)}, bf16[2,576,128]{2,1,0:T(8,128)(2,1)S(1)}, u32[]{:S(2)}, u32[]{:S(2)}) collective-permute-start(bf16[2,576,128]{2,1,0:T(8,128)(2,1)S(1)} %copy-done.3), channel_id=1, source_target_pairs={{0,12},{2,14},{4,0},{6,2},{8,4},{10,6},{12,8},{14,10},{1,13},{3,15... | collective-permute-start | bytes 884744 | tf_op jit(solution)/shard_map/ppermute | solution.py:220
  70.3 11.9 %collective-permute-start.3 = (bf16[2,384,128]{2,1,0:T(8,128)(2,1)S(1)}, bf16[2,384,128]{2,1,0:T(8,128)(2,1)S(1)}, u32[]{:S(2)}, u32[]{:S(2)}) collective-permute-start(bf16[2,384,128]{2,1,0:T(8,128)(2,1)S(1)} %get-tuple-element.29), channel_id=1, source_target_pairs={{0,4},{2,6},{4,8},{6,10},{8,12},{10,14},{12,0},{14,2},{1,5},{3,7},... | collective-permute-start | bytes 589832 | tf_op jit(solution)/shard_map/ppermute | solution.py:220
  73.8 8.4 %collective-permute-start.4 = (bf16[2,384,128]{2,1,0:T(8,128)(2,1)S(1)}, bf16[2,384,128]{2,1,0:T(8,128)(2,1)S(1)}, u32[]{:S(2)}, u32[]{:S(2)}) collective-permute-start(bf16[2,384,128]{2,1,0:T(8,128)(2,1)S(1)} %get-tuple-element.30), channel_id=1, source_target_pairs={{0,12},{2,14},{4,0},{6,2},{8,4},{10,6},{12,8},{14,10},{1,13},{3,15... | collective-permute-start | bytes 589832 | tf_op jit(solution)/shard_map/ppermute | solution.py:220
  73.9 12.1 %collective-permute-start.5 = (bf16[2,384,128]{2,1,0:T(8,128)(2,1)S(1)}, bf16[2,384,128]{2,1,0:T(8,128)(2,1)S(1)}, u32[]{:S(2)}, u32[]{:S(2)}) collective-permute-start(bf16[2,384,128]{2,1,0:T(8,128)(2,1)S(1)} %get-tuple-element.31), channel_id=1, source_target_pairs={{0,2},{2,4},{4,6},{6,8},{8,10},{10,12},{12,14},{14,0},{1,3},{3,5},... | collective-permute-start | bytes 589832 | tf_op jit(solution)/shard_map/ppermute | solution.py:220
  73.9 12.4 %collective-permute-start.6 = (bf16[2,384,128]{2,1,0:T(8,128)(2,1)S(1)}, bf16[2,384,128]{2,1,0:T(8,128)(2,1)S(1)}, u32[]{:S(2)}, u32[]{:S(2)}) collective-permute-start(bf16[2,384,128]{2,1,0:T(8,128)(2,1)S(1)} %get-tuple-element.32), channel_id=1, source_target_pairs={{0,14},{2,0},{4,2},{6,4},{8,6},{10,8},{12,10},{14,12},{1,15},{3,1}... | collective-permute-start | bytes 589832 | tf_op jit(solution)/shard_map/ppermute | solution.py:220

commit v9 on v8

--- a/solution.py
+++ b/solution.py
@@ -23,6 +23,7 @@
 GRANT = 20 * 1024 * 1024
 NT = (((1,), (1,)), ((), ()))
 NN = (((1,), (0,)), ((), ()))
+TN = (((0,), (0,)), ((), ()))
 VMEM = pl.BlockSpec(memory_space=pltpu.VMEM)
 HBM = pl.BlockSpec(memory_space=pltpu.HBM)
 
@@ -71,9 +72,14 @@
     return q, do, p.astype(jnp.bfloat16), ds
 
 
-def far_kernel(q_ref, do_ref, mask_ref, lse_ref, delta_ref, own_ref, par_ref, right, left, kz, vz, kt, held):
+def far_kernel(q_ref, do_ref, lse_ref, delta_ref, seen_ref, own_ref, par_ref,
+               right, left, mask_ref, kz, vz, kt, held):
     per_owner, _, count = right.shape
     me = lax.axis_index("ka")
+    block = lax.broadcasted_iota(jnp.int32, (seen_ref.shape[0], LANES), 0)
+    lane = lax.broadcasted_iota(jnp.int32, (seen_ref.shape[0], LANES), 1)
+    select = jnp.where(block == lane // QBLK, 1.0, 0.0)
+    mask_ref[...] = dot(seen_ref[...], select, TN)
     load_keys(own_ref, par_ref, kz, vz, kt)
 
     def one(i, carry):
@@ -94,7 +100,7 @@
     left[:, width:, :] = held[2, :, DK:, :]
 
 
-def near_kernel(q_ref, do_ref, mask_ref, lse_ref, delta_ref, kz, vz, kt, near, own_out, par_out, acc_k, acc_v):
+def near_kernel(q_ref, do_ref, lse_ref, delta_ref, mask_ref, kz, vz, kt, near, own_out, par_out, acc_k, acc_v):
     _, per_owner, _, count = near.shape
     half = own_out.shape[0]
     me = lax.axis_index("ka")
@@ -237,32 +243,32 @@
     ])
     seen = visible.reshape(visible.shape[0], chips, 2, rows)
     seen = jnp.where(core == 0, seen, seen[:, :, ::-1])
-    seen = seen.transpose(2, 1, 3, 0).reshape(keys, visible.shape[0])
-    mask = jnp.repeat(seen.astype(f32), QBLK, axis=1)
+    seen = seen.transpose(0, 2, 1, 3).reshape(visible.shape[0], keys).astype(f32)
+    seen = jnp.pad(seen, ((0, 8 - seen.shape[0]), (0, 0)))
     me = lax.axis_index("ka")
     far_q = jnp.concatenate([
         lax.dynamic_slice_in_dim(queries, per_owner * lax.rem(me + step, ka), per_owner, 0) for step in FAR
     ])
-    own, delta, mask, far_q = lax.optimization_barrier((own, delta, mask, far_q))
+    own, delta, seen, far_q = lax.optimization_barrier((own, delta, seen, far_q))
     par = lax.ppermute(own, "pb", other_core)
 
-    args = (grad_out, mask, log_sums, delta)
+    args = (grad_out, log_sums, delta)
     hops = shape((per_owner, width + DK, count), bf16)
     chunk = (per_owner, width, count)
-    right, left, kz, vz, kt = grads(
+    right, left, mask, kz, vz, kt = grads(
         far_kernel, len(FAR) * per_owner * count, keys, 2 * DK + DV,
         (
-            hops, hops, shape((GROUPS, keys, WIN), bf16), shape((GROUPS, keys, DV), bf16),
+            hops, hops, shape((keys, LANES), f32), shape((GROUPS, keys, WIN), bf16), shape((GROUPS, keys, DV), bf16),
             shape((GROUPS, DK, keys), bf16),
         ),
-        [pltpu.VMEM((len(FAR), *chunk), bf16)], far_q, *args, own, par,
+        [pltpu.VMEM((len(FAR), *chunk), bf16)], far_q, *args, seen, own, par,
     )
     from_left = along(right, 2)
     from_right = along(left, -2)
     near, own_kv, par_kv = grads(
         near_kernel, heads * count, keys, 3 * DK + 2 * DV,
         (shape((len(NEAR), *chunk), f32), shape((half, both), f32), shape((half, both), bf16)),
-        [pltpu.VMEM((GROUPS, keys, WIN), f32), pltpu.VMEM((GROUPS, keys, DV), f32)], queries, *args, kz, vz, kt,
+        [pltpu.VMEM((GROUPS, keys, WIN), f32), pltpu.VMEM((GROUPS, keys, DV), f32)], queries, *args, mask, kz, vz, kt,
     )
     from_other = lax.ppermute(par_kv, "pb", other_core)
 

time: 87.7 us -> 86.2 us (0.983)
  local copies, waits for them, and re-layouts: 4.91 us -> 2.1 us
  waiting for transfers between devices: 34.8 us -> 36 us
    ppermute x1, waiting for transfers between devices: 0.46 us -> 1.72 us  [per_device(): par = lax.ppermute(own, 'pb', other_core)]
    optimization_barrier x1 -> x0, local copies, waits for them, and re-layouts: 1.23 us -> none  [per_device(): lax.optimization_barrier((own, delta, mask, far_q))]
  transfers between devices with their start and end apart: 10 -> 10, of which waited for: 8 -> 8; matrix products, arithmetic and copies ran while one was open for 5% -> 4% of each run, Pallas kernels for 0% -> 0%
where the time goes in v9:
time: 86.2 us; the launch traced here: 85.8 us
  waiting for transfers between devices  36 us (42%)
  starting transfers between devices  25.5 us (30%)
  Pallas kernels  18.5 us (21%)
  other arithmetic  2.87 us (3%)
  local copies, waits for them, and re-layouts  2.1 us (2%)
    ppermute x6, waiting for transfers between devices, along(): return lax.ppermute(x, 'ka', [(i, (i + step) % ka) for i in range(ka)])  24.1 us
    pallas_call x2, Pallas kernels, grads(): pl.pallas_call(kernel, out_shape=outs, in_specs=[VMEM] * len(args), out_s...  15.7 us
    ppermute x6, starting transfers between devices, along(): return lax.ppermute(x, 'ka', [(i, (i + step) % ka) for i in range(ka)])  12.5 us
    all_to_all x1, waiting for transfers between devices, per_device(): lax.all_to_all(copies, 'pb', 0, 0, axis_index_groups=same_core, tiled=True)  8.48 us
    all_to_all x1, starting transfers between devices, per_device(): lax.all_to_all(copies, 'pb', 0, 0, axis_index_groups=same_core, tiled=True)  7.61 us
    all_to_all x1, starting transfers between devices, per_device(): lax.all_to_all(chip_sum.reshape(chips, rows, both), 'pb', 0, 0, axis_inde...  3.67 us
    reduce_sum x1, other arithmetic, per_device(): jnp.sum(grad_out[:, :, g * DV:(g + 1) * DV].astype(f32) * outputs[:, :, g...  1.82 us
    pallas_call x1, Pallas kernels, per_device(): pl.pallas_call(copies_kernel, out_shape=shape((chips, rows, both), bf16),...  1.74 us
  transfers between devices with their start and end apart: 10, of which 8 were waited for; matrix products, arithmetic and copies ran while one was open for 4% of the time, Pallas kernels for 0%

profile of v9, /device:TPU:1, one launch (start us, length us, event | category | flops | bytes accessed | tf_op | source)
XLA Modules:
  0.0 85.8 jit_solution(13804653299825034978)
XLA Ops:
  0.6 1.7 %copies.1 = bf16[8,64,640]{2,1,0:T(8,128)(2,1)} custom-call(bf16[64,384]{1,0:T(8,128)(2,1)} %keys.1, bf16[64,256]{1,0:T(8,128)(2,1)} %values.1), custom_call_target="tpu_custom_call" | custom-call | tf_op jit(solution)/shard_map/copies/pallas_call | solution.py:228
  2.4 0.0 copy-start
  2.4 7.6 %all-to-all-start = ((bf16[8,64,640]{2,1,0:T(8,128)(2,1)}), bf16[8,64,640]{2,1,0:T(8,128)(2,1)S(1)}, u32[]{:S(2)}, u32[]{:S(2)}) async-start(bf16[8,64,640]{2,1,0:T(8,128)(2,1)} %copies.1), calls=%async_computation | async-start | bytes 1310720 | tf_op jit(solution)/shard_map/all_to_all | solution.py:237
  10.0 0.1 reshape.18
  10.1 0.1 convert_element_type.35
  10.2 1.8 %multiply_reduce_fusion.1 = (f32[16,128]{1,0:T(8,128)S(1)}, f32[16,128]{1,0:T(8,128)S(1)}) fusion(bf16[16,128,256]{2,1,0:T(8,128)(2,1)} %param.10, bf16[16,128,256]{2,1,0:T(8,128)(2,1)S(1)} %copy-done), kind=kLoop, calls=%fused_computation.2 | loop fusion | flops 2093056 | bytes 2113536 | tf_op jit(solution)/shard_map/reduce_sum | solution.py:239
  12.1 0.0 copy-start.4
  12.1 1.2 %constant_dynamic-slice_fusion.2 = (bf16[2,128,384]{2,1,0:T(8,128)(2,1)S(1)}, bf16[2,128,384]{2,1,0:T(8,128)(2,1)S(1)}, bf16[2,128,384]{2,1,0:T(8,128)(2,1)S(1)}) fusion(bf16[16,128,384]{2,1,0:T(8,128)(2,1)} %q_ref.1, s32[]{:T(128)S(6)} %select_n.19, s32[]{:T(128)S(6)} %select_n.20, s32[]{:T(128)S(6)} %select_n.21), kind=kLoop, calls=%fused_computation.10 | loop fusion | bytes 1179660 | tf_op jit(solution)/shard_map/dynamic_slice | solution.py:250
  13.3 0.1 pad_maximum_fusion.q_ref
  13.4 8.5 %all-to-all-done = bf16[8,64,640]{2,1,0:T(8,128)(2,1)S(1)} async-done(((bf16[8,64,640]{2,1,0:T(8,128)(2,1)}), bf16[8,64,640]{2,1,0:T(8,128)(2,1)S(1)}, u32[]{:S(2)}, u32[]{:S(2)}) %all-to-all-start) | async-done | bytes 655392 | tf_op jit(solution)/shard_map/all_to_all | solution.py:237
  21.8 1.2 %collective-permute-start = (bf16[512,640]{1,0:T(8,128)(2,1)S(1)}, bf16[512,640]{1,0:T(8,128)(2,1)S(1)}, u32[]{:S(2)}, u32[]{:S(2)}) collective-permute-start(bf16[512,640]{1,0:T(8,128)(2,1)S(1)} %bitcast.8), channel_id=1, source_target_pairs={{0,16},{16,0},{32,48},{48,32},{64,80},{80,64},{96,112},{112,96},{1... | collective-permute-start | bytes 1966088 | tf_op jit(solution)/shard_map/ppermute | solution.py:253
  23.1 1.7 %collective-permute-done.par_ref = bf16[512,640]{1,0:T(8,128)(2,1)S(1)} collective-permute-done((bf16[512,640]{1,0:T(8,128)(2,1)S(1)}, bf16[512,640]{1,0:T(8,128)(2,1)S(1)}, u32[]{:S(2)}, u32[]{:S(2)}) %collective-permute-start) | collective-permute-done | bytes 655392 | tf_op jit(solution)/shard_map/ppermute | solution.py:253
  24.8 4.0 %shard_map.94 = (bf16[2,576,128]{2,1,0:T(8,128)(2,1)S(1)}, bf16[2,576,128]{2,1,0:T(8,128)(2,1)S(1)}, f32[1024,128]{1,0:T(8,128)S(1)}, bf16[2,1024,256]{2,1,0:T(8...) custom-call(bf16[6,128,384]{2,1,0:T(8,128)(2,1)S(1)} %pad_maximum_fusion.q_ref, ...), custom_call_target="tpu_custom_call" | custom-call | flops 1610612736 | bytes 6000000 | tf_op jit(solution)/shard_map/pallas_call | solution.py:147
  28.8 0.0 copy-start.2
  28.8 0.7 copy-done.2
  29.5 11.7 %shard_map.95 = (f32[5,2,384,128]{3,2,1,0:T(8,128)S(1)}, f32[512,640]{1,0:T(8,128)S(1)}, bf16[512,640]{1,0:T(8,128)(2,1)S(1)}) custom-call(bf16[16,128,384]{2,1,0:T(8,128)(2,1)S(1)} %copy-done.1, bf16[16,128,256]{2,1,0:T(8,128)(2,1)S(1)} %copy-done, f32[2,16,128]{2,1,0:T(8,128)S(1)} %copy-done.4, f32[2,16,128]{2,1,0:T(8,128)S(1)} %pad_maximum_fusion.1.delta_ref, ...), custom_call_target="tpu_custom_call" | custom-call | flops 6979321856 | bytes 6000000 | tf_op jit(solution)/shard_map/pallas_call | solution.py:147
  41.2 0.5 collective-permute-start.7
  41.7 1.7 %collective-permute-done.7 = bf16[512,640]{1,0:T(8,128)(2,1)S(1)} collective-permute-done((bf16[512,640]{1,0:T(8,128)(2,1)S(1)}, bf16[512,640]{1,0:T(8,128)(2,1)S(1)}, u32[]{:S(2)}, u32[]{:S(2)}) %collective-permute-start.7) | collective-permute-done | bytes 655392 | tf_op jit(solution)/shard_map/ppermute | solution.py:273
  43.4 1.0 %add_convert_fusion = bf16[512,640]{1,0:T(8,128)(2,1)} fusion(f32[512,640]{1,0:T(8,128)S(1)} %get-tuple-element.35, bf16[512,640]{1,0:T(8,128)(2,1)S(1)} %collective-permute-done.7), kind=kLoop, calls=%fused_computation | loop fusion | flops 983040 | bytes 2621440 | tf_op jit(solution)/shard_map/convert_element_type | solution.py:280
  44.4 3.7 %all-to-all-start.1 = ((bf16[8,64,640]{2,1,0:T(8,128)(2,1)}), bf16[8,64,640]{2,1,0:T(8,128)(2,1)S(1)}, u32[]{:S(2)}, u32[]{:S(2)}) async-start(bf16[8,64,640]{2,1,0:T(8,128)(2,1)} %bitcast.10), calls=%async_computation.1 | async-start | bytes 1310720 | tf_op jit(solution)/shard_map/all_to_all | solution.py:281
  48.1 3.1 %collective-permute-start.1 = (bf16[2,576,128]{2,1,0:T(8,128)(2,1)S(1)}, bf16[2,576,128]{2,1,0:T(8,128)(2,1)S(1)}, u32[]{:S(2)}, u32[]{:S(2)}) collective-permute-start(bf16[2,576,128]{2,1,0:T(8,128)(2,1)S(1)} %copy-done.3), channel_id=1, source_target_pairs={{0,4},{2,6},{4,8},{6,10},{8,12},{10,14},{12,0},{14,2},{1,5},{3,7},... | collective-permute-start | bytes 884744 | tf_op jit(solution)/shard_map/ppermute | solution.py:226
  51.1 3.1 %collective-permute-start.2 = (bf16[2,576,128]{2,1,0:T(8,128)(2,1)S(1)}, bf16[2,576,128]{2,1,0:T(8,128)(2,1)S(1)}, u32[]{:S(2)}, u32[]{:S(2)}) collective-permute-start(bf16[2,576,128]{2,1,0:T(8,128)(2,1)S(1)} %get-tuple-element.30), channel_id=1, source_target_pairs={{0,12},{2,14},{4,0},{6,2},{8,4},{10,6},{12,8},{14,10},{1,13},{3,15... | collective-permute-start | bytes 884744 | tf_op jit(solution)/shard_map/ppermute | solution.py:226
  54.3 8.9 %collective-permute-done.1.from_left = bf16[2,576,128]{2,1,0:T(8,128)(2,1)S(1)} collective-permute-done((bf16[2,576,128]{2,1,0:T(8,128)(2,1)S(1)}, bf16[2,576,128]{2,1,0:T(8,128)(2,1)S(1)}, u32[]{:S(2)}, u32[]{:S(2)}) %collective-permute-start.1) | collective-permute-done | bytes 294944 | tf_op jit(solution)/shard_map/ppermute | solution.py:226
  63.1 5.5 %collective-permute-done.2.from_right = bf16[2,576,128]{2,1,0:T(8,128)(2,1)S(1)} collective-permute-done((bf16[2,576,128]{2,1,0:T(8,128)(2,1)S(1)}, bf16[2,576,128]{2,1,0:T(8,128)(2,1)S(1)}, u32[]{:S(2)}, u32[]{:S(2)}) %collective-permute-start.2) | collective-permute-done | bytes 294944 | tf_op jit(solution)/shard_map/ppermute | solution.py:226
  68.7 0.1 shard_map.96
  68.8 3.5 %collective-permute-start.3 = (bf16[2,384,128]{2,1,0:T(8,128)(2,1)S(1)}, bf16[2,384,128]{2,1,0:T(8,128)(2,1)S(1)}, u32[]{:S(2)}, u32[]{:S(2)}) collective-permute-start(bf16[2,384,128]{2,1,0:T(8,128)(2,1)S(1)} %get-tuple-element.31), channel_id=1, source_target_pairs={{0,4},{2,6},{4,8},{6,10},{8,12},{10,14},{12,0},{14,2},{1,5},{3,7},... | collective-permute-start | bytes 589832 | tf_op jit(solution)/shard_map/ppermute | solution.py:226
  72.3 0.2 collective-permute-start.4
  72.4 2.7 %collective-permute-start.6 = (bf16[2,384,128]{2,1,0:T(8,128)(2,1)S(1)}, bf16[2,384,128]{2,1,0:T(8,128)(2,1)S(1)}, u32[]{:S(2)}, u32[]{:S(2)}) collective-permute-start(bf16[2,384,128]{2,1,0:T(8,128)(2,1)S(1)} %get-tuple-element.34), channel_id=1, source_target_pairs={{0,14},{2,0},{4,2},{6,4},{8,6},{10,8},{12,10},{14,12},{1,15},{3,1}... | collective-permute-start | bytes 589832 | tf_op jit(solution)/shard_map/ppermute | solution.py:226
  75.1 5.6 %collective-permute-done.3.a = bf16[2,384,128]{2,1,0:T(8,128)(2,1)S(1)} collective-permute-done((bf16[2,384,128]{2,1,0:T(8,128)(2,1)S(1)}, bf16[2,384,128]{2,1,0:T(8,128)(2,1)S(1)}, u32[]{:S(2)}, u32[]{:S(2)}) %collective-permute-start.3) | collective-permute-done | bytes 196640 | tf_op jit(solution)/shard_map/ppermute | solution.py:226
  80.7 3.9 %collective-permute-done.5.c = bf16[2,384,128]{2,1,0:T(8,128)(2,1)S(1)} collective-permute-done((bf16[2,384,128]{2,1,0:T(8,128)(2,1)S(1)}, bf16[2,384,128]{2,1,0:T(8,128)(2,1)S(1)}, u32[]{:S(2)}, u32[]{:S(2)}) %collective-permute-start.5) | collective-permute-done | bytes 196640 | tf_op jit(solution)/shard_map/ppermute | solution.py:226
  84.6 0.2 collective-permute-done.6.d
  84.8 0.9 %shard_map.97 = (f32[2,128,384]{2,1,0:T(8,128)}, f32[64,384]{1,0:T(8,128)}, f32[64,256]{1,0:T(8,128)}) custom-call(f32[5,2,384,128]{3,2,1,0:T(8,128)S(1)} %get-tuple-element.28.near, bf16[2,384,128]{2,1,0:T(8,128)(2,1)S(1)} %collective-permute-done.3.a, bf16[2,384,128]{2,1,0:T(8,128)(2,1)S(1)} %collective-permute-done.4.b, ...), custom_call_target="tpu_custom_call" | custom-call | tf_op jit(solution)/shard_map/pallas_call | solution.py:159
  (15 shorter events, 0.1 us)
Async XLA Ops:
  0.6 9.4 %copy-start.5 = (s32[2,1024]{1,0:T(2,128)S(1)}, s32[2,1024]{1,0:T(2,128)}, u32[]{:S(2)}) copy-start(s32[2,1024]{1,0:T(2,128)} %param.13) | copy-start | bytes 24580
  2.4 7.9 %copy-start = (bf16[16,128,256]{2,1,0:T(8,128)(2,1)S(1)}, bf16[16,128,256]{2,1,0:T(8,128)(2,1)}, u32[]{:S(2)}) copy-start(bf16[16,128,256]{2,1,0:T(8,128)(2,1)} %do_ref.3) | copy-start | bytes 3145732
  2.4 19.4 %all-to-all-start = ((bf16[8,64,640]{2,1,0:T(8,128)(2,1)}), bf16[8,64,640]{2,1,0:T(8,128)(2,1)S(1)}, u32[]{:S(2)}, u32[]{:S(2)}) async-start(bf16[8,64,640]{2,1,0:T(8,128)(2,1)} %copies.1), calls=%async_computation | async-start | bytes 1310720 | tf_op jit(solution)/shard_map/all_to_all | solution.py:237
  12.1 12.7 %copy-start.4 = (f32[2,16,128]{2,1,0:T(8,128)S(1)}, f32[2,16,128]{2,1,0:T(8,128)}, u32[]{:S(2)}) copy-start(f32[2,16,128]{2,1,0:T(8,128)} %lse_ref.3) | copy-start | bytes 49156
  21.8 7.7 %copy-start.1 = (bf16[16,128,384]{2,1,0:T(8,128)(2,1)S(1)}, bf16[16,128,384]{2,1,0:T(8,128)(2,1)}, u32[]{:S(2)}) copy-start(bf16[16,128,384]{2,1,0:T(8,128)(2,1)} %q_ref.1) | copy-start | bytes 4718596
  21.8 3.0 %collective-permute-start = (bf16[512,640]{1,0:T(8,128)(2,1)S(1)}, bf16[512,640]{1,0:T(8,128)(2,1)S(1)}, u32[]{:S(2)}, u32[]{:S(2)}) collective-permute-start(bf16[512,640]{1,0:T(8,128)(2,1)S(1)} %bitcast.8), channel_id=1, source_target_pairs={{0,16},{16,0},{32,48},{48,32},{64,80},{80,64},{96,112},{112,96},{1... | collective-permute-start | bytes 1966088 | tf_op jit(solution)/shard_map/ppermute | solution.py:253
  28.8 0.7 copy-start.2
  41.2 2.2 %collective-permute-start.7 = (bf16[512,640]{1,0:T(8,128)(2,1)S(1)}, bf16[512,640]{1,0:T(8,128)(2,1)S(1)}, u32[]{:S(2)}, u32[]{:S(2)}) collective-permute-start(bf16[512,640]{1,0:T(8,128)(2,1)S(1)} %get-tuple-element.36), channel_id=1, source_target_pairs={{0,16},{16,0},{32,48},{48,32},{64,80},{80,64},{96,112},{112,96},{1... | collective-permute-start | bytes 1966088 | tf_op jit(solution)/shard_map/ppermute | solution.py:273
  44.4 3.7 %copy-start.3 = (bf16[2,576,128]{2,1,0:T(8,128)(2,1)S(1)}, bf16[2,576,128]{2,1,0:T(8,128)(2,1)}, u32[]{:S(2)}) copy-start(bf16[2,576,128]{2,1,0:T(8,128)(2,1)} %copy-done.2) | copy-start | bytes 884740
  44.4 40.4 %all-to-all-start.1 = ((bf16[8,64,640]{2,1,0:T(8,128)(2,1)}), bf16[8,64,640]{2,1,0:T(8,128)(2,1)S(1)}, u32[]{:S(2)}, u32[]{:S(2)}) async-start(bf16[8,64,640]{2,1,0:T(8,128)(2,1)} %bitcast.10), calls=%async_computation.1 | async-start | bytes 1310720 | tf_op jit(solution)/shard_map/all_to_all | solution.py:281
  48.1 15.1 %collective-permute-start.1 = (bf16[2,576,128]{2,1,0:T(8,128)(2,1)S(1)}, bf16[2,576,128]{2,1,0:T(8,128)(2,1)S(1)}, u32[]{:S(2)}, u32[]{:S(2)}) collective-permute-start(bf16[2,576,128]{2,1,0:T(8,128)(2,1)S(1)} %copy-done.3), channel_id=1, source_target_pairs={{0,4},{2,6},{4,8},{6,10},{8,12},{10,14},{12,0},{14,2},{1,5},{3,7},... | collective-permute-start | bytes 884744 | tf_op jit(solution)/shard_map/ppermute | solution.py:226
  51.1 17.5 %collective-permute-start.2 = (bf16[2,576,128]{2,1,0:T(8,128)(2,1)S(1)}, bf16[2,576,128]{2,1,0:T(8,128)(2,1)S(1)}, u32[]{:S(2)}, u32[]{:S(2)}) collective-permute-start(bf16[2,576,128]{2,1,0:T(8,128)(2,1)S(1)} %get-tuple-element.30), channel_id=1, source_target_pairs={{0,12},{2,14},{4,0},{6,2},{8,4},{10,6},{12,8},{14,10},{1,13},{3,15... | collective-permute-start | bytes 884744 | tf_op jit(solution)/shard_map/ppermute | solution.py:226
  68.8 11.9 %collective-permute-start.3 = (bf16[2,384,128]{2,1,0:T(8,128)(2,1)S(1)}, bf16[2,384,128]{2,1,0:T(8,128)(2,1)S(1)}, u32[]{:S(2)}, u32[]{:S(2)}) collective-permute-start(bf16[2,384,128]{2,1,0:T(8,128)(2,1)S(1)} %get-tuple-element.31), channel_id=1, source_target_pairs={{0,4},{2,6},{4,8},{6,10},{8,12},{10,14},{12,0},{14,2},{1,5},{3,7},... | collective-permute-start | bytes 589832 | tf_op jit(solution)/shard_map/ppermute | solution.py:226
  72.3 8.4 %collective-permute-start.4 = (bf16[2,384,128]{2,1,0:T(8,128)(2,1)S(1)}, bf16[2,384,128]{2,1,0:T(8,128)(2,1)S(1)}, u32[]{:S(2)}, u32[]{:S(2)}) collective-permute-start(bf16[2,384,128]{2,1,0:T(8,128)(2,1)S(1)} %get-tuple-element.32), channel_id=1, source_target_pairs={{0,12},{2,14},{4,0},{6,2},{8,4},{10,6},{12,8},{14,10},{1,13},{3,15... | collective-permute-start | bytes 589832 | tf_op jit(solution)/shard_map/ppermute | solution.py:226
  72.4 12.1 %collective-permute-start.5 = (bf16[2,384,128]{2,1,0:T(8,128)(2,1)S(1)}, bf16[2,384,128]{2,1,0:T(8,128)(2,1)S(1)}, u32[]{:S(2)}, u32[]{:S(2)}) collective-permute-start(bf16[2,384,128]{2,1,0:T(8,128)(2,1)S(1)} %get-tuple-element.33), channel_id=1, source_target_pairs={{0,2},{2,4},{4,6},{6,8},{8,10},{10,12},{12,14},{14,0},{1,3},{3,5},... | collective-permute-start | bytes 589832 | tf_op jit(solution)/shard_map/ppermute | solution.py:226
  72.4 12.4 %collective-permute-start.6 = (bf16[2,384,128]{2,1,0:T(8,128)(2,1)S(1)}, bf16[2,384,128]{2,1,0:T(8,128)(2,1)S(1)}, u32[]{:S(2)}, u32[]{:S(2)}) collective-permute-start(bf16[2,384,128]{2,1,0:T(8,128)(2,1)S(1)} %get-tuple-element.34), channel_id=1, source_target_pairs={{0,14},{2,0},{4,2},{6,4},{8,6},{10,8},{12,10},{14,12},{1,15},{3,1}... | collective-permute-start | bytes 589832 | tf_op jit(solution)/shard_map/ppermute | solution.py:226
